TPU v7x, 32 devices: a whole 2x2x4 slice. The times are simulated.
32 devices in a mesh: gx: 4 (over z), gy: 2 (over core), gz: 4 (over y, x).
Axes of the slice: x: 2, y: 2, z: 4, core: 2. Of those that a mesh axis runs over, the one named last changes fastest.
Arguments:
- e_field: float32 [3, 16, 32, 512], P(None, 'gx', 'gy', 'gz'), may hold values from -6 to 6
- h_field: float32 [3, 16, 32, 512], P(None, 'gx', 'gy', 'gz'), may hold values from -6 to 6
- current: float32 [3, 16, 32, 512], P(None, 'gx', 'gy', 'gz'), may hold values from -6 to 6
- material: int32 [16, 32, 512], P('gx', 'gy', 'gz'), may hold values from 0 to 2
- sigma_table: float32 [3], replicated, may hold values from 0.05 to 2
- gamma_table: float32 [3], replicated, may hold values from 0.05 to 1
- plasma_table: float32 [3], replicated, may hold values from 0.3 to 2
- g_kernel: float32 [4], replicated, may hold values from -4 to 4
- surf_cell: int32 [4, 2, 4, 1024], P('gx', 'gy', 'gz'), may hold values from 0 to 8191
- surf_owner: int32 [4, 2, 4, 1024, 1], P('gx', 'gy', 'gz'), may hold values from 0 to 7; in each aligned block of 1024 rows (0 to 1023, 1024 to 2047, ..., all dimensions but the last counted through in order) at most 192 rows name the same one
- surf_tile: int32 [4, 2, 4, 1024], P('gx', 'gy', 'gz'), may hold values from 0 to 127
- surf_normal: int32 [4, 2, 4, 1024], P('gx', 'gy', 'gz'), may hold values from 0 to 5
- row_count: int32 [4, 2, 4], P('gx', 'gy', 'gz'), may hold values from 256 to 1024, as said below
Outputs:
- e_out: float32 [3, 16, 32, 512], P(None, 'gx', 'gy', 'gz')
- h_out: float32 [3, 16, 32, 512], P(None, 'gx', 'gy', 'gz')
- force: float32 [3, 4096], P(None, ('gx', 'gy', 'gz'))
Inputs may be any that keep to these rules, and one draw needn't show every extreme that they name: `surf_owner`: among the slots of one device no owner is named more than 192 times, a bound that some block reaches. `row_count`: some brick has all 1024 slots live.
All inputs are finite; a program needn't handle non-finite values.
Results may differ from a plain program's by a relative error of at most 0.00019.
Values sent between devices are 32-bit elements; how exact they have to be, the bound alone decides.
No kernel may reach another device: no remote copies, remote signals or barrier semaphores. Data moves between devices by JAX's collectives and lax.ppermute only.
A program may use at most 64 MiB of HBM per device.

v0:
```python
import jax
import jax.numpy as jnp
from jax import lax
from jax.sharding import PartitionSpec as P

TILE_DEV = 128


STEP_DT = 0.5
FACE_AREA = 0.25


def passed_along(shard, axis, by):
    peers = lax.axis_size(axis)
    pairs = [(i, i + by) for i in range(peers) if 0 <= i + by < peers]
    return lax.ppermute(shard, axis, pairs)


def lookup(material, table):
    result = jnp.zeros(material.shape, table.dtype)
    for which in range(table.shape[0]):
        result = result + jnp.where(material == which, table[which], jnp.zeros((), table.dtype))
    return result


def coefficients(material, sigma_table, gamma_table, plasma_table):
    sigma = lookup(material, sigma_table)
    gamma = lookup(material, gamma_table)
    plasma = lookup(material, plasma_table)
    keep_e = (1.0 - sigma * STEP_DT / 2) / (1.0 + sigma * STEP_DT / 2)
    gain_e = STEP_DT / (1.0 + sigma * STEP_DT / 2)
    keep_j = (1.0 - gamma * STEP_DT / 2) / (1.0 + gamma * STEP_DT / 2)
    gain_j = plasma * STEP_DT / (1.0 + gamma * STEP_DT / 2)
    return (keep_e, gain_e, keep_j, gain_j)


def row_forces(elec_rows, magn_rows, normal):
    axis_of = normal // 2
    sign_of = (1 - 2 * (normal % 2)).astype(elec_rows.dtype)
    picked = (axis_of[None, :] == jnp.arange(3, dtype=jnp.int32)[:, None]).astype(elec_rows.dtype)
    elec_n = jnp.sum(elec_rows * picked, axis=0)
    magn_n = jnp.sum(magn_rows * picked, axis=0)
    energy = 0.5 * (jnp.sum(elec_rows * elec_rows, axis=0) + jnp.sum(magn_rows * magn_rows, axis=0))
    return sign_of * (elec_rows * elec_n + magn_rows * magn_n - picked * energy)


def curl_upper(electric):
    rim_x = passed_along(electric[1:3, :1], "gx", -1)
    rim_y = passed_along(electric[0::2, :, :1], "gy", -1)
    rim_z = passed_along(electric[0:2, :, :, :1], "gz", -1)
    elec_x, elec_y, elec_z = (electric[0], electric[1], electric[2])
    y_next_x = jnp.concatenate([elec_y[1:], rim_x[0]], 0)
    z_next_x = jnp.concatenate([elec_z[1:], rim_x[1]], 0)
    x_next_y = jnp.concatenate([elec_x[:, 1:], rim_y[0]], 1)
    z_next_y = jnp.concatenate([elec_z[:, 1:], rim_y[1]], 1)
    x_next_z = jnp.concatenate([elec_x[:, :, 1:], rim_z[0]], 2)
    y_next_z = jnp.concatenate([elec_y[:, :, 1:], rim_z[1]], 2)
    curl_x = z_next_y - elec_z - (y_next_z - elec_y)
    curl_y = x_next_z - elec_x - (z_next_x - elec_z)
    curl_z = y_next_x - elec_y - (x_next_y - elec_x)
    return jnp.stack([curl_x, curl_y, curl_z])


def curl_lower(magnetic):
    rim_x = passed_along(magnetic[1:3, -1:], "gx", 1)
    rim_y = passed_along(magnetic[0::2, :, -1:], "gy", 1)
    rim_z = passed_along(magnetic[0:2, :, :, -1:], "gz", 1)
    magn_x, magn_y, magn_z = (magnetic[0], magnetic[1], magnetic[2])
    y_prev_x = jnp.concatenate([rim_x[0], magn_y[:-1]], 0)
    z_prev_x = jnp.concatenate([rim_x[1], magn_z[:-1]], 0)
    x_prev_y = jnp.concatenate([rim_y[0], magn_x[:, :-1]], 1)
    z_prev_y = jnp.concatenate([rim_y[1], magn_z[:, :-1]], 1)
    x_prev_z = jnp.concatenate([rim_z[0], magn_x[:, :, :-1]], 2)
    y_prev_z = jnp.concatenate([rim_z[1], magn_y[:, :, :-1]], 2)
    curl_x = magn_z - z_prev_y - (magn_y - y_prev_z)
    curl_y = magn_x - x_prev_z - (magn_z - z_prev_x)
    curl_z = magn_y - y_prev_x - (magn_x - x_prev_y)
    return jnp.stack([curl_x, curl_y, curl_z])


def local(
    e_field,
    h_field,
    current,
    material,
    sigma_table,
    gamma_table,
    plasma_table,
    g_kernel,
    surf_cell,
    surf_owner,
    surf_tile,
    surf_normal,
    row_count,
):
    keep_e, gain_e, keep_j, gain_j = coefficients(material, sigma_table, gamma_table, plasma_table)
    electric, magnetic, drude = (e_field, h_field, current)
    slot_cells = surf_cell.reshape(-1)
    normal = surf_normal.reshape(-1)
    owners = surf_owner.reshape(-1)
    tile_ids = surf_tile.reshape(-1)
    slot_total = slot_cells.shape[0]
    live_mask = (jnp.arange(slot_total, dtype=jnp.int32) < row_count.reshape(())).astype(
        jnp.float32
    )
    summed = jnp.zeros((3, slot_total), jnp.float32)
    for moment in range(g_kernel.shape[0]):
        magnetic = magnetic - STEP_DT * curl_upper(electric)
        curl_magn = curl_lower(magnetic)
        drude = keep_j * drude + gain_j * electric
        electric = keep_e * electric + gain_e * (curl_magn - drude)
        elec_rows = electric.reshape(3, -1)[:, slot_cells]
        magn_rows = magnetic.reshape(3, -1)[:, slot_cells]
        summed = summed + g_kernel[moment] * row_forces(elec_rows, magn_rows, normal)
    row_force = FACE_AREA * summed * live_mask
    groups = lax.axis_size("gx") * lax.axis_size("gy")
    capacity = 3 * slot_total // (2 * groups)
    owner_hot = (owners[:, None] == jnp.arange(groups, dtype=jnp.int32)[None, :]).astype(jnp.int32)
    ranks = jnp.sum(jnp.cumsum(owner_hot, axis=0) * owner_hot, axis=1) - 1
    force_buf = jnp.zeros((3, capacity, groups), jnp.float32).at[:, ranks, owners].set(row_force)
    tile_buf = (
        jnp.full((1, capacity, groups), -1.0, jnp.float32)
        .at[0, ranks, owners]
        .set(tile_ids.astype(jnp.float32))
    )
    got_force, got_tile = (
        lax.all_to_all(force_buf, ("gx", "gy"), split_axis=2, concat_axis=2, tiled=True),
        lax.all_to_all(tile_buf, ("gx", "gy"), split_axis=2, concat_axis=2, tiled=True),
    )
    tile_hot = (
        got_tile[0][:, :, None] == jnp.arange(TILE_DEV, dtype=jnp.float32)[None, None, :]
    ).astype(jnp.float32)
    force = jnp.einsum("acs,cst->at", got_force, tile_hot, precision=lax.Precision.HIGHEST)
    return (electric, magnetic, force)


def solution(mesh):
    return jax.shard_map(
        local,
        mesh=mesh,
        in_specs=(
            P(None, "gx", "gy", "gz"),
            P(None, "gx", "gy", "gz"),
            P(None, "gx", "gy", "gz"),
            P("gx", "gy", "gz"),
            P(),
            P(),
            P(),
            P(),
            P("gx", "gy", "gz", None),
            P("gx", "gy", "gz", None, None),
            P("gx", "gy", "gz", None),
            P("gx", "gy", "gz", None),
            P("gx", "gy", "gz"),
        ),
        out_specs=(
            P(None, "gx", "gy", "gz"),
            P(None, "gx", "gy", "gz"),
            P(None, ("gx", "gy", "gz")),
        ),
        check_vma=False,
    )
```

profile of v0, /device:TPU:0, one launch (start us, length us, event | category | flops | bytes accessed | tf_op | source)
XLA Modules:
  0.0 190.6 jit_solution(9184814041773252684)
XLA Ops:
  11.8 4.3 %scatter_custom_fusion.1 = f32[1536]{0:T(1024)S(1)} fusion(s32[1024]{0:T(1024)S(1)} %broadcast_select_fusion, f32[1024]{0:T(1024)S(1)} %bitcast.311, f32[]{:T(128)} %constant.91.clone.1), kind=kCustom, calls=%fused_computation.263 | custom fusion | bytes 6148
  16.8 7.9 %all-to-all-start.1 = ((f32[1,192,8]{1,0,2:T(1,128)}), f32[1,192,8]{1,0,2:T(1,128)S(1)}, u32[]{:S(2)}, u32[]{:S(2)}) async-start(f32[1,192,8]{1,0,2:T(1,128)} %bitcast.99), calls=%async_computation.1 | async-start | bytes 16384 | tf_op jit(solution)/shard_map/all_to_all | solution.py:128
  37.7 2.7 %subtract_divide_fusion.1 = (f32[4,16,128]{2,1,0:T(8,128)S(1)}, pred[4,16,128]{2,1,0:T(8,128)(4,1)S(1)}, pred[4,16,128]{2,1,0:T(8,128)(4,1)S(1)}, pred[4,16,128]{2,1,0:T(8,128)(4,1)S(1)}) fusion(f32[]{:T(128)} %bitcast.2, f32[]{:T(128)} %bitcast.1, f32[]{:T(128)} %bitcast, s32[4,16,128]{2,1,0:T(8,128)} %param.16), kind=kLoop, calls=%fused_computation.152 | loop fusion | flops 98304 | bytes 90124 | tf_op jit(solution)/shard_map/div | solution.py:30
  40.4 5.7 %add_divide_fusion = (f32[4,16,128]{2,1,0:T(8,128)S(1)}, f32[4,16,128]{2,1,0:T(8,128)S(1)}, f32[4,16,128]{2,1,0:T(8,128)S(1)}) fusion(pred[4,16,128]{2,1,0:T(8,128)(4,1)S(1)} %get-tuple-element.38, pred[4,16,128]{2,1,0:T(8,128)(4,1)S(1)} %get-tuple-element.37, pred[4,16,128]{2,1,0:T(8,128)(4,1)S(1)} %get-tuple-element.36, f32[]{:T(128)} %bitcast.2, ...), kind=kLoop, calls=%fused_computation.155 | loop fusion | flops 196608 | bytes 122916 | tf_op jit(solution)/shard_map/div | solution.py:31
  50.6 3.5 %collective-permute-start.5 = (f32[2,1,16,128]{3,2,1,0:T(8,128)S(1)}, f32[2,1,16,128]{3,2,1,0:T(8,128)S(1)}, u32[]{:S(2)}, u32[]{:S(2)}) collective-permute-start(f32[2,1,16,128]{3,2,1,0:T(8,128)S(1)} %slice.704), channel_id=1, source_target_pairs={{0,8},{8,16},{16,24},{1,9},{9,17},{17,25},{2,10},{10,18},{18,26},{... | collective-permute-start | bytes 49160 | tf_op jit(solution)/shard_map/ppermute | solution.py:16
  54.2 4.3 %collective-permute-start.4 = (f32[2,4,16,1]{3,2,1,0:T(8,128)S(1)}, f32[2,4,16,1]{3,2,1,0:T(8,128)S(1)}, u32[]{:S(2)}, u32[]{:S(2)}) collective-permute-start(f32[2,4,16,1]{3,2,1,0:T(8,128)S(1)} %slice.698), channel_id=1, source_target_pairs={{0,1},{1,2},{2,3},{4,5},{5,6},{6,7},{8,9},{9,10},{10,11},{12,13},{... | collective-permute-start | bytes 1544 | tf_op jit(solution)/shard_map/ppermute | solution.py:16
  58.5 2.6 %copy.46 = f32[3,4,16,128]{0,3,2,1:T(8,128)} copy(f32[3,4,16,128]{3,2,1,0:T(8,128)S(1)} %fusion.3) | data formatting | bytes 196608 | tf_op jit(solution)/shard_map/sub | solution.py:108
  61.1 5.0 %gather_fusion.1 = f32[1024,3]{1,0:T(8,128)S(1)} fusion(f32[3,8192]{0,1:T(8,128)} %bitcast.295, s32[1024]{0:T(1024)S(1)} %broadcast_clamp_fusion), kind=kCustom, calls=%fused_computation.1 | custom fusion | bytes 28672 | tf_op jit(solution)/shard_map/gather | solution.py:113
  70.7 2.6 %copy.44 = f32[3,4,16,128]{0,3,2,1:T(8,128)} copy(f32[3,4,16,128]{3,2,1,0:T(8,128)S(1)} %fusion.5) | data formatting | bytes 196608 | tf_op jit(solution)/shard_map/add | solution.py:111
  73.3 5.0 %gather_fusion = f32[1024,3]{1,0:T(8,128)S(1)} fusion(f32[3,8192]{0,1:T(8,128)} %bitcast.296, s32[1024]{0:T(1024)S(1)} %broadcast_clamp_fusion), kind=kCustom, calls=%fused_computation | custom fusion | bytes 28672 | tf_op jit(solution)/shard_map/gather | solution.py:112
  78.9 3.0 %collective-permute-start.9 = (f32[2,4,1,128]{3,2,1,0:T(1,128)S(1)}, f32[2,4,1,128]{3,2,1,0:T(1,128)S(1)}, u32[]{:S(2)}, u32[]{:S(2)}) collective-permute-start(f32[2,4,1,128]{3,2,1,0:T(1,128)S(1)} %slice.573), channel_id=1, source_target_pairs={{0,4},{1,5},{2,6},{3,7},{8,12},{9,13},{10,14},{11,15},{16,20},{17,... | collective-permute-start | bytes 12296 | tf_op jit(solution)/shard_map/ppermute | solution.py:16
  81.9 4.3 %collective-permute-start.11 = (f32[2,1,16,128]{3,2,1,0:T(8,128)S(1)}, f32[2,1,16,128]{3,2,1,0:T(8,128)S(1)}, u32[]{:S(2)}, u32[]{:S(2)}) collective-permute-start(f32[2,1,16,128]{3,2,1,0:T(8,128)S(1)} %slice.738), channel_id=1, source_target_pairs={{0,8},{8,16},{16,24},{1,9},{9,17},{17,25},{2,10},{10,18},{18,26},{... | collective-permute-start | bytes 49160 | tf_op jit(solution)/shard_map/ppermute | solution.py:16
  86.2 4.9 %collective-permute-start.10 = (f32[2,4,16,1]{3,2,1,0:T(8,128)S(1)}, f32[2,4,16,1]{3,2,1,0:T(8,128)S(1)}, u32[]{:S(2)}, u32[]{:S(2)}) collective-permute-start(f32[2,4,16,1]{3,2,1,0:T(8,128)S(1)} %slice.732), channel_id=1, source_target_pairs={{0,1},{1,2},{2,3},{4,5},{5,6},{6,7},{8,9},{9,10},{10,11},{12,13},{... | collective-permute-start | bytes 1544 | tf_op jit(solution)/shard_map/ppermute | solution.py:16
  93.8 5.0 %gather_fusion.3 = f32[1024,3]{1,0:T(8,128)S(1)} fusion(f32[3,8192]{0,1:T(8,128)} %bitcast.297, s32[1024]{0:T(1024)S(1)} %broadcast_clamp_fusion), kind=kCustom, calls=%fused_computation.3 | custom fusion | bytes 28672 | tf_op jit(solution)/shard_map/gather | solution.py:113
  103.3 2.6 %copy.48 = f32[3,4,16,128]{0,3,2,1:T(8,128)} copy(f32[3,4,16,128]{3,2,1,0:T(8,128)S(1)} %get-tuple-element.33) | data formatting | bytes 196608 | tf_op jit(solution)/shard_map/add | solution.py:111
  106.0 5.0 %gather_fusion.2 = f32[1024,3]{1,0:T(8,128)S(1)} fusion(f32[3,8192]{0,1:T(8,128)} %bitcast.298, s32[1024]{0:T(1024)S(1)} %broadcast_clamp_fusion), kind=kCustom, calls=%fused_computation.2 | custom fusion | bytes 28672 | tf_op jit(solution)/shard_map/gather | solution.py:112
  111.5 3.0 %collective-permute-start.15 = (f32[2,4,1,128]{3,2,1,0:T(1,128)S(1)}, f32[2,4,1,128]{3,2,1,0:T(1,128)S(1)}, u32[]{:S(2)}, u32[]{:S(2)}) collective-permute-start(f32[2,4,1,128]{3,2,1,0:T(1,128)S(1)} %slice.609), channel_id=1, source_target_pairs={{0,4},{1,5},{2,6},{3,7},{8,12},{9,13},{10,14},{11,15},{16,20},{17,... | collective-permute-start | bytes 12296 | tf_op jit(solution)/shard_map/ppermute | solution.py:16
  114.5 4.3 %collective-permute-start.17 = (f32[2,1,16,128]{3,2,1,0:T(8,128)S(1)}, f32[2,1,16,128]{3,2,1,0:T(8,128)S(1)}, u32[]{:S(2)}, u32[]{:S(2)}) collective-permute-start(f32[2,1,16,128]{3,2,1,0:T(8,128)S(1)} %slice.772), channel_id=1, source_target_pairs={{0,8},{8,16},{16,24},{1,9},{9,17},{17,25},{2,10},{10,18},{18,26},{... | collective-permute-start | bytes 49160 | tf_op jit(solution)/shard_map/ppermute | solution.py:16
  118.8 5.2 %collective-permute-start.16 = (f32[2,4,16,1]{3,2,1,0:T(8,128)S(1)}, f32[2,4,16,1]{3,2,1,0:T(8,128)S(1)}, u32[]{:S(2)}, u32[]{:S(2)}) collective-permute-start(f32[2,4,16,1]{3,2,1,0:T(8,128)S(1)} %slice.766), channel_id=1, source_target_pairs={{0,1},{1,2},{2,3},{4,5},{5,6},{6,7},{8,9},{9,10},{10,11},{12,13},{... | collective-permute-start | bytes 1544 | tf_op jit(solution)/shard_map/ppermute | solution.py:16
  124.0 2.6 %copy.54 = f32[3,4,16,128]{0,3,2,1:T(8,128)} copy(f32[3,4,16,128]{3,2,1,0:T(8,128)S(1)} %fusion.9) | data formatting | bytes 196608 | tf_op jit(solution)/shard_map/sub | solution.py:108
  126.6 5.0 %gather_fusion.5 = f32[1024,3]{1,0:T(8,128)S(1)} fusion(f32[3,8192]{0,1:T(8,128)} %bitcast.299, s32[1024]{0:T(1024)S(1)} %broadcast_clamp_fusion), kind=kCustom, calls=%fused_computation.5 | custom fusion | bytes 28672 | tf_op jit(solution)/shard_map/gather | solution.py:113
  136.2 2.6 %copy.52 = f32[3,4,16,128]{0,3,2,1:T(8,128)} copy(f32[3,4,16,128]{3,2,1,0:T(8,128)S(1)} %fusion.11) | data formatting | bytes 196608 | tf_op jit(solution)/shard_map/add | solution.py:111
  138.8 5.0 %gather_fusion.4 = f32[1024,3]{1,0:T(8,128)S(1)} fusion(f32[3,8192]{0,1:T(8,128)} %bitcast.300, s32[1024]{0:T(1024)S(1)} %broadcast_clamp_fusion), kind=kCustom, calls=%fused_computation.4 | custom fusion | bytes 28672 | tf_op jit(solution)/shard_map/gather | solution.py:112
  144.4 3.0 %collective-permute-start.21 = (f32[2,4,1,128]{3,2,1,0:T(1,128)S(1)}, f32[2,4,1,128]{3,2,1,0:T(1,128)S(1)}, u32[]{:S(2)}, u32[]{:S(2)}) collective-permute-start(f32[2,4,1,128]{3,2,1,0:T(1,128)S(1)} %slice.645), channel_id=1, source_target_pairs={{0,4},{1,5},{2,6},{3,7},{8,12},{9,13},{10,14},{11,15},{16,20},{17,... | collective-permute-start | bytes 12296 | tf_op jit(solution)/shard_map/ppermute | solution.py:16
  147.4 4.3 %collective-permute-start.23 = (f32[2,1,16,128]{3,2,1,0:T(8,128)S(1)}, f32[2,1,16,128]{3,2,1,0:T(8,128)S(1)}, u32[]{:S(2)}, u32[]{:S(2)}) collective-permute-start(f32[2,1,16,128]{3,2,1,0:T(8,128)S(1)} %slice.806), channel_id=1, source_target_pairs={{0,8},{8,16},{16,24},{1,9},{9,17},{17,25},{2,10},{10,18},{18,26},{... | collective-permute-start | bytes 49160 | tf_op jit(solution)/shard_map/ppermute | solution.py:16
  151.7 5.2 %collective-permute-start.22 = (f32[2,4,16,1]{3,2,1,0:T(8,128)S(1)}, f32[2,4,16,1]{3,2,1,0:T(8,128)S(1)}, u32[]{:S(2)}, u32[]{:S(2)}) collective-permute-start(f32[2,4,16,1]{3,2,1,0:T(8,128)S(1)} %slice.800), channel_id=1, source_target_pairs={{0,1},{1,2},{2,3},{4,5},{5,6},{6,7},{8,9},{9,10},{10,11},{12,13},{... | collective-permute-start | bytes 1544 | tf_op jit(solution)/shard_map/ppermute | solution.py:16
  159.5 5.0 %gather_fusion.7 = f32[1024,3]{1,0:T(8,128)S(1)} fusion(f32[3,8192]{0,1:T(8,128)} %bitcast.301, s32[1024]{0:T(1024)S(1)} %broadcast_clamp_fusion), kind=kCustom, calls=%fused_computation.7 | custom fusion | bytes 28672 | tf_op jit(solution)/shard_map/gather | solution.py:113
  167.6 5.0 %gather_fusion.6 = f32[1024,3]{1,0:T(8,128)S(1)} fusion(f32[3,8192]{0,1:T(8,128)} %bitcast.294, s32[1024]{0:T(1024)S(1)} %broadcast_clamp_fusion), kind=kCustom, calls=%fused_computation.6 | custom fusion | bytes 28672 | tf_op jit(solution)/shard_map/gather | solution.py:112
  173.0 2.7 %fusion.50 = f32[1024,3]{0,1:T(4,128)S(1)} fusion(f32[1024,3]{0,1:T(4,128)S(1)} %copy.59, f32[1024,3]{0,1:T(4,128)S(1)} %copy.57, f32[1024,3]{0,1:T(4,128)S(1)} %copy.55, f32[1024,3]{0,1:T(4,128)S(1)} %copy.53, f32[1024,3]{0,1:T(4,128)S(1)} %copy.51, f32[1024,3]{0,1:T(4,128)S(1)} %copy.49, f32[1024,3]{0,1:T(4,128)S(1)} %copy.47, f32[1024,3]{0,1:T(4,128)S(1)} %copy.45, ...), kind=kLoop, calls=%fused_computation.195 | loop fusion | flops 101376 | bytes 172048 | tf_op jit(solution)/shard_map/mul | solution.py:115
  175.9 3.3 %scatter_custom_fusion = f32[3,1536]{0,1:T(8,128)S(1)} fusion(s32[1024]{0:T(1024)S(1)} %broadcast_select_fusion.1, f32[1024,3]{1,0:T(8,128)S(1)} %copy.60, f32[]{:T(128)} %constant.82.clone.1), kind=kCustom, calls=%fused_computation.12 | custom fusion | bytes 18436
  180.2 3.6 %all-to-all-start = ((f32[3,192,8]{1,0,2:T(4,128)}), f32[3,192,8]{1,0,2:T(4,128)S(1)}, u32[]{:S(2)}, u32[]{:S(2)}) async-start(f32[3,192,8]{1,0,2:T(4,128)} %bitcast.97), calls=%async_computation | async-start | bytes 65536 | tf_op jit(solution)/shard_map/all_to_all | solution.py:127
  183.8 5.7 %all-to-all-done = f32[3,192,8]{1,0,2:T(4,128)S(1)} async-done(((f32[3,192,8]{1,0,2:T(4,128)}), f32[3,192,8]{1,0,2:T(4,128)S(1)}, u32[]{:S(2)}, u32[]{:S(2)}) %all-to-all-start) | async-done | bytes 18464 | tf_op jit(solution)/shard_map/all_to_all | solution.py:127
  (203 shorter events, 54.0 us)
Async XLA Ops:
  1.4 44.8 %collective-permute-start = (f32[2,4,1,128]{3,2,1,0:T(1,128)S(1)}, f32[2,4,1,128]{3,2,1,0:T(1,128)S(1)}, u32[]{:S(2)}, u32[]{:S(2)}) collective-permute-start(f32[2,4,1,128]{3,2,1,0:T(1,128)S(1)} %slice.514), channel_id=1, source_target_pairs={{4,0},{5,1},{6,2},{7,3},{12,8},{13,9},{14,10},{15,11},{20,16},{21,... | collective-permute-start | bytes 12296 | tf_op jit(solution)/shard_map/ppermute | solution.py:16
  3.4 42.8 %collective-permute-start.2 = (f32[2,1,16,128]{3,2,1,0:T(8,128)S(1)}, f32[2,1,16,128]{3,2,1,0:T(8,128)S(1)}, u32[]{:S(2)}, u32[]{:S(2)}) collective-permute-start(f32[2,1,16,128]{3,2,1,0:T(8,128)S(1)} %slice.524), channel_id=1, source_target_pairs={{8,0},{16,8},{24,16},{9,1},{17,9},{25,17},{10,2},{18,10},{26,18},{... | collective-permute-start | bytes 49160 | tf_op jit(solution)/shard_map/ppermute | solution.py:16
  16.8 163.3 %all-to-all-start.1 = ((f32[1,192,8]{1,0,2:T(1,128)}), f32[1,192,8]{1,0,2:T(1,128)S(1)}, u32[]{:S(2)}, u32[]{:S(2)}) async-start(f32[1,192,8]{1,0,2:T(1,128)} %bitcast.99), calls=%async_computation.1 | async-start | bytes 16384 | tf_op jit(solution)/shard_map/all_to_all | solution.py:128
  24.7 41.8 %copy-start = (f32[3,4,16,128]{3,2,1,0:T(8,128)S(1)}, f32[3,4,16,128]{3,2,1,0:T(8,128)}, u32[]{:S(2)}) copy-start(f32[3,4,16,128]{3,2,1,0:T(8,128)} %param.13) | copy-start | bytes 294916
  24.7 41.8 %copy-start.3 = (f32[3,4,16,128]{3,2,1,0:T(8,128)S(1)}, f32[3,4,16,128]{3,2,1,0:T(8,128)}, u32[]{:S(2)}) copy-start(f32[3,4,16,128]{3,2,1,0:T(8,128)} %param.15) | copy-start | bytes 294916
  25.6 20.6 %collective-permute-start.1 = (f32[2,4,16,1]{3,2,1,0:T(8,128)S(1)}, f32[2,4,16,1]{3,2,1,0:T(8,128)S(1)}, u32[]{:S(2)}, u32[]{:S(2)}) collective-permute-start(f32[2,4,16,1]{3,2,1,0:T(8,128)S(1)} %slice.518), channel_id=1, source_target_pairs={{1,0},{2,1},{3,2},{5,4},{6,5},{7,6},{9,8},{10,9},{11,10},{13,12},{... | collective-permute-start | bytes 1544 | tf_op jit(solution)/shard_map/ppermute | solution.py:16
  48.2 18.1 %collective-permute-start.3 = (f32[2,4,1,128]{3,2,1,0:T(1,128)S(1)}, f32[2,4,1,128]{3,2,1,0:T(1,128)S(1)}, u32[]{:S(2)}, u32[]{:S(2)}) collective-permute-start(f32[2,4,1,128]{3,2,1,0:T(1,128)S(1)} %slice.531), channel_id=1, source_target_pairs={{0,4},{1,5},{2,6},{3,7},{8,12},{9,13},{10,14},{11,15},{16,20},{17,... | collective-permute-start | bytes 12296 | tf_op jit(solution)/shard_map/ppermute | solution.py:16
  50.6 15.8 %collective-permute-start.5 = (f32[2,1,16,128]{3,2,1,0:T(8,128)S(1)}, f32[2,1,16,128]{3,2,1,0:T(8,128)S(1)}, u32[]{:S(2)}, u32[]{:S(2)}) collective-permute-start(f32[2,1,16,128]{3,2,1,0:T(8,128)S(1)} %slice.704), channel_id=1, source_target_pairs={{0,8},{8,16},{16,24},{1,9},{9,17},{17,25},{2,10},{10,18},{18,26},{... | collective-permute-start | bytes 49160 | tf_op jit(solution)/shard_map/ppermute | solution.py:16
  54.2 12.2 %collective-permute-start.4 = (f32[2,4,16,1]{3,2,1,0:T(8,128)S(1)}, f32[2,4,16,1]{3,2,1,0:T(8,128)S(1)}, u32[]{:S(2)}, u32[]{:S(2)}) collective-permute-start(f32[2,4,16,1]{3,2,1,0:T(8,128)S(1)} %slice.698), channel_id=1, source_target_pairs={{0,1},{1,2},{2,3},{4,5},{5,6},{6,7},{8,9},{9,10},{10,11},{12,13},{... | collective-permute-start | bytes 1544 | tf_op jit(solution)/shard_map/ppermute | solution.py:16
  61.1 17.6 %copy-start.2 = (f32[3,4,16,128]{3,2,1,0:T(8,128)S(1)}, f32[3,4,16,128]{3,2,1,0:T(8,128)}, u32[]{:S(2)}) copy-start(f32[3,4,16,128]{3,2,1,0:T(8,128)} %param.14) | copy-start | bytes 294916
  66.7 11.8 %collective-permute-start.6 = (f32[2,4,1,128]{3,2,1,0:T(1,128)S(1)}, f32[2,4,1,128]{3,2,1,0:T(1,128)S(1)}, u32[]{:S(2)}, u32[]{:S(2)}) collective-permute-start(f32[2,4,1,128]{3,2,1,0:T(1,128)S(1)} %slice.556), channel_id=1, source_target_pairs={{4,0},{5,1},{6,2},{7,3},{12,8},{13,9},{14,10},{15,11},{20,16},{21,... | collective-permute-start | bytes 12296 | tf_op jit(solution)/shard_map/ppermute | solution.py:16
  68.0 10.6 %collective-permute-start.8 = (f32[2,1,16,128]{3,2,1,0:T(8,128)S(1)}, f32[2,1,16,128]{3,2,1,0:T(8,128)S(1)}, u32[]{:S(2)}, u32[]{:S(2)}) collective-permute-start(f32[2,1,16,128]{3,2,1,0:T(8,128)S(1)} %slice.722), channel_id=1, source_target_pairs={{8,0},{16,8},{24,16},{9,1},{17,9},{25,17},{10,2},{18,10},{26,18},{... | collective-permute-start | bytes 49160 | tf_op jit(solution)/shard_map/ppermute | solution.py:16
  69.3 9.2 %collective-permute-start.7 = (f32[2,4,16,1]{3,2,1,0:T(8,128)S(1)}, f32[2,4,16,1]{3,2,1,0:T(8,128)S(1)}, u32[]{:S(2)}, u32[]{:S(2)}) collective-permute-start(f32[2,4,16,1]{3,2,1,0:T(8,128)S(1)} %slice.716), channel_id=1, source_target_pairs={{1,0},{2,1},{3,2},{5,4},{6,5},{7,6},{9,8},{10,9},{11,10},{13,12},{... | collective-permute-start | bytes 1544 | tf_op jit(solution)/shard_map/ppermute | solution.py:16
  78.9 20.1 %collective-permute-start.9 = (f32[2,4,1,128]{3,2,1,0:T(1,128)S(1)}, f32[2,4,1,128]{3,2,1,0:T(1,128)S(1)}, u32[]{:S(2)}, u32[]{:S(2)}) collective-permute-start(f32[2,4,1,128]{3,2,1,0:T(1,128)S(1)} %slice.573), channel_id=1, source_target_pairs={{0,4},{1,5},{2,6},{3,7},{8,12},{9,13},{10,14},{11,15},{16,20},{17,... | collective-permute-start | bytes 12296 | tf_op jit(solution)/shard_map/ppermute | solution.py:16
  81.9 17.1 %collective-permute-start.11 = (f32[2,1,16,128]{3,2,1,0:T(8,128)S(1)}, f32[2,1,16,128]{3,2,1,0:T(8,128)S(1)}, u32[]{:S(2)}, u32[]{:S(2)}) collective-permute-start(f32[2,1,16,128]{3,2,1,0:T(8,128)S(1)} %slice.738), channel_id=1, source_target_pairs={{0,8},{8,16},{16,24},{1,9},{9,17},{17,25},{2,10},{10,18},{18,26},{... | collective-permute-start | bytes 49160 | tf_op jit(solution)/shard_map/ppermute | solution.py:16
  86.2 12.8 %collective-permute-start.10 = (f32[2,4,16,1]{3,2,1,0:T(8,128)S(1)}, f32[2,4,16,1]{3,2,1,0:T(8,128)S(1)}, u32[]{:S(2)}, u32[]{:S(2)}) collective-permute-start(f32[2,4,16,1]{3,2,1,0:T(8,128)S(1)} %slice.732), channel_id=1, source_target_pairs={{0,1},{1,2},{2,3},{4,5},{5,6},{6,7},{8,9},{9,10},{10,11},{12,13},{... | collective-permute-start | bytes 1544 | tf_op jit(solution)/shard_map/ppermute | solution.py:16
  99.3 11.8 %collective-permute-start.12 = (f32[2,4,1,128]{3,2,1,0:T(1,128)S(1)}, f32[2,4,1,128]{3,2,1,0:T(1,128)S(1)}, u32[]{:S(2)}, u32[]{:S(2)}) collective-permute-start(f32[2,4,1,128]{3,2,1,0:T(1,128)S(1)} %slice.592), channel_id=1, source_target_pairs={{4,0},{5,1},{6,2},{7,3},{12,8},{13,9},{14,10},{15,11},{20,16},{21,... | collective-permute-start | bytes 12296 | tf_op jit(solution)/shard_map/ppermute | solution.py:16
  100.6 10.6 %collective-permute-start.14 = (f32[2,1,16,128]{3,2,1,0:T(8,128)S(1)}, f32[2,1,16,128]{3,2,1,0:T(8,128)S(1)}, u32[]{:S(2)}, u32[]{:S(2)}) collective-permute-start(f32[2,1,16,128]{3,2,1,0:T(8,128)S(1)} %slice.756), channel_id=1, source_target_pairs={{8,0},{16,8},{24,16},{9,1},{17,9},{25,17},{10,2},{18,10},{26,18},{... | collective-permute-start | bytes 49160 | tf_op jit(solution)/shard_map/ppermute | solution.py:16
  101.9 9.2 %collective-permute-start.13 = (f32[2,4,16,1]{3,2,1,0:T(8,128)S(1)}, f32[2,4,16,1]{3,2,1,0:T(8,128)S(1)}, u32[]{:S(2)}, u32[]{:S(2)}) collective-permute-start(f32[2,4,16,1]{3,2,1,0:T(8,128)S(1)} %slice.750), channel_id=1, source_target_pairs={{1,0},{2,1},{3,2},{5,4},{6,5},{7,6},{9,8},{10,9},{11,10},{13,12},{... | collective-permute-start | bytes 1544 | tf_op jit(solution)/shard_map/ppermute | solution.py:16
  111.5 20.4 %collective-permute-start.15 = (f32[2,4,1,128]{3,2,1,0:T(1,128)S(1)}, f32[2,4,1,128]{3,2,1,0:T(1,128)S(1)}, u32[]{:S(2)}, u32[]{:S(2)}) collective-permute-start(f32[2,4,1,128]{3,2,1,0:T(1,128)S(1)} %slice.609), channel_id=1, source_target_pairs={{0,4},{1,5},{2,6},{3,7},{8,12},{9,13},{10,14},{11,15},{16,20},{17,... | collective-permute-start | bytes 12296 | tf_op jit(solution)/shard_map/ppermute | solution.py:16
  114.5 17.3 %collective-permute-start.17 = (f32[2,1,16,128]{3,2,1,0:T(8,128)S(1)}, f32[2,1,16,128]{3,2,1,0:T(8,128)S(1)}, u32[]{:S(2)}, u32[]{:S(2)}) collective-permute-start(f32[2,1,16,128]{3,2,1,0:T(8,128)S(1)} %slice.772), channel_id=1, source_target_pairs={{0,8},{8,16},{16,24},{1,9},{9,17},{17,25},{2,10},{10,18},{18,26},{... | collective-permute-start | bytes 49160 | tf_op jit(solution)/shard_map/ppermute | solution.py:16
  118.8 13.0 %collective-permute-start.16 = (f32[2,4,16,1]{3,2,1,0:T(8,128)S(1)}, f32[2,4,16,1]{3,2,1,0:T(8,128)S(1)}, u32[]{:S(2)}, u32[]{:S(2)}) collective-permute-start(f32[2,4,16,1]{3,2,1,0:T(8,128)S(1)} %slice.766), channel_id=1, source_target_pairs={{0,1},{1,2},{2,3},{4,5},{5,6},{6,7},{8,9},{9,10},{10,11},{12,13},{... | collective-permute-start | bytes 1544 | tf_op jit(solution)/shard_map/ppermute | solution.py:16
  132.2 11.8 %collective-permute-start.18 = (f32[2,4,1,128]{3,2,1,0:T(1,128)S(1)}, f32[2,4,1,128]{3,2,1,0:T(1,128)S(1)}, u32[]{:S(2)}, u32[]{:S(2)}) collective-permute-start(f32[2,4,1,128]{3,2,1,0:T(1,128)S(1)} %slice.628), channel_id=1, source_target_pairs={{4,0},{5,1},{6,2},{7,3},{12,8},{13,9},{14,10},{15,11},{20,16},{21,... | collective-permute-start | bytes 12296 | tf_op jit(solution)/shard_map/ppermute | solution.py:16
  133.5 10.6 %collective-permute-start.20 = (f32[2,1,16,128]{3,2,1,0:T(8,128)S(1)}, f32[2,1,16,128]{3,2,1,0:T(8,128)S(1)}, u32[]{:S(2)}, u32[]{:S(2)}) collective-permute-start(f32[2,1,16,128]{3,2,1,0:T(8,128)S(1)} %slice.790), channel_id=1, source_target_pairs={{8,0},{16,8},{24,16},{9,1},{17,9},{25,17},{10,2},{18,10},{26,18},{... | collective-permute-start | bytes 49160 | tf_op jit(solution)/shard_map/ppermute | solution.py:16
  134.8 9.2 %collective-permute-start.19 = (f32[2,4,16,1]{3,2,1,0:T(8,128)S(1)}, f32[2,4,16,1]{3,2,1,0:T(8,128)S(1)}, u32[]{:S(2)}, u32[]{:S(2)}) collective-permute-start(f32[2,4,16,1]{3,2,1,0:T(8,128)S(1)} %slice.784), channel_id=1, source_target_pairs={{1,0},{2,1},{3,2},{5,4},{6,5},{7,6},{9,8},{10,9},{11,10},{13,12},{... | collective-permute-start | bytes 1544 | tf_op jit(solution)/shard_map/ppermute | solution.py:16
  144.2 23.4 %copy-start.1 = (f32[3,4,16,128]{3,2,1,0:T(8,128)}, f32[3,4,16,128]{3,2,1,0:T(8,128)S(1)}, u32[]{:S(2)}) copy-start(f32[3,4,16,128]{3,2,1,0:T(8,128)S(1)} %fusion.12) | copy-start | bytes 294916
  144.4 20.4 %collective-permute-start.21 = (f32[2,4,1,128]{3,2,1,0:T(1,128)S(1)}, f32[2,4,1,128]{3,2,1,0:T(1,128)S(1)}, u32[]{:S(2)}, u32[]{:S(2)}) collective-permute-start(f32[2,4,1,128]{3,2,1,0:T(1,128)S(1)} %slice.645), channel_id=1, source_target_pairs={{0,4},{1,5},{2,6},{3,7},{8,12},{9,13},{10,14},{11,15},{16,20},{17,... | collective-permute-start | bytes 12296 | tf_op jit(solution)/shard_map/ppermute | solution.py:16
  147.4 17.3 %collective-permute-start.23 = (f32[2,1,16,128]{3,2,1,0:T(8,128)S(1)}, f32[2,1,16,128]{3,2,1,0:T(8,128)S(1)}, u32[]{:S(2)}, u32[]{:S(2)}) collective-permute-start(f32[2,1,16,128]{3,2,1,0:T(8,128)S(1)} %slice.806), channel_id=1, source_target_pairs={{0,8},{8,16},{16,24},{1,9},{9,17},{17,25},{2,10},{10,18},{18,26},{... | collective-permute-start | bytes 49160 | tf_op jit(solution)/shard_map/ppermute | solution.py:16
  151.7 13.0 %collective-permute-start.22 = (f32[2,4,16,1]{3,2,1,0:T(8,128)S(1)}, f32[2,4,16,1]{3,2,1,0:T(8,128)S(1)}, u32[]{:S(2)}, u32[]{:S(2)}) collective-permute-start(f32[2,4,16,1]{3,2,1,0:T(8,128)S(1)} %slice.800), channel_id=1, source_target_pairs={{0,1},{1,2},{2,3},{4,5},{5,6},{6,7},{8,9},{9,10},{10,11},{12,13},{... | collective-permute-start | bytes 1544 | tf_op jit(solution)/shard_map/ppermute | solution.py:16
  164.9 25.7 %copy-start.4 = (f32[3,4,16,128]{3,2,1,0:T(8,128)}, f32[3,4,16,128]{3,2,1,0:T(8,128)S(1)}, u32[]{:S(2)}) copy-start(f32[3,4,16,128]{3,2,1,0:T(8,128)S(1)} %fusion.14) | copy-start | bytes 294916
  180.2 9.4 %all-to-all-start = ((f32[3,192,8]{1,0,2:T(4,128)}), f32[3,192,8]{1,0,2:T(4,128)S(1)}, u32[]{:S(2)}, u32[]{:S(2)}) async-start(f32[3,192,8]{1,0,2:T(4,128)} %bitcast.97), calls=%async_computation | async-start | bytes 65536 | tf_op jit(solution)/shard_map/all_to_all | solution.py:127
where the time goes:
time: 193 us; the launch traced here: 191 us
  local copies, waits for them, and re-layouts  83.1 us (43%)
  starting transfers between devices  74.3 us (38%)
  other arithmetic  23.8 us (12%)
  waiting for transfers between devices  5.8 us (3%)
  between operations  2.54 us (1%)
    ppermute x24, starting transfers between devices, passed_along(): return lax.ppermute(shard, axis, pairs)  62.8 us
    gather x8, local copies, waits for them, and re-layouts, local(): magn_rows = magnetic.reshape(3, -1)[:, slot_cells]  20.8 us
    gather x8, local copies, waits for them, and re-layouts, local(): elec_rows = electric.reshape(3, -1)[:, slot_cells]  20.7 us
    add x4, local copies, waits for them, and re-layouts, local(): electric = keep_e * electric + gain_e * (curl_magn - drude)  10.5 us
    sub x4, local copies, waits for them, and re-layouts, local(): magnetic = magnetic - STEP_DT * curl_upper(electric)  10.5 us
    unnamed x15, local copies, waits for them, and re-layouts  9.26 us
    all_to_all x1, starting transfers between devices, local(): lax.all_to_all(tile_buf, ('gx', 'gy'), split_axis=2, concat_axis=2, tiled...  7.86 us
    all_to_all x1, waiting for transfers between devices, local(): lax.all_to_all(force_buf, ('gx', 'gy'), split_axis=2, concat_axis=2, tile...  5.74 us
  transfers between devices with their start and end apart: 26, of which 1 were waited for; matrix products, arithmetic and copies ran while one was open for 56% of the time, Pallas kernels for 0%

commit v1 on v0

v1 whole, which is shorter than its diff:
```python
import functools

import jax
import jax.numpy as jnp
from jax import lax
from jax.experimental import pallas as pl
from jax.experimental.pallas import tpu as pltpu
from jax.sharding import PartitionSpec as P

STEP_DT = 0.5
FACE_AREA = 0.25
TILE_DEV = 128
PAIRS = ((0, 0), (0, 1), (0, 2), (1, 1), (1, 2), (2, 2))
AXES = ("gx", "gy", "gz")
VMEM = pl.BlockSpec(memory_space=pltpu.VMEM)
SMEM = pl.BlockSpec(memory_space=pltpu.SMEM)


def partner(index, size, second):
    if not second:
        return index ^ 1
    return (index - 1) % size if index % 2 == 0 else (index + 1) % size


def full_swap(sizes, second_x=None, second_y=None, second_z=None, local_ends=False):
    n_x, n_y, n_z = sizes
    pairs = []
    for x in range(n_x):
        for y in range(n_y):
            for z in range(n_z):
                to = [x, y, z]
                if second_x is not None:
                    if local_ends and second_x and x in (0, n_x - 1):
                        to[1] = y ^ 1
                    else:
                        to[0] = partner(x, n_x, second_x)
                if second_y is not None:
                    to[1] = partner(y, n_y, second_y)
                if second_z is not None:
                    to[2] = partner(z, n_z, second_z)
                pairs.append(((x * n_y + y) * n_z + z, (to[0] * n_y + to[1]) * n_z + to[2]))
    return pairs


def fields_of(e_ref, h_ref, j_ref, m_ref, planes):
    out = []
    for ref in (e_ref, h_ref, j_ref):
        for comp in range(3):
            for plane in range(planes):
                out.append(ref[comp, plane])
    for plane in range(planes):
        out.append((m_ref[plane] + 1).astype(jnp.float32))
    return out


def pack_kernel(depth, e_ref, h_ref, j_ref, m_ref, brick_ref, even_ref, odd_ref):
    planes, rows, lanes = m_ref.shape
    per_tile = lanes // depth
    lane = lax.broadcasted_iota(jnp.int32, (rows, lanes), 1)
    group = lane // depth
    fields = fields_of(e_ref, h_ref, j_ref, m_ref, planes)
    tiles = even_ref.shape[0]
    low = [jnp.zeros((rows, lanes), jnp.float32) for _ in range(tiles)]
    high = [jnp.zeros((rows, lanes), jnp.float32) for _ in range(tiles)]
    for j, value in enumerate(fields):
        brick_ref[j] = value
        tile, slot = j // per_tile, j % per_tile
        up = pltpu.roll(value, depth * slot, 1) if slot else value
        down = pltpu.roll(value, lanes - depth * slot, 1) if slot else value
        low[tile] = jnp.where(group == slot, up, low[tile])
        high[tile] = jnp.where(group == per_tile - 1 - slot, down, high[tile])
    is_even = lax.axis_index("gz") % 2 == 0
    for tile in range(tiles):
        even_ref[tile] = jnp.where(is_even, high[tile], low[tile])
        odd_ref[tile] = jnp.where(is_even, low[tile], high[tile])


def rows_kernel(n_in, n_y, *refs):
    ins, outs = refs[:n_in], refs[n_in:]
    is_odd = lax.axis_index("gy") % 2
    at = 0
    for ref in ins:
        count, rows, _ = ref.shape
        for which, out in enumerate(outs):
            last = (1 - is_odd) if which == 0 else is_odd
            start = pl.multiple_of(last * (rows - 8), 8)
            out[pl.ds(at, count)] = ref[:, pl.ds(start, 8), :]
        at += count


def main_kernel(sizes, steps, materials, counts, *refs):
    n_x, n_y, n_z = sizes
    n_in = len(counts)
    n_ghost = 1 if n_y == 2 else 2
    parts, refs = refs[:n_in], refs[n_in:]
    ghosts, refs = refs[:n_ghost], refs[n_ghost:]
    sigma_ref, gamma_ref, plasma_ref, g_ref, count_ref = refs[:5]
    cell_ref, owner_ref, tile_ref, normal_ref = refs[5:9]
    e_out, h_out, part_out = refs[9:12]
    field, coef, gain_h, tensor = refs[12:16]
    _, rows, lanes = parts[0].shape
    planes = e_out.shape[1]
    depth = steps
    per_tile = lanes // depth
    x, y, z = (lax.axis_index(a) for a in AXES)
    even_x, even_y, even_z = x % 2 == 0, y % 2 == 0, z % 2 == 0
    low_x, high_x = x > 0, x < n_x - 1
    low_y, high_y = y > 0, y < n_y - 1
    low_z, high_z = z > 0, z < n_z - 1
    row8 = lax.broadcasted_iota(jnp.int32, (8, lanes), 0)
    lower_from = jnp.where(low_y, 8 - depth, 8)
    upper_to = jnp.where(high_y, depth, 0)
    lower_rows = row8 >= lower_from
    upper_rows = row8 < upper_to
    one_side = (row8 >= jnp.where(even_y, 0, lower_from)) & (row8 < jnp.where(even_y, upper_to, 8))

    offsets = [sum(counts[:i]) for i in range(n_in)]

    def ghost_rows(at):
        if n_ghost == 1:
            value = ghosts[0][at]
            return jnp.where(one_side, value, 0.0)
        first, second = ghosts[0][at], ghosts[1][at]
        upper = jnp.where(even_y, first, second)
        lower = jnp.where(even_y, second, first)
        return jnp.where(upper_rows, upper, jnp.where(lower_rows, lower, 0.0))

    def whole(part, j):
        return jnp.concatenate([parts[part][j], ghost_rows(offsets[part] + j)], 0)

    full_rows = rows + 8
    lane = lax.broadcasted_iota(jnp.int32, (full_rows, lanes), 1)
    upper_lanes = lane < jnp.where(high_z, depth, 0)
    lower_lanes = lane >= jnp.where(low_z, lanes - depth, lanes)
    n_fields = 10
    z_tiles = counts[3]

    def edges(base):
        out = []
        for tile in range(z_tiles):
            first, second = whole(base, tile), whole(base + 1, tile)
            out.append((jnp.where(even_z, first, second), jnp.where(even_z, second, first)))
        return out

    own_edges, first_edges, second_edges = edges(3), edges(5), edges(7)
    for cls in range(3):
        for j in range(n_fields * planes):
            tile, slot = j // per_tile, j % per_tile
            if cls == 1:
                main = whole(0, j)
                upper, lower = own_edges[tile]
            else:
                first, second = whole(1, j), whole(2, j)
                take_first = even_x if cls == 2 else jnp.logical_not(even_x)
                valid = high_x if cls == 2 else low_x
                main = jnp.where(valid, jnp.where(take_first, first, second), 0.0)
                upper = jnp.where(valid, jnp.where(take_first, first_edges[tile][0], second_edges[tile][0]), 0.0)
                lower = jnp.where(valid, jnp.where(take_first, first_edges[tile][1], second_edges[tile][1]), 0.0)
            if slot:
                upper = pltpu.roll(upper, lanes - depth * slot, 1)
                lower = pltpu.roll(lower, depth * slot, 1)
            side = jnp.where(upper_lanes, upper, jnp.where(lower_lanes, lower, 0.0))
            at = cls * planes + j % planes
            field[j // planes, at, :, :lanes] = main
            field[j // planes, at, :, lanes:] = side

    wide = 2 * lanes

    def splat(value):
        return jnp.full((8, lanes), value, jnp.float32)

    table = []
    for which in range(materials):
        sigma, gamma, plasma = splat(sigma_ref[which]), splat(gamma_ref[which]), splat(plasma_ref[which])
        table.append((
            (1.0 - sigma * STEP_DT / 2) / (1.0 + sigma * STEP_DT / 2),
            STEP_DT / (1.0 + sigma * STEP_DT / 2),
            (1.0 - gamma * STEP_DT / 2) / (1.0 + gamma * STEP_DT / 2),
            plasma * STEP_DT / (1.0 + gamma * STEP_DT / 2),
        ))
    for plane in range(1, 3 * planes - 1):
        for r in range(0, full_rows, 8):
            for c in range(0, wide, lanes):
                code = field[9, plane, r : r + 8, c : c + lanes]
                for which in range(4):
                    value = jnp.zeros((8, lanes), jnp.float32)
                    for m in range(materials):
                        value = jnp.where(code == float(m + 1), table[m][which], value)
                    coef[which, plane, r : r + 8, c : c + lanes] = value

    row = lax.broadcasted_iota(jnp.int32, (full_rows, wide), 0)
    col = lax.broadcasted_iota(jnp.int32, (full_rows, wide), 1)
    inside = (row < jnp.where(low_y, full_rows, full_rows - depth)) & (col < jnp.where(low_z, wide, wide - depth))
    gain = jnp.where(inside, STEP_DT, 0.0)
    gain_h[1] = gain
    gain_h[0] = jnp.where(low_x, gain, 0.0)

    def next_y(v):
        return pltpu.roll(v, full_rows - 1, 0)

    def next_z(v):
        return pltpu.roll(v, wide - 1, 1)

    def prev_y(v):
        return pltpu.roll(v, 1, 0)

    def prev_z(v):
        return pltpu.roll(v, 1, 1)

    last = 3 * planes - 1
    for t in range(1, steps + 1):
        for plane in range(t - 1, last - t + 1):
            ex, ey, ez = field[0, plane], field[1, plane], field[2, plane]
            hx, hy, hz = field[3, plane], field[4, plane], field[5, plane]
            ey_x, ez_x = field[1, plane + 1], field[2, plane + 1]
            dt = gain_h[0 if plane < planes else 1]
            hy = hy - dt * ((next_z(ex) - ex) - (ez_x - ez))
            hz = hz - dt * ((ey_x - ey) - (next_y(ex) - ex))
            field[4, plane] = hy
            field[5, plane] = hz
            if plane < t:
                continue
            hx = hx - dt * ((next_y(ez) - ez) - (next_z(ey) - ey))
            field[3, plane] = hx
            hy_x, hz_x = field[4, plane - 1], field[5, plane - 1]
            keep_e, gain_e, keep_j, gain_j = (coef[i, plane] for i in range(4))
            curl_x = (hz - prev_y(hz)) - (hy - prev_z(hy))
            curl_y = (hx - prev_z(hx)) - (hz - hz_x)
            curl_z = (hy - hy_x) - (hx - prev_y(hx))
            for comp, (old, curl) in enumerate(((ex, curl_x), (ey, curl_y), (ez, curl_z))):
                drude = keep_j * field[6 + comp, plane] + gain_j * old
                field[6 + comp, plane] = drude
                field[comp, plane] = keep_e * old + gain_e * (curl - drude)
        g = g_ref[t - 1]
        for plane in range(planes):
            e = [field[i, planes + plane, :rows, :lanes] for i in range(3)]
            h = [field[3 + i, planes + plane, :rows, :lanes] for i in range(3)]
            prod = {p: e[p[0]] * e[p[1]] + h[p[0]] * h[p[1]] for p in PAIRS}
            energy = 0.5 * (prod[0, 0] + prod[1, 1] + prod[2, 2])
            for i, p in enumerate(PAIRS):
                value = prod[p] - energy if p[0] == p[1] else prod[p]
                value = g * value
                if t > 1:
                    value = tensor[i, pl.ds(plane * rows, rows), :] + value
                tensor[i, pl.ds(plane * rows, rows), :] = value
            if t == steps:
                for i in range(3):
                    e_out[i, plane] = e[i]
                    h_out[i, plane] = h[i]

    def halves(v):
        high = v.astype(jnp.bfloat16)
        return high, (v - high.astype(jnp.float32)).astype(jnp.bfloat16)

    cells = planes * rows
    high, low = halves(tensor[...].reshape(len(PAIRS) * cells, lanes))
    lhs = jnp.concatenate([high, low], 1)
    slots = cell_ref.shape[1]
    owners = part_out.shape[0]
    chunk = 256
    total = jnp.zeros((2 * owners * 8, TILE_DEV), jnp.float32)
    for at in range(0, slots, chunk):
        cell = cell_ref[:, at : at + chunk]
        owner = owner_ref[:, at : at + chunk]
        normal = normal_ref[:, at : at + chunk]
        tile = tile_ref[:, at : at + chunk]
        live = (at + lax.broadcasted_iota(jnp.int32, (1, chunk), 1)) < count_ref[0]
        hot = jnp.where(lax.broadcasted_iota(jnp.int32, (lanes, chunk), 0) == cell % lanes, 1.0, 0.0).astype(jnp.bfloat16)
        picked = jnp.dot(lhs, jnp.concatenate([hot, hot], 0), preferred_element_type=jnp.float32)
        in_row = lax.broadcasted_iota(jnp.int32, (cells, chunk), 0) == cell // lanes
        vals = {
            p: jnp.sum(jnp.where(in_row, picked[i * cells : (i + 1) * cells], 0.0), axis=0, keepdims=True)
            for i, p in enumerate(PAIRS)
        }
        axis = normal // 2
        sign = (1 - 2 * (normal % 2)).astype(jnp.float32)
        scale = jnp.where(live, FACE_AREA * sign, 0.0)
        row_force = []
        for i in range(3):
            by = [vals[min(i, a), max(i, a)] for a in range(3)]
            row_force.append(scale * jnp.where(axis == 0, by[0], jnp.where(axis == 1, by[1], by[2])))
        stacked = jnp.concatenate(row_force + [jnp.zeros((5, chunk), jnp.float32)], 0)
        spread = jnp.concatenate([jnp.where(owner == o, stacked, 0.0) for o in range(owners)], 0)
        a_high, a_low = halves(spread)
        a = jnp.concatenate([a_high, a_low], 0)
        tile_hot = jnp.where(lax.broadcasted_iota(jnp.int32, (TILE_DEV, chunk), 0) == tile, 1.0, 0.0).astype(jnp.bfloat16)
        total = total + lax.dot_general(a, tile_hot, (((1,), (1,)), ((), ())), preferred_element_type=jnp.float32)
    part = total[: owners * 8] + total[owners * 8 :]
    for o in range(owners):
        part_out[o] = part[o * 8 : (o + 1) * 8]


def local(sizes, e_field, h_field, current, material, sigma_table, gamma_table, plasma_table, g_kernel,
          surf_cell, surf_owner, surf_tile, surf_normal, row_count):
    n_x, n_y, n_z = sizes
    steps = g_kernel.shape[0]
    planes, rows, lanes = material.shape
    f32 = jnp.float32
    n_msg = 10 * planes
    z_tiles = -(-n_msg * steps // lanes)
    brick, z_first, z_second = pl.pallas_call(
        functools.partial(pack_kernel, steps),
        out_shape=(
            jax.ShapeDtypeStruct((n_msg, rows, lanes), f32),
            jax.ShapeDtypeStruct((z_tiles, rows, lanes), f32),
            jax.ShapeDtypeStruct((z_tiles, rows, lanes), f32),
        ),
        in_specs=[VMEM] * 4,
        out_specs=(VMEM,) * 3,
        name="pack",
    )(e_field, h_field, current, material)

    def send(value, **how):
        return lax.ppermute(value, AXES, full_swap(sizes, **how))

    parts = [
        brick,
        send(brick, second_x=False),
        send(brick, second_x=True, local_ends=True),
        send(z_first, second_z=False),
        send(z_second, second_z=True),
        send(z_first, second_x=False, second_z=False),
        send(z_second, second_x=False, second_z=True),
        send(z_first, second_x=True, second_z=False),
        send(z_second, second_x=True, second_z=True),
    ]
    counts = [p.shape[0] for p in parts]
    n_ghost = 1 if n_y == 2 else 2
    outgoing = pl.pallas_call(
        functools.partial(rows_kernel, len(parts), n_y),
        out_shape=[jax.ShapeDtypeStruct((sum(counts), 8, lanes), f32)] * n_ghost,
        in_specs=[VMEM] * len(parts),
        out_specs=[VMEM] * n_ghost,
        name="rows",
    )(*parts)
    ghosts = [send(v, second_y=bool(i)) for i, v in enumerate(outgoing)]

    owners = n_x * n_y
    slots = surf_cell.size
    wide = 2 * lanes
    e_out, h_out, part = pl.pallas_call(
        functools.partial(main_kernel, sizes, steps, sigma_table.shape[0], counts),
        out_shape=(
            jax.ShapeDtypeStruct(e_field.shape, f32),
            jax.ShapeDtypeStruct(h_field.shape, f32),
            jax.ShapeDtypeStruct((owners, 8, TILE_DEV), f32),
        ),
        in_specs=[VMEM] * (len(parts) + n_ghost) + [SMEM] * 5 + [VMEM] * 4,
        out_specs=(VMEM,) * 3,
        scratch_shapes=[
            pltpu.VMEM((10, 3 * planes, rows + 8, wide), f32),
            pltpu.VMEM((4, 3 * planes, rows + 8, wide), f32),
            pltpu.VMEM((2, rows + 8, wide), f32),
            pltpu.VMEM((len(PAIRS), planes * rows, lanes), f32),
        ],
        name="march",
    )(*parts, *ghosts, sigma_table, gamma_table, plasma_table, g_kernel, row_count.reshape(1),
      surf_cell.reshape(1, slots), surf_owner.reshape(1, slots), surf_tile.reshape(1, slots), surf_normal.reshape(1, slots))
    got = lax.all_to_all(part, ("gx", "gy"), split_axis=0, concat_axis=0, tiled=True)
    force = jnp.sum(got, axis=0)[:3]
    return e_out, h_out, force


def solution(mesh):
    sizes = tuple(mesh.shape[a] for a in AXES)
    return jax.shard_map(
        functools.partial(local, sizes),
        mesh=mesh,
        in_specs=(
            P(None, "gx", "gy", "gz"),
            P(None, "gx", "gy", "gz"),
            P(None, "gx", "gy", "gz"),
            P("gx", "gy", "gz"),
            P(),
            P(),
            P(),
            P(),
            P("gx", "gy", "gz", None),
            P("gx", "gy", "gz", None, None),
            P("gx", "gy", "gz", None),
            P("gx", "gy", "gz", None),
            P("gx", "gy", "gz"),
        ),
        out_specs=(
            P(None, "gx", "gy", "gz"),
            P(None, "gx", "gy", "gz"),
            P(None, ("gx", "gy", "gz")),
        ),
        check_vma=False,
    )
```

time: 193 us -> 45.5 us (0.24); the launches traced: 191 us -> 45.2 us
  local copies, waits for them, and re-layouts: 83.1 us -> 2.84 us
  starting transfers between devices: 74.3 us -> 17.1 us
  other arithmetic: 23.8 us -> 0.01 us
  blocking collectives: 0 us -> 10.3 us
  Pallas kernels: 0 us -> 8.75 us
    ppermute x24 -> x9, starting transfers between devices: 62.8 us -> 17.1 us  [send(): return lax.ppermute(value, AXES, full_swap(sizes, **how))]
    gather x16 -> x0, local copies, waits for them, and re-layouts: 41.5 us -> none  [the longest x8 20.8 us: local(): magn_rows = magnetic.reshape(3, -1)[:, slot_cells]]
    all_to_all x2 -> x0, starting transfers between devices: 11.5 us -> none  [the longest x1 7.86 us: local(): lax.all_to_all(tile_buf, ('gx', 'gy'), split_axis=2, concat_axis=2, tiled...]
    add x4 -> x0, local copies, waits for them, and re-layouts: 10.5 us -> none  [local(): electric = keep_e * electric + gain_e * (curl_magn - drude)]
    sub x4 -> x0, local copies, waits for them, and re-layouts: 10.5 us -> none  [local(): magnetic = magnetic - STEP_DT * curl_upper(electric)]
    all_to_all x0 -> x1, blocking collectives: none -> 10.3 us  [local(): lax.all_to_all(part, ('gx', 'gy'), split_axis=0, concat_axis=0, tiled=True)]
    slice x61 -> x1, local copies, waits for them, and re-layouts: 9.62 us -> 0.58 us  [local(): force = jnp.sum(got, axis=0)[:3]]
    pallas_call x0 -> x3, Pallas kernels: none -> 8.75 us  [the longest x1 4.8 us: local(): pl.pallas_call(functools.partial(main_kernel, sizes, steps, sigma_table.s...]
  transfers between devices with their start and end apart: 26 -> 9, of which waited for: 1 -> 3; matrix products, arithmetic and copies ran while one was open for 56% -> 0% of each run, Pallas kernels for 0% -> 0%
where the time goes in v1:
time: 45.5 us; the launch traced here: 45.2 us
  starting transfers between devices  17.1 us (38%)
  blocking collectives  10.3 us (23%)
  Pallas kernels  8.75 us (19%)
  waiting for transfers between devices  4.85 us (11%)
  local copies, waits for them, and re-layouts  2.84 us (6%)
  between operations  1.34 us (3%)
    ppermute x9, starting transfers between devices, send(): return lax.ppermute(value, AXES, full_swap(sizes, **how))  17.1 us
    all_to_all x1, blocking collectives, local(): lax.all_to_all(part, ('gx', 'gy'), split_axis=0, concat_axis=0, tiled=True)  10.3 us
    ppermute x9, waiting for transfers between devices, send(): return lax.ppermute(value, AXES, full_swap(sizes, **how))  4.85 us
    pallas_call x1, Pallas kernels, local(): pl.pallas_call(functools.partial(main_kernel, sizes, steps, sigma_table.s...  4.8 us
    unnamed x18, local copies, waits for them, and re-layouts  2.25 us
    pallas_call x1, Pallas kernels, local(): pl.pallas_call(functools.partial(rows_kernel, len(parts), n_y), out_shape...  2.07 us
    pallas_call x1, Pallas kernels, local(): pl.pallas_call(functools.partial(pack_kernel, steps), out_shape=(jax.Shap...  1.88 us
  transfers between devices with their start and end apart: 9, of which 3 were waited for; matrix products, arithmetic and copies ran while one was open for 0% of the time, Pallas kernels for 0%

profile of v1, /device:TPU:0, one launch (start us, length us, event | category | flops | bytes accessed | tf_op | source)
XLA Modules:
  0.0 45.2 jit_solution(9724254518874223610)
XLA Ops:
  0.6 1.9 %pack.1 = (f32[40,16,128]{2,1,0:T(8,128)}, f32[2,16,128]{2,1,0:T(8,128)}, f32[2,16,128]{2,1,0:T(8,128)}) custom-call(f32[3,4,16,128]{3,2,1,0:T(8,128)} %e_ref.1, f32[3,4,16,128]{3,2,1,0:T(8,128)} %h_ref.1, f32[3,4,16,128]{3,2,1,0:T(8,128)} %j_ref.1, s32[4,16,128]{2,1,0:T(8,128)} %m_ref.1), custom_call_target="tpu_custom_call" | custom-call | tf_op jit(solution)/shard_map/pack/pallas_call | solution.py:301
  2.5 3.1 %collective-permute-start = (f32[40,16,128]{2,1,0:T(8,128)}, f32[40,16,128]{2,1,0:T(8,128)S(1)}, u32[]{:S(2)}, u32[]{:S(2)}) collective-permute-start(f32[40,16,128]{2,1,0:T(8,128)} %get-tuple-element.9.refs_0_), channel_id=1, source_target_pairs={{0,8},{1,9},{2,10},{3,11},{4,12},{5,13},{6,14},{7,15},{8,0},{9,1},... | collective-permute-start | bytes 983048 | tf_op jit(solution)/shard_map/ppermute | solution.py:314
  5.6 0.0 collective-permute-start.1
  5.6 1.5 %collective-permute-start.2 = (f32[2,16,128]{2,1,0:T(8,128)}, f32[2,16,128]{2,1,0:T(8,128)S(1)}, u32[]{:S(2)}, u32[]{:S(2)}) collective-permute-start(f32[2,16,128]{2,1,0:T(8,128)} %get-tuple-element.10), channel_id=1, source_target_pairs={{0,1},{1,0},{2,3},{3,2},{4,5},{5,4},{6,7},{7,6},{8,9},{9,8},{10,11... | collective-permute-start | bytes 49160 | tf_op jit(solution)/shard_map/ppermute | solution.py:314
  7.1 1.5 %collective-permute-start.3 = (f32[2,16,128]{2,1,0:T(8,128)}, f32[2,16,128]{2,1,0:T(8,128)S(1)}, u32[]{:S(2)}, u32[]{:S(2)}) collective-permute-start(f32[2,16,128]{2,1,0:T(8,128)} %get-tuple-element.11), channel_id=1, source_target_pairs={{0,3},{1,2},{2,1},{3,0},{4,7},{5,6},{6,5},{7,4},{8,11},{9,10},{10,... | collective-permute-start | bytes 49160 | tf_op jit(solution)/shard_map/ppermute | solution.py:314
  8.5 4.1 %collective-permute-start.4 = (f32[2,16,128]{2,1,0:T(8,128)}, f32[2,16,128]{2,1,0:T(8,128)S(1)}, u32[]{:S(2)}, u32[]{:S(2)}) collective-permute-start(f32[2,16,128]{2,1,0:T(8,128)} %get-tuple-element.10), channel_id=1, source_target_pairs={{0,9},{1,8},{2,11},{3,10},{4,13},{5,12},{6,15},{7,14},{8,1},{9,0},... | collective-permute-start | bytes 49160 | tf_op jit(solution)/shard_map/ppermute | solution.py:314
  12.6 0.0 collective-permute-done.2.refs_3_
  12.6 1.9 %collective-permute-start.5 = (f32[2,16,128]{2,1,0:T(8,128)}, f32[2,16,128]{2,1,0:T(8,128)S(1)}, u32[]{:S(2)}, u32[]{:S(2)}) collective-permute-start(f32[2,16,128]{2,1,0:T(8,128)} %get-tuple-element.11), channel_id=1, source_target_pairs={{0,11},{1,10},{2,9},{3,8},{4,15},{5,14},{6,13},{7,12},{8,3},{9,2},... | collective-permute-start | bytes 49160 | tf_op jit(solution)/shard_map/ppermute | solution.py:314
  14.6 0.0 collective-permute-done.3.refs_4_
  14.6 0.9 %collective-permute-start.6 = (f32[2,16,128]{2,1,0:T(8,128)}, f32[2,16,128]{2,1,0:T(8,128)S(1)}, u32[]{:S(2)}, u32[]{:S(2)}) collective-permute-start(f32[2,16,128]{2,1,0:T(8,128)} %get-tuple-element.10), channel_id=1, source_target_pairs={{0,25},{1,24},{2,27},{3,26},{4,29},{5,28},{6,31},{7,30},{8,17},{9,... | collective-permute-start | bytes 49160 | tf_op jit(solution)/shard_map/ppermute | solution.py:314
  15.4 0.0 collective-permute-done.4.refs_5_
  15.4 4.2 %collective-permute-start.7 = (f32[2,16,128]{2,1,0:T(8,128)}, f32[2,16,128]{2,1,0:T(8,128)S(1)}, u32[]{:S(2)}, u32[]{:S(2)}) collective-permute-start(f32[2,16,128]{2,1,0:T(8,128)} %get-tuple-element.11), channel_id=1, source_target_pairs={{0,27},{1,26},{2,25},{3,24},{4,31},{5,30},{6,29},{7,28},{8,19},{9,... | collective-permute-start | bytes 49160 | tf_op jit(solution)/shard_map/ppermute | solution.py:314
  19.6 0.0 collective-permute-done.5.refs_6_
  19.6 1.6 %collective-permute-done.6.refs_7_ = f32[2,16,128]{2,1,0:T(8,128)S(1)} collective-permute-done((f32[2,16,128]{2,1,0:T(8,128)}, f32[2,16,128]{2,1,0:T(8,128)S(1)}, u32[]{:S(2)}, u32[]{:S(2)}) %collective-permute-start.6) | collective-permute-done | bytes 16416 | tf_op jit(solution)/shard_map/ppermute | solution.py:314
  21.2 1.8 %collective-permute-done.7.refs_8_ = f32[2,16,128]{2,1,0:T(8,128)S(1)} collective-permute-done((f32[2,16,128]{2,1,0:T(8,128)}, f32[2,16,128]{2,1,0:T(8,128)S(1)}, u32[]{:S(2)}, u32[]{:S(2)}) %collective-permute-start.7) | collective-permute-done | bytes 16416 | tf_op jit(solution)/shard_map/ppermute | solution.py:314
  23.0 0.0 collective-permute-done.refs_1_
  23.0 0.0 collective-permute-done.1.refs_2_
  23.0 0.0 copy-done.3
  23.0 0.0 copy-done.4
  23.0 0.0 copy-done.5
  23.0 0.0 copy-done.6
  23.0 0.0 copy-done.7
  23.0 0.5 %copy-done.8 = f32[2,16,128]{2,1,0:T(8,128)} copy-done((f32[2,16,128]{2,1,0:T(8,128)}, f32[2,16,128]{2,1,0:T(8,128)S(1)}, u32[]{:S(2)}) %copy-start.8) | copy-done | bytes 16408
  23.6 0.1 copy-done
  23.7 0.7 %copy-done.1 = f32[40,16,128]{2,1,0:T(8,128)} copy-done((f32[40,16,128]{2,1,0:T(8,128)}, f32[40,16,128]{2,1,0:T(8,128)S(1)}, u32[]{:S(2)}) %copy-start.1) | copy-done | bytes 327704
  24.5 2.1 %rows.1 = f32[132,8,128]{2,1,0:T(8,128)} custom-call(f32[40,16,128]{2,1,0:T(8,128)} %get-tuple-element.9.refs_0_, f32[40,16,128]{2,1,0:T(8,128)} %copy-done, f32[40,16,128]{2,1,0:T(8,128)} %copy-done.1, f32[2,16,128]{2,1,0:T(8,128)} %copy-done.3, f32[2,16,128]{2,1,0:T(8,128)} %copy-done.4, f32[2,16,128]{2,1,0:T(8,128)} %copy-done.5, ...), custom_call_target="tpu_custom_call" | custom-call | tf_op jit(solution)/shard_map/rows/pallas_call | solution.py:329
  26.5 0.0 collective-permute-start.8
  27.2 1.5 %collective-permute-done.8.refs_9_ = f32[132,8,128]{2,1,0:T(8,128)S(1)} collective-permute-done((f32[132,8,128]{2,1,0:T(8,128)}, f32[132,8,128]{2,1,0:T(8,128)S(1)}, u32[]{:S(2)}, u32[]{:S(2)}) %collective-permute-start.8) | collective-permute-done | bytes 540704 | tf_op jit(solution)/shard_map/ppermute | solution.py:314
  28.7 0.8 %copy-done.2 = f32[132,8,128]{2,1,0:T(8,128)} copy-done((f32[132,8,128]{2,1,0:T(8,128)}, f32[132,8,128]{2,1,0:T(8,128)S(1)}, u32[]{:S(2)}) %copy-start.2) | copy-done | bytes 540696
  29.5 4.8 %march.1 = (f32[3,4,16,128]{3,2,1,0:T(8,128)}, f32[3,4,16,128]{3,2,1,0:T(8,128)}, f32[8,8,128]{2,1,0:T(8,128)}) custom-call(f32[40,16,128]{2,1,0:T(8,128)} %get-tuple-element.9.refs_0_, f32[40,16,128]{2,1,0:T(8,128)} %copy-done, f32[40,16,128]{2,1,0:T(8,128)} %copy-done.1, f32[2,16,128]{2,1,0:T(8,128)} %copy-done.3, f32[2,16,128]{2,1,0:T(8,128)} %copy-done.4, ...), custom_call_target="tpu_custom_call" | custom-call | tf_op jit(solution)/shard_map/march/pallas_call | solution.py:341
  34.3 10.3 %all_to_all.5 = f32[8,8,128]{2,1,0:T(8,128)S(1)} all-to-all(f32[8,8,128]{2,1,0:T(8,128)} %get-tuple-element.14), channel_id=1, replica_groups=mesh['gx'=4,'gy'=2,'gz'=4] {'gx','gy'}, dimensions={0} | all-to-all | bytes 65536 | tf_op jit(solution)/shard_map/all_to_all | solution.py:359
  44.6 0.6 %slice.3 = f32[3,128]{1,0:T(4,128)} slice(f32[8,128]{1,0:T(8,128)S(1)} %reduce_sum.9), slice={[0:3], [0:128]} | slice | bytes 3072 | tf_op jit(solution)/shard_map/slice | solution.py:360
  (10 shorter events, 0.0 us)
Async XLA Ops:
  2.5 20.5 %collective-permute-start = (f32[40,16,128]{2,1,0:T(8,128)}, f32[40,16,128]{2,1,0:T(8,128)S(1)}, u32[]{:S(2)}, u32[]{:S(2)}) collective-permute-start(f32[40,16,128]{2,1,0:T(8,128)} %get-tuple-element.9.refs_0_), channel_id=1, source_target_pairs={{0,8},{1,9},{2,10},{3,11},{4,12},{5,13},{6,14},{7,15},{8,0},{9,1},... | collective-permute-start | bytes 983048 | tf_op jit(solution)/shard_map/ppermute | solution.py:314
  5.6 17.4 %collective-permute-start.1 = (f32[40,16,128]{2,1,0:T(8,128)}, f32[40,16,128]{2,1,0:T(8,128)S(1)}, u32[]{:S(2)}, u32[]{:S(2)}) collective-permute-start(f32[40,16,128]{2,1,0:T(8,128)} %get-tuple-element.9.refs_0_), channel_id=1, source_target_pairs={{0,4},{1,5},{2,6},{3,7},{4,0},{5,1},{6,2},{7,3},{8,16},{9,17},{10,... | collective-permute-start | bytes 983048 | tf_op jit(solution)/shard_map/ppermute | solution.py:314
  5.6 7.1 %collective-permute-start.2 = (f32[2,16,128]{2,1,0:T(8,128)}, f32[2,16,128]{2,1,0:T(8,128)S(1)}, u32[]{:S(2)}, u32[]{:S(2)}) collective-permute-start(f32[2,16,128]{2,1,0:T(8,128)} %get-tuple-element.10), channel_id=1, source_target_pairs={{0,1},{1,0},{2,3},{3,2},{4,5},{5,4},{6,7},{7,6},{8,9},{9,8},{10,11... | collective-permute-start | bytes 49160 | tf_op jit(solution)/shard_map/ppermute | solution.py:314
  7.1 7.5 %collective-permute-start.3 = (f32[2,16,128]{2,1,0:T(8,128)}, f32[2,16,128]{2,1,0:T(8,128)S(1)}, u32[]{:S(2)}, u32[]{:S(2)}) collective-permute-start(f32[2,16,128]{2,1,0:T(8,128)} %get-tuple-element.11), channel_id=1, source_target_pairs={{0,3},{1,2},{2,1},{3,0},{4,7},{5,6},{6,5},{7,4},{8,11},{9,10},{10,... | collective-permute-start | bytes 49160 | tf_op jit(solution)/shard_map/ppermute | solution.py:314
  8.5 6.9 %collective-permute-start.4 = (f32[2,16,128]{2,1,0:T(8,128)}, f32[2,16,128]{2,1,0:T(8,128)S(1)}, u32[]{:S(2)}, u32[]{:S(2)}) collective-permute-start(f32[2,16,128]{2,1,0:T(8,128)} %get-tuple-element.10), channel_id=1, source_target_pairs={{0,9},{1,8},{2,11},{3,10},{4,13},{5,12},{6,15},{7,14},{8,1},{9,0},... | collective-permute-start | bytes 49160 | tf_op jit(solution)/shard_map/ppermute | solution.py:314
  12.6 10.4 %copy-start.3 = (f32[2,16,128]{2,1,0:T(8,128)}, f32[2,16,128]{2,1,0:T(8,128)S(1)}, u32[]{:S(2)}) copy-start(f32[2,16,128]{2,1,0:T(8,128)S(1)} %collective-permute-done.2.refs_3_) | copy-start | bytes 49156
  12.6 7.0 %collective-permute-start.5 = (f32[2,16,128]{2,1,0:T(8,128)}, f32[2,16,128]{2,1,0:T(8,128)S(1)}, u32[]{:S(2)}, u32[]{:S(2)}) collective-permute-start(f32[2,16,128]{2,1,0:T(8,128)} %get-tuple-element.11), channel_id=1, source_target_pairs={{0,11},{1,10},{2,9},{3,8},{4,15},{5,14},{6,13},{7,12},{8,3},{9,2},... | collective-permute-start | bytes 49160 | tf_op jit(solution)/shard_map/ppermute | solution.py:314
  14.6 8.5 %copy-start.4 = (f32[2,16,128]{2,1,0:T(8,128)}, f32[2,16,128]{2,1,0:T(8,128)S(1)}, u32[]{:S(2)}) copy-start(f32[2,16,128]{2,1,0:T(8,128)S(1)} %collective-permute-done.3.refs_4_) | copy-start | bytes 49156
  14.6 6.6 %collective-permute-start.6 = (f32[2,16,128]{2,1,0:T(8,128)}, f32[2,16,128]{2,1,0:T(8,128)S(1)}, u32[]{:S(2)}, u32[]{:S(2)}) collective-permute-start(f32[2,16,128]{2,1,0:T(8,128)} %get-tuple-element.10), channel_id=1, source_target_pairs={{0,25},{1,24},{2,27},{3,26},{4,29},{5,28},{6,31},{7,30},{8,17},{9,... | collective-permute-start | bytes 49160 | tf_op jit(solution)/shard_map/ppermute | solution.py:314
  15.4 7.6 %copy-start.5 = (f32[2,16,128]{2,1,0:T(8,128)}, f32[2,16,128]{2,1,0:T(8,128)S(1)}, u32[]{:S(2)}) copy-start(f32[2,16,128]{2,1,0:T(8,128)S(1)} %collective-permute-done.4.refs_5_) | copy-start | bytes 49156
  15.4 7.5 %collective-permute-start.7 = (f32[2,16,128]{2,1,0:T(8,128)}, f32[2,16,128]{2,1,0:T(8,128)S(1)}, u32[]{:S(2)}, u32[]{:S(2)}) collective-permute-start(f32[2,16,128]{2,1,0:T(8,128)} %get-tuple-element.11), channel_id=1, source_target_pairs={{0,27},{1,26},{2,25},{3,24},{4,31},{5,30},{6,29},{7,28},{8,19},{9,... | collective-permute-start | bytes 49160 | tf_op jit(solution)/shard_map/ppermute | solution.py:314
  19.6 3.4 %copy-start.6 = (f32[2,16,128]{2,1,0:T(8,128)}, f32[2,16,128]{2,1,0:T(8,128)S(1)}, u32[]{:S(2)}) copy-start(f32[2,16,128]{2,1,0:T(8,128)S(1)} %collective-permute-done.5.refs_6_) | copy-start | bytes 49156
  21.2 1.8 %copy-start.7 = (f32[2,16,128]{2,1,0:T(8,128)}, f32[2,16,128]{2,1,0:T(8,128)S(1)}, u32[]{:S(2)}) copy-start(f32[2,16,128]{2,1,0:T(8,128)S(1)} %collective-permute-done.6.refs_7_) | copy-start | bytes 49156
  23.0 0.6 %copy-start.8 = (f32[2,16,128]{2,1,0:T(8,128)}, f32[2,16,128]{2,1,0:T(8,128)S(1)}, u32[]{:S(2)}) copy-start(f32[2,16,128]{2,1,0:T(8,128)S(1)} %collective-permute-done.7.refs_8_) | copy-start | bytes 49156
  23.0 0.7 %copy-start = (f32[40,16,128]{2,1,0:T(8,128)}, f32[40,16,128]{2,1,0:T(8,128)S(1)}, u32[]{:S(2)}) copy-start(f32[40,16,128]{2,1,0:T(8,128)S(1)} %collective-permute-done.refs_1_) | copy-start | bytes 983044
  23.7 0.7 %copy-start.1 = (f32[40,16,128]{2,1,0:T(8,128)}, f32[40,16,128]{2,1,0:T(8,128)S(1)}, u32[]{:S(2)}) copy-start(f32[40,16,128]{2,1,0:T(8,128)S(1)} %collective-permute-done.1.refs_2_) | copy-start | bytes 983044
  26.5 2.1 %collective-permute-start.8 = (f32[132,8,128]{2,1,0:T(8,128)}, f32[132,8,128]{2,1,0:T(8,128)S(1)}, u32[]{:S(2)}, u32[]{:S(2)}) collective-permute-start(f32[132,8,128]{2,1,0:T(8,128)} %rows.1), channel_id=1, source_target_pairs={{0,4},{1,5},{2,6},{3,7},{4,0},{5,1},{6,2},{7,3},{8,12},{9,13},{10,... | collective-permute-start | bytes 1622024 | tf_op jit(solution)/shard_map/ppermute | solution.py:314
  28.7 0.8 %copy-start.2 = (f32[132,8,128]{2,1,0:T(8,128)}, f32[132,8,128]{2,1,0:T(8,128)S(1)}, u32[]{:S(2)}) copy-start(f32[132,8,128]{2,1,0:T(8,128)S(1)} %collective-permute-done.8.refs_9_) | copy-start | bytes 1622020

commit v2 on v1

--- a/solution.py
+++ b/solution.py
@@ -22,23 +22,18 @@
     return (index - 1) % size if index % 2 == 0 else (index + 1) % size
 
 
-def full_swap(sizes, second_x=None, second_y=None, second_z=None, local_ends=False):
-    n_x, n_y, n_z = sizes
+def full_swap(sizes, axis, second=False):
     pairs = []
-    for x in range(n_x):
-        for y in range(n_y):
-            for z in range(n_z):
+    at = AXES.index(axis)
+    for x in range(sizes[0]):
+        for y in range(sizes[1]):
+            for z in range(sizes[2]):
                 to = [x, y, z]
-                if second_x is not None:
-                    if local_ends and second_x and x in (0, n_x - 1):
-                        to[1] = y ^ 1
-                    else:
-                        to[0] = partner(x, n_x, second_x)
-                if second_y is not None:
-                    to[1] = partner(y, n_y, second_y)
-                if second_z is not None:
-                    to[2] = partner(z, n_z, second_z)
-                pairs.append(((x * n_y + y) * n_z + z, (to[0] * n_y + to[1]) * n_z + to[2]))
+                if second and to[at] in (0, sizes[at] - 1) and axis != "gy":
+                    to[1] = y ^ 1
+                else:
+                    to[at] = partner(to[at], sizes[at], second)
+                pairs.append(((x * sizes[1] + y) * sizes[2] + z, (to[0] * sizes[1] + to[1]) * sizes[2] + to[2]))
     return pairs
 
 
@@ -264,7 +259,7 @@
         owner = owner_ref[:, at : at + chunk]
         normal = normal_ref[:, at : at + chunk]
         tile = tile_ref[:, at : at + chunk]
-        live = (at + lax.broadcasted_iota(jnp.int32, (1, chunk), 1)) < count_ref[0]
+        live = (at + lax.broadcasted_iota(jnp.int32, (1, chunk), 1)) < count_ref[0, 0, 0]
         hot = jnp.where(lax.broadcasted_iota(jnp.int32, (lanes, chunk), 0) == cell % lanes, 1.0, 0.0).astype(jnp.bfloat16)
         picked = jnp.dot(lhs, jnp.concatenate([hot, hot], 0), preferred_element_type=jnp.float32)
         in_row = lax.broadcasted_iota(jnp.int32, (cells, chunk), 0) == cell // lanes
@@ -307,22 +302,25 @@
         ),
         in_specs=[VMEM] * 4,
         out_specs=(VMEM,) * 3,
+        compiler_params=pltpu.CompilerParams(vmem_limit_bytes=4 << 20),
         name="pack",
     )(e_field, h_field, current, material)
 
-    def send(value, **how):
-        return lax.ppermute(value, AXES, full_swap(sizes, **how))
-
+    def send(value, axis, second=False):
+        return lax.ppermute(value, AXES, full_swap(sizes, axis, second))
+
+    x_first, x_second = send(brick, "gx"), send(brick, "gx", True)
+    z_first, z_second = send(z_first, "gz"), send(z_second, "gz", True)
     parts = [
         brick,
-        send(brick, second_x=False),
-        send(brick, second_x=True, local_ends=True),
-        send(z_first, second_z=False),
-        send(z_second, second_z=True),
-        send(z_first, second_x=False, second_z=False),
-        send(z_second, second_x=False, second_z=True),
-        send(z_first, second_x=True, second_z=False),
-        send(z_second, second_x=True, second_z=True),
+        x_first,
+        x_second,
+        z_first,
+        z_second,
+        send(z_first, "gx"),
+        send(z_second, "gx"),
+        send(z_first, "gx", True),
+        send(z_second, "gx", True),
     ]
     counts = [p.shape[0] for p in parts]
     n_ghost = 1 if n_y == 2 else 2
@@ -331,9 +329,10 @@
         out_shape=[jax.ShapeDtypeStruct((sum(counts), 8, lanes), f32)] * n_ghost,
         in_specs=[VMEM] * len(parts),
         out_specs=[VMEM] * n_ghost,
+        compiler_params=pltpu.CompilerParams(vmem_limit_bytes=6 << 20),
         name="rows",
     )(*parts)
-    ghosts = [send(v, second_y=bool(i)) for i, v in enumerate(outgoing)]
+    ghosts = [send(v, "gy", bool(i)) for i, v in enumerate(outgoing)]
 
     owners = n_x * n_y
     slots = surf_cell.size
@@ -353,11 +352,12 @@
             pltpu.VMEM((2, rows + 8, wide), f32),
             pltpu.VMEM((len(PAIRS), planes * rows, lanes), f32),
         ],
+        compiler_params=pltpu.CompilerParams(vmem_limit_bytes=24 << 20),
         name="march",
-    )(*parts, *ghosts, sigma_table, gamma_table, plasma_table, g_kernel, row_count.reshape(1),
+    )(*parts, *ghosts, sigma_table, gamma_table, plasma_table, g_kernel, row_count,
       surf_cell.reshape(1, slots), surf_owner.reshape(1, slots), surf_tile.reshape(1, slots), surf_normal.reshape(1, slots))
     got = lax.all_to_all(part, ("gx", "gy"), split_axis=0, concat_axis=0, tiled=True)
-    force = jnp.sum(got, axis=0)[:3]
+    force = jnp.sum(got[:, :3], axis=0)
     return e_out, h_out, force
 
 

time: 45.5 us -> 36.4 us (0.80)
  starting transfers between devices: 17.1 us -> 8.51 us
  Pallas kernels: 8.75 us -> 3.98 us
  waiting for transfers between devices: 4.85 us -> 6.56 us
  local copies, waits for them, and re-layouts: 2.84 us -> 4.09 us
  blocking collectives: 10.3 us -> 10.9 us
  other arithmetic: 0.01 us -> 0.59 us
    ppermute x9, starting transfers between devices: 17.1 us -> 8.51 us  [send(): return lax.ppermute(value, AXES, full_swap(sizes, axis, second))]
    pallas_call x1, Pallas kernels: 2.07 us -> 0.05 us  [local(): pl.pallas_call(functools.partial(rows_kernel, len(parts), n_y), out_shape...]
    unnamed x18 -> x24, local copies, waits for them, and re-layouts: 2.25 us -> 4.09 us
    ppermute x9, waiting for transfers between devices: 4.85 us -> 6.56 us  [send(): return lax.ppermute(value, AXES, full_swap(sizes, axis, second))]
    pallas_call x1, Pallas kernels: 1.88 us -> 0.22 us  [local(): pl.pallas_call(functools.partial(pack_kernel, steps), out_shape=(jax.Shap...]
    pallas_call x1, Pallas kernels: 4.8 us -> 3.7 us  [local(): pl.pallas_call(functools.partial(main_kernel, sizes, steps, sigma_table.s...]
    all_to_all x1, blocking collectives: 10.3 us -> 10.9 us  [local(): lax.all_to_all(part, ('gx', 'gy'), split_axis=0, concat_axis=0, tiled=True)]
    slice x1 -> x0, local copies, waits for them, and re-layouts: 0.58 us -> none  [local(): force = jnp.sum(got, axis=0)[:3]]
  transfers between devices with their start and end apart: 9 -> 9, of which waited for: 3 -> 4; matrix products, arithmetic and copies ran while one was open for 0% -> 0% of each run, Pallas kernels for 0% -> 0%
where the time goes in v2:
time: 36.4 us; the launch traced here: 36 us
  blocking collectives  10.9 us (30%)
  starting transfers between devices  8.51 us (23%)
  waiting for transfers between devices  6.56 us (18%)
  local copies, waits for them, and re-layouts  4.09 us (11%)
  Pallas kernels  3.98 us (11%)
  between operations  1.43 us (4%)
  other arithmetic  0.59 us (2%)
    all_to_all x1, blocking collectives, local(): lax.all_to_all(part, ('gx', 'gy'), split_axis=0, concat_axis=0, tiled=True)  10.9 us
    ppermute x9, starting transfers between devices, send(): return lax.ppermute(value, AXES, full_swap(sizes, axis, second))  8.51 us
    ppermute x9, waiting for transfers between devices, send(): return lax.ppermute(value, AXES, full_swap(sizes, axis, second))  6.56 us
    unnamed x24, local copies, waits for them, and re-layouts  4.09 us
    pallas_call x1, Pallas kernels, local(): pl.pallas_call(functools.partial(main_kernel, sizes, steps, sigma_table.s...  3.7 us
  transfers between devices with their start and end apart: 9, of which 4 were waited for; matrix products, arithmetic and copies ran while one was open for 0% of the time, Pallas kernels for 0%

profile of v2, /device:TPU:0, one launch (start us, length us, event | category | flops | bytes accessed | tf_op | source)
XLA Modules:
  0.0 36.0 jit_solution(18395458016482383837)
XLA Ops:
  0.6 0.9 %copy-done = f32[3,4,16,128]{3,2,1,0:T(8,128)S(1)} copy-done((f32[3,4,16,128]{3,2,1,0:T(8,128)S(1)}, f32[3,4,16,128]{3,2,1,0:T(8,128)}, u32[]{:S(2)}) %copy-start) | copy-done | bytes 98328
  1.5 0.9 %copy-done.1 = f32[3,4,16,128]{3,2,1,0:T(8,128)S(1)} copy-done((f32[3,4,16,128]{3,2,1,0:T(8,128)S(1)}, f32[3,4,16,128]{3,2,1,0:T(8,128)}, u32[]{:S(2)}) %copy-start.1) | copy-done | bytes 98328
  2.4 0.9 %copy-done.2 = f32[3,4,16,128]{3,2,1,0:T(8,128)S(1)} copy-done((f32[3,4,16,128]{3,2,1,0:T(8,128)S(1)}, f32[3,4,16,128]{3,2,1,0:T(8,128)}, u32[]{:S(2)}) %copy-start.2) | copy-done | bytes 98328
  3.3 0.8 %copy-done.3 = s32[4,16,128]{2,1,0:T(8,128)S(1)} copy-done((s32[4,16,128]{2,1,0:T(8,128)S(1)}, s32[4,16,128]{2,1,0:T(8,128)}, u32[]{:S(2)}) %copy-start.3) | copy-done | bytes 32792
  4.1 0.2 pack.1
  4.3 3.1 %collective-permute-start = (f32[40,16,128]{2,1,0:T(8,128)S(1)}, f32[40,16,128]{2,1,0:T(8,128)S(1)}, u32[]{:S(2)}, u32[]{:S(2)}) collective-permute-start(f32[40,16,128]{2,1,0:T(8,128)S(1)} %get-tuple-element.9.refs_0_), channel_id=1, source_target_pairs={{0,8},{1,9},{2,10},{3,11},{4,12},{5,13},{6,14},{7,15},{8,0},{9,1},... | collective-permute-start | bytes 983048 | tf_op jit(solution)/shard_map/ppermute | solution.py:310
  7.4 0.0 collective-permute-start.1
  7.4 1.5 %collective-permute-start.2 = (f32[2,16,128]{2,1,0:T(8,128)S(1)}, f32[2,16,128]{2,1,0:T(8,128)S(1)}, u32[]{:S(2)}, u32[]{:S(2)}) collective-permute-start(f32[2,16,128]{2,1,0:T(8,128)S(1)} %get-tuple-element.10), channel_id=1, source_target_pairs={{0,1},{1,0},{2,3},{3,2},{4,5},{5,4},{6,7},{7,6},{8,9},{9,8},{10,11... | collective-permute-start | bytes 49160 | tf_op jit(solution)/shard_map/ppermute | solution.py:310
  8.9 0.2 collective-permute-start.3
  9.1 2.0 %collective-permute-done.2.refs_3_ = f32[2,16,128]{2,1,0:T(8,128)S(1)} collective-permute-done((f32[2,16,128]{2,1,0:T(8,128)S(1)}, f32[2,16,128]{2,1,0:T(8,128)S(1)}, u32[]{:S(2)}, u32[]{:S(2)}) %collective-permute-start.2) | collective-permute-done | bytes 16416 | tf_op jit(solution)/shard_map/ppermute | solution.py:310
  11.2 3.1 %collective-permute-start.4 = (f32[2,16,128]{2,1,0:T(8,128)S(1)}, f32[2,16,128]{2,1,0:T(8,128)S(1)}, u32[]{:S(2)}, u32[]{:S(2)}) collective-permute-start(f32[2,16,128]{2,1,0:T(8,128)S(1)} %collective-permute-done.2.refs_3_), channel_id=1, source_target_pairs={{0,8},{1,9},{2,10},{3,11},{4,12},{5,13},{6,14},{7,15},{8,0},{9,1},... | collective-permute-start | bytes 49160 | tf_op jit(solution)/shard_map/ppermute | solution.py:310
  14.3 0.0 collective-permute-start.6
  14.3 0.0 collective-permute-done.3.refs_4_
  14.3 0.5 %collective-permute-start.5 = (f32[2,16,128]{2,1,0:T(8,128)S(1)}, f32[2,16,128]{2,1,0:T(8,128)S(1)}, u32[]{:S(2)}, u32[]{:S(2)}) collective-permute-start(f32[2,16,128]{2,1,0:T(8,128)S(1)} %collective-permute-done.3.refs_4_), channel_id=1, source_target_pairs={{0,8},{1,9},{2,10},{3,11},{4,12},{5,13},{6,14},{7,15},{8,0},{9,1},... | collective-permute-start | bytes 49160 | tf_op jit(solution)/shard_map/ppermute | solution.py:310
  14.8 1.3 %collective-permute-done.4.refs_5_ = f32[2,16,128]{2,1,0:T(8,128)S(1)} collective-permute-done((f32[2,16,128]{2,1,0:T(8,128)S(1)}, f32[2,16,128]{2,1,0:T(8,128)S(1)}, u32[]{:S(2)}, u32[]{:S(2)}) %collective-permute-start.4) | collective-permute-done | bytes 16416 | tf_op jit(solution)/shard_map/ppermute | solution.py:310
  16.0 2.0 %collective-permute-done.5.refs_6_ = f32[2,16,128]{2,1,0:T(8,128)S(1)} collective-permute-done((f32[2,16,128]{2,1,0:T(8,128)S(1)}, f32[2,16,128]{2,1,0:T(8,128)S(1)}, u32[]{:S(2)}, u32[]{:S(2)}) %collective-permute-start.5) | collective-permute-done | bytes 16416 | tf_op jit(solution)/shard_map/ppermute | solution.py:310
  18.1 0.0 collective-permute-done.6.refs_7_
  18.1 0.0 collective-permute-done.7.refs_8_
  18.1 0.0 copy-start.6
  18.1 0.0 copy-start.7
  18.1 0.0 copy-start.10
  18.1 0.0 copy-start.11
  18.1 0.1 rows.1
  18.2 0.1 collective-permute-start.8
  18.3 0.0 copy-start.5
  18.9 0.0 copy-start.4
  19.0 1.2 %collective-permute-done.8.refs_9_ = f32[132,8,128]{2,1,0:T(8,128)S(1)} collective-permute-done((f32[132,8,128]{2,1,0:T(8,128)S(1)}, f32[132,8,128]{2,1,0:T(8,128)S(1)}, u32[]{:S(2)}, u32[]{:S(2)}) %collective-permute-start.8) | collective-permute-done | bytes 540704 | tf_op jit(solution)/shard_map/ppermute | solution.py:310
  20.2 0.6 %copy-done.8 = f32[3]{0:T(128)S(1)} copy-done((f32[3]{0:T(128)S(1)}, f32[3]{0:T(128)}, u32[]{:S(2)}) %copy-start.8) | copy-done | bytes 36
  20.8 0.0 copy-done.9
  20.9 3.7 %march.1 = (f32[3,4,16,128]{3,2,1,0:T(8,128)}, f32[3,4,16,128]{3,2,1,0:T(8,128)}, f32[8,8,128]{2,1,0:T(8,128)S(1)}) custom-call(f32[40,16,128]{2,1,0:T(8,128)S(1)} %get-tuple-element.9.refs_0_, f32[40,16,128]{2,1,0:T(8,128)S(1)} %collective-permute-done.refs_1_, f32[40,16,128]{2,1,0:T(8,128)S(1)} %collective-permute-done.1.refs_2_, ...), custom_call_target="tpu_custom_call" | custom-call | tf_op jit(solution)/shard_map/march/pallas_call | solution.py:340
  24.6 10.9 %all_to_all.5 = f32[8,8,128]{2,1,0:T(8,128)S(1)} all-to-all(f32[8,8,128]{2,1,0:T(8,128)S(1)} %get-tuple-element.14), channel_id=1, replica_groups=mesh['gx'=4,'gy'=2,'gz'=4] {'gx','gy'}, dimensions={0} | all-to-all | bytes 65536 | tf_op jit(solution)/shard_map/all_to_all | solution.py:359
  35.4 0.6 %slice_reduce_fusion = f32[3,128]{1,0:T(4,128)} fusion(f32[8,8,128]{2,1,0:T(8,128)S(1)} %all_to_all.5), kind=kLoop, calls=%fused_computation | loop fusion | flops 2688 | bytes 13824 | tf_op jit(solution)/shard_map/reduce_sum | solution.py:360
  (15 shorter events, 0.0 us)
Async XLA Ops:
  0.6 0.9 %copy-start = (f32[3,4,16,128]{3,2,1,0:T(8,128)S(1)}, f32[3,4,16,128]{3,2,1,0:T(8,128)}, u32[]{:S(2)}) copy-start(f32[3,4,16,128]{3,2,1,0:T(8,128)} %e_ref.1) | copy-start | bytes 294916
  1.5 0.9 %copy-start.1 = (f32[3,4,16,128]{3,2,1,0:T(8,128)S(1)}, f32[3,4,16,128]{3,2,1,0:T(8,128)}, u32[]{:S(2)}) copy-start(f32[3,4,16,128]{3,2,1,0:T(8,128)} %h_ref.1) | copy-start | bytes 294916
  2.4 0.9 %copy-start.2 = (f32[3,4,16,128]{3,2,1,0:T(8,128)S(1)}, f32[3,4,16,128]{3,2,1,0:T(8,128)}, u32[]{:S(2)}) copy-start(f32[3,4,16,128]{3,2,1,0:T(8,128)} %j_ref.1) | copy-start | bytes 294916
  3.3 0.8 %copy-start.3 = (s32[4,16,128]{2,1,0:T(8,128)S(1)}, s32[4,16,128]{2,1,0:T(8,128)}, u32[]{:S(2)}) copy-start(s32[4,16,128]{2,1,0:T(8,128)} %m_ref.1) | copy-start | bytes 98308
  4.3 13.8 %collective-permute-start = (f32[40,16,128]{2,1,0:T(8,128)S(1)}, f32[40,16,128]{2,1,0:T(8,128)S(1)}, u32[]{:S(2)}, u32[]{:S(2)}) collective-permute-start(f32[40,16,128]{2,1,0:T(8,128)S(1)} %get-tuple-element.9.refs_0_), channel_id=1, source_target_pairs={{0,8},{1,9},{2,10},{3,11},{4,12},{5,13},{6,14},{7,15},{8,0},{9,1},... | collective-permute-start | bytes 983048 | tf_op jit(solution)/shard_map/ppermute | solution.py:310
  7.4 10.7 %collective-permute-start.1 = (f32[40,16,128]{2,1,0:T(8,128)S(1)}, f32[40,16,128]{2,1,0:T(8,128)S(1)}, u32[]{:S(2)}, u32[]{:S(2)}) collective-permute-start(f32[40,16,128]{2,1,0:T(8,128)S(1)} %get-tuple-element.9.refs_0_), channel_id=1, source_target_pairs={{0,4},{1,5},{2,6},{3,7},{4,0},{5,1},{6,2},{7,3},{8,16},{9,17},{10,... | collective-permute-start | bytes 983048 | tf_op jit(solution)/shard_map/ppermute | solution.py:310
  7.4 3.7 %collective-permute-start.2 = (f32[2,16,128]{2,1,0:T(8,128)S(1)}, f32[2,16,128]{2,1,0:T(8,128)S(1)}, u32[]{:S(2)}, u32[]{:S(2)}) collective-permute-start(f32[2,16,128]{2,1,0:T(8,128)S(1)} %get-tuple-element.10), channel_id=1, source_target_pairs={{0,1},{1,0},{2,3},{3,2},{4,5},{5,4},{6,7},{7,6},{8,9},{9,8},{10,11... | collective-permute-start | bytes 49160 | tf_op jit(solution)/shard_map/ppermute | solution.py:310
  8.9 5.4 %collective-permute-start.3 = (f32[2,16,128]{2,1,0:T(8,128)S(1)}, f32[2,16,128]{2,1,0:T(8,128)S(1)}, u32[]{:S(2)}, u32[]{:S(2)}) collective-permute-start(f32[2,16,128]{2,1,0:T(8,128)S(1)} %get-tuple-element.11), channel_id=1, source_target_pairs={{0,4},{1,2},{2,1},{3,7},{4,0},{5,6},{6,5},{7,3},{8,12},{9,10},{10,... | collective-permute-start | bytes 49160 | tf_op jit(solution)/shard_map/ppermute | solution.py:310
  11.2 4.9 %collective-permute-start.4 = (f32[2,16,128]{2,1,0:T(8,128)S(1)}, f32[2,16,128]{2,1,0:T(8,128)S(1)}, u32[]{:S(2)}, u32[]{:S(2)}) collective-permute-start(f32[2,16,128]{2,1,0:T(8,128)S(1)} %collective-permute-done.2.refs_3_), channel_id=1, source_target_pairs={{0,8},{1,9},{2,10},{3,11},{4,12},{5,13},{6,14},{7,15},{8,0},{9,1},... | collective-permute-start | bytes 49160 | tf_op jit(solution)/shard_map/ppermute | solution.py:310
  14.3 3.7 %collective-permute-start.6 = (f32[2,16,128]{2,1,0:T(8,128)S(1)}, f32[2,16,128]{2,1,0:T(8,128)S(1)}, u32[]{:S(2)}, u32[]{:S(2)}) collective-permute-start(f32[2,16,128]{2,1,0:T(8,128)S(1)} %collective-permute-done.2.refs_3_), channel_id=1, source_target_pairs={{0,4},{1,5},{2,6},{3,7},{4,0},{5,1},{6,2},{7,3},{8,16},{9,17},{10,... | collective-permute-start | bytes 49160 | tf_op jit(solution)/shard_map/ppermute | solution.py:310
  14.3 3.7 %collective-permute-start.5 = (f32[2,16,128]{2,1,0:T(8,128)S(1)}, f32[2,16,128]{2,1,0:T(8,128)S(1)}, u32[]{:S(2)}, u32[]{:S(2)}) collective-permute-start(f32[2,16,128]{2,1,0:T(8,128)S(1)} %collective-permute-done.3.refs_4_), channel_id=1, source_target_pairs={{0,8},{1,9},{2,10},{3,11},{4,12},{5,13},{6,14},{7,15},{8,0},{9,1},... | collective-permute-start | bytes 49160 | tf_op jit(solution)/shard_map/ppermute | solution.py:310
  16.0 2.0 %collective-permute-start.7 = (f32[2,16,128]{2,1,0:T(8,128)S(1)}, f32[2,16,128]{2,1,0:T(8,128)S(1)}, u32[]{:S(2)}, u32[]{:S(2)}) collective-permute-start(f32[2,16,128]{2,1,0:T(8,128)S(1)} %collective-permute-done.3.refs_4_), channel_id=1, source_target_pairs={{0,4},{1,5},{2,6},{3,7},{4,0},{5,1},{6,2},{7,3},{8,16},{9,17},{10,... | collective-permute-start | bytes 49160 | tf_op jit(solution)/shard_map/ppermute | solution.py:310
  18.1 2.1 %copy-start.6 = (s32[1,1,1,1024]{3,2,1,0:T(1,128)S(1)}, s32[1,1,1,1024]{3,2,1,0:T(1,128)}, u32[]{:S(2)}) copy-start(s32[1,1,1,1024]{3,2,1,0:T(1,128)} %param.23) | copy-start | bytes 12292
  18.1 2.1 %copy-start.7 = (s32[1,1,1,1024]{3,2,1,0:T(1,128)S(1)}, s32[1,1,1,1024]{3,2,1,0:T(1,128)}, u32[]{:S(2)}) copy-start(s32[1,1,1,1024]{3,2,1,0:T(1,128)} %param.24) | copy-start | bytes 12292
  18.1 2.1 %copy-start.10 = (f32[3]{0:T(128)S(1)}, f32[3]{0:T(128)}, u32[]{:S(2)}) copy-start(f32[3]{0:T(128)} %refs_12_.1) | copy-start | bytes 40
  18.1 2.1 %copy-start.11 = (f32[4]{0:T(128)S(1)}, f32[4]{0:T(128)}, u32[]{:S(2)}) copy-start(f32[4]{0:T(128)} %refs_13_.1) | copy-start | bytes 52
  18.2 2.0 %collective-permute-start.8 = (f32[132,8,128]{2,1,0:T(8,128)S(1)}, f32[132,8,128]{2,1,0:T(8,128)S(1)}, u32[]{:S(2)}, u32[]{:S(2)}) collective-permute-start(f32[132,8,128]{2,1,0:T(8,128)S(1)} %rows.1), channel_id=1, source_target_pairs={{0,4},{1,5},{2,6},{3,7},{4,0},{5,1},{6,2},{7,3},{8,12},{9,13},{10,... | collective-permute-start | bytes 1622024 | tf_op jit(solution)/shard_map/ppermute | solution.py:310
  18.3 2.0 %copy-start.5 = (s32[1,1,1,1024,1]{3,4,2,1,0:T(1,128)S(1)}, s32[1,1,1,1024,1]{3,4,2,1,0:T(1,128)}, u32[]{:S(2)}) copy-start(s32[1,1,1,1024,1]{3,4,2,1,0:T(1,128)} %param.22) | copy-start | bytes 12292
  18.9 1.3 %copy-start.4 = (s32[1,1,1,1024]{3,2,1,0:T(1,128)S(1)}, s32[1,1,1,1024]{3,2,1,0:T(1,128)}, u32[]{:S(2)}) copy-start(s32[1,1,1,1024]{3,2,1,0:T(1,128)} %param.21) | copy-start | bytes 12292
  20.2 0.7 %copy-start.8 = (f32[3]{0:T(128)S(1)}, f32[3]{0:T(128)}, u32[]{:S(2)}) copy-start(f32[3]{0:T(128)} %refs_10_.1) | copy-start | bytes 40
  20.2 0.7 %copy-start.9 = (f32[3]{0:T(128)S(1)}, f32[3]{0:T(128)}, u32[]{:S(2)}) copy-start(f32[3]{0:T(128)} %refs_11_.1) | copy-start | bytes 40

commit v3 on v2

--- a/solution.py
+++ b/solution.py
@@ -37,28 +37,24 @@
     return pairs
 
 
-def fields_of(e_ref, h_ref, j_ref, m_ref, planes):
-    out = []
-    for ref in (e_ref, h_ref, j_ref):
-        for comp in range(3):
-            for plane in range(planes):
-                out.append(ref[comp, plane])
-    for plane in range(planes):
-        out.append((m_ref[plane] + 1).astype(jnp.float32))
-    return out
-
-
-def pack_kernel(depth, e_ref, h_ref, j_ref, m_ref, brick_ref, even_ref, odd_ref):
+def pack_kernel(depth, e_ref, h_ref, j_ref, m_ref, brick_ref, even_ref, odd_ref, m_buf, sems):
     planes, rows, lanes = m_ref.shape
+    count = 3 * planes
+    copies = [pltpu.make_async_copy(ref, brick_ref.at[pl.ds(i * count, count)], sems.at[i]) for i, ref in enumerate((e_ref, h_ref, j_ref))]
+    copies.append(pltpu.make_async_copy(m_ref, m_buf, sems.at[3]))
+    for copy in copies:
+        copy.start()
     per_tile = lanes // depth
-    lane = lax.broadcasted_iota(jnp.int32, (rows, lanes), 1)
-    group = lane // depth
-    fields = fields_of(e_ref, h_ref, j_ref, m_ref, planes)
+    group = lax.broadcasted_iota(jnp.int32, (rows, lanes), 1) // depth
     tiles = even_ref.shape[0]
     low = [jnp.zeros((rows, lanes), jnp.float32) for _ in range(tiles)]
     high = [jnp.zeros((rows, lanes), jnp.float32) for _ in range(tiles)]
-    for j, value in enumerate(fields):
-        brick_ref[j] = value
+    for j in range(3 * count + planes):
+        if j % count == 0:
+            copies[j // count].wait()
+        if j >= 3 * count:
+            brick_ref[j] = (m_buf[j - 3 * count] + 1).astype(jnp.float32)
+        value = brick_ref[j]
         tile, slot = j // per_tile, j % per_tile
         up = pltpu.roll(value, depth * slot, 1) if slot else value
         down = pltpu.roll(value, lanes - depth * slot, 1) if slot else value
@@ -70,8 +66,40 @@
         odd_ref[tile] = jnp.where(is_even, low[tile], high[tile])
 
 
-def rows_kernel(n_in, n_y, *refs):
-    ins, outs = refs[:n_in], refs[n_in:]
+def prepare_kernel(materials, steps, cells, lanes, sigma_ref, gamma_ref, plasma_ref, g_ref, count_ref,
+                   cell_ref, owner_ref, tile_ref, normal_ref, after_ref,
+                   table_ref, hot_ref, tile_hot_ref, ints_ref, scale_ref):
+    del after_ref
+    slots = cell_ref.shape[1]
+    shape = table_ref.shape[1:]
+
+    def splat(value):
+        return jnp.full(shape, value, jnp.float32)
+
+    for which in range(materials):
+        sigma, gamma, plasma = splat(sigma_ref[which]), splat(gamma_ref[which]), splat(plasma_ref[which])
+        table_ref[4 * which] = (1.0 - sigma * STEP_DT / 2) / (1.0 + sigma * STEP_DT / 2)
+        table_ref[4 * which + 1] = STEP_DT / (1.0 + sigma * STEP_DT / 2)
+        table_ref[4 * which + 2] = (1.0 - gamma * STEP_DT / 2) / (1.0 + gamma * STEP_DT / 2)
+        table_ref[4 * which + 3] = plasma * STEP_DT / (1.0 + gamma * STEP_DT / 2)
+    for t in range(steps):
+        table_ref[4 * materials + t] = splat(g_ref[t])
+    cell, normal = cell_ref[...], normal_ref[...]
+    in_lane, in_row = cell % lanes, cell // lanes
+    hot = lax.broadcasted_iota(jnp.int32, (lanes, slots), 0) == in_lane
+    hot_ref[...] = jnp.where(hot, 1.0, 0.0).astype(jnp.bfloat16)
+    tile_hot = lax.broadcasted_iota(jnp.int32, (TILE_DEV, slots), 0) == tile_ref[...]
+    tile_hot_ref[...] = jnp.where(tile_hot, 1.0, 0.0).astype(jnp.bfloat16)
+    ints_ref[0:1] = in_row
+    ints_ref[1:2] = owner_ref[...]
+    ints_ref[2:3] = normal // 2
+    live = lax.broadcasted_iota(jnp.int32, (1, slots), 1) < count_ref[0]
+    sign = (1 - 2 * (normal % 2)).astype(jnp.float32)
+    scale_ref[...] = jnp.where(live, FACE_AREA * sign, 0.0)
+
+
+def rows_kernel(n_in, *refs):
+    ins, outs = refs[:n_in], refs[n_in + 1 :]
     is_odd = lax.axis_index("gy") % 2
     at = 0
     for ref in ins:
@@ -89,10 +117,9 @@
     n_ghost = 1 if n_y == 2 else 2
     parts, refs = refs[:n_in], refs[n_in:]
     ghosts, refs = refs[:n_ghost], refs[n_ghost:]
-    sigma_ref, gamma_ref, plasma_ref, g_ref, count_ref = refs[:5]
-    cell_ref, owner_ref, tile_ref, normal_ref = refs[5:9]
-    e_out, h_out, part_out = refs[9:12]
-    field, coef, gain_h, tensor = refs[12:16]
+    table_ref, hot_ref, tile_hot_ref, ints_ref, scale_ref = refs[:5]
+    e_out, h_out, part_out = refs[5:8]
+    field, coef, gain_h, tensor = refs[8:12]
     _, rows, lanes = parts[0].shape
     planes = e_out.shape[1]
     depth = steps
@@ -128,16 +155,16 @@
     upper_lanes = lane < jnp.where(high_z, depth, 0)
     lower_lanes = lane >= jnp.where(low_z, lanes - depth, lanes)
     n_fields = 10
-    z_tiles = counts[3]
-
-    def edges(base):
+    z_tiles = counts[3] // 2
+
+    def edges(part):
         out = []
         for tile in range(z_tiles):
-            first, second = whole(base, tile), whole(base + 1, tile)
+            first, second = whole(part, tile), whole(part, z_tiles + tile)
             out.append((jnp.where(even_z, first, second), jnp.where(even_z, second, first)))
         return out
 
-    own_edges, first_edges, second_edges = edges(3), edges(5), edges(7)
+    own_edges, first_edges, second_edges = edges(3), edges(4), edges(5)
     for cls in range(3):
         for j in range(n_fields * planes):
             tile, slot = j // per_tile, j % per_tile
@@ -161,18 +188,7 @@
 
     wide = 2 * lanes
 
-    def splat(value):
-        return jnp.full((8, lanes), value, jnp.float32)
-
-    table = []
-    for which in range(materials):
-        sigma, gamma, plasma = splat(sigma_ref[which]), splat(gamma_ref[which]), splat(plasma_ref[which])
-        table.append((
-            (1.0 - sigma * STEP_DT / 2) / (1.0 + sigma * STEP_DT / 2),
-            STEP_DT / (1.0 + sigma * STEP_DT / 2),
-            (1.0 - gamma * STEP_DT / 2) / (1.0 + gamma * STEP_DT / 2),
-            plasma * STEP_DT / (1.0 + gamma * STEP_DT / 2),
-        ))
+    table = [[table_ref[4 * m + i] for i in range(4)] for m in range(materials)]
     for plane in range(1, 3 * planes - 1):
         for r in range(0, full_rows, 8):
             for c in range(0, wide, lanes):
@@ -226,7 +242,8 @@
                 drude = keep_j * field[6 + comp, plane] + gain_j * old
                 field[6 + comp, plane] = drude
                 field[comp, plane] = keep_e * old + gain_e * (curl - drude)
-        g = g_ref[t - 1]
+        g = table_ref[4 * materials + t - 1]
+        g = jnp.concatenate([g] * (rows // 8), 0)
         for plane in range(planes):
             e = [field[i, planes + plane, :rows, :lanes] for i in range(3)]
             h = [field[3 + i, planes + plane, :rows, :lanes] for i in range(3)]
@@ -250,36 +267,29 @@
     cells = planes * rows
     high, low = halves(tensor[...].reshape(len(PAIRS) * cells, lanes))
     lhs = jnp.concatenate([high, low], 1)
-    slots = cell_ref.shape[1]
+    slots = hot_ref.shape[1]
     owners = part_out.shape[0]
     chunk = 256
     total = jnp.zeros((2 * owners * 8, TILE_DEV), jnp.float32)
     for at in range(0, slots, chunk):
-        cell = cell_ref[:, at : at + chunk]
-        owner = owner_ref[:, at : at + chunk]
-        normal = normal_ref[:, at : at + chunk]
-        tile = tile_ref[:, at : at + chunk]
-        live = (at + lax.broadcasted_iota(jnp.int32, (1, chunk), 1)) < count_ref[0, 0, 0]
-        hot = jnp.where(lax.broadcasted_iota(jnp.int32, (lanes, chunk), 0) == cell % lanes, 1.0, 0.0).astype(jnp.bfloat16)
+        here = slice(at, at + chunk)
+        in_row, owner, axis = ints_ref[0:1, here], ints_ref[1:2, here], ints_ref[2:3, here]
+        hot = hot_ref[:, here]
         picked = jnp.dot(lhs, jnp.concatenate([hot, hot], 0), preferred_element_type=jnp.float32)
-        in_row = lax.broadcasted_iota(jnp.int32, (cells, chunk), 0) == cell // lanes
+        in_row = lax.broadcasted_iota(jnp.int32, (cells, chunk), 0) == in_row
         vals = {
             p: jnp.sum(jnp.where(in_row, picked[i * cells : (i + 1) * cells], 0.0), axis=0, keepdims=True)
             for i, p in enumerate(PAIRS)
         }
-        axis = normal // 2
-        sign = (1 - 2 * (normal % 2)).astype(jnp.float32)
-        scale = jnp.where(live, FACE_AREA * sign, 0.0)
         row_force = []
         for i in range(3):
             by = [vals[min(i, a), max(i, a)] for a in range(3)]
-            row_force.append(scale * jnp.where(axis == 0, by[0], jnp.where(axis == 1, by[1], by[2])))
+            row_force.append(scale_ref[:, here] * jnp.where(axis == 0, by[0], jnp.where(axis == 1, by[1], by[2])))
         stacked = jnp.concatenate(row_force + [jnp.zeros((5, chunk), jnp.float32)], 0)
         spread = jnp.concatenate([jnp.where(owner == o, stacked, 0.0) for o in range(owners)], 0)
         a_high, a_low = halves(spread)
         a = jnp.concatenate([a_high, a_low], 0)
-        tile_hot = jnp.where(lax.broadcasted_iota(jnp.int32, (TILE_DEV, chunk), 0) == tile, 1.0, 0.0).astype(jnp.bfloat16)
-        total = total + lax.dot_general(a, tile_hot, (((1,), (1,)), ((), ())), preferred_element_type=jnp.float32)
+        total = total + lax.dot_general(a, tile_hot_ref[:, here], (((1,), (1,)), ((), ())), preferred_element_type=jnp.float32)
     part = total[: owners * 8] + total[owners * 8 :]
     for o in range(owners):
         part_out[o] = part[o * 8 : (o + 1) * 8]
@@ -300,42 +310,53 @@
             jax.ShapeDtypeStruct((z_tiles, rows, lanes), f32),
             jax.ShapeDtypeStruct((z_tiles, rows, lanes), f32),
         ),
-        in_specs=[VMEM] * 4,
+        in_specs=[pl.BlockSpec(memory_space=pltpu.HBM)] * 4,
         out_specs=(VMEM,) * 3,
+        scratch_shapes=[pltpu.VMEM((planes, rows, lanes), jnp.int32), pltpu.SemaphoreType.DMA((4,))],
         compiler_params=pltpu.CompilerParams(vmem_limit_bytes=4 << 20),
         name="pack",
-    )(e_field, h_field, current, material)
+    )(*(pltpu.with_memory_space_constraint(v, pltpu.HBM) for v in (
+        e_field.reshape(3 * planes, rows, lanes), h_field.reshape(3 * planes, rows, lanes),
+        current.reshape(3 * planes, rows, lanes), material)))
 
     def send(value, axis, second=False):
         return lax.ppermute(value, AXES, full_swap(sizes, axis, second))
 
     x_first, x_second = send(brick, "gx"), send(brick, "gx", True)
-    z_first, z_second = send(z_first, "gz"), send(z_second, "gz", True)
-    parts = [
-        brick,
-        x_first,
-        x_second,
-        z_first,
-        z_second,
-        send(z_first, "gx"),
-        send(z_second, "gx"),
-        send(z_first, "gx", True),
-        send(z_second, "gx", True),
-    ]
+    edges = jnp.concatenate([send(z_first, "gz"), send(z_second, "gz", True)])
+    parts = [brick, x_first, x_second, edges, send(edges, "gx"), send(edges, "gx", True)]
+
+    slots = surf_cell.size
+    materials = sigma_table.shape[0]
+    prepared = pl.pallas_call(
+        functools.partial(prepare_kernel, materials, steps, planes * rows, lanes),
+        out_shape=(
+            jax.ShapeDtypeStruct((4 * materials + steps, 8, lanes), f32),
+            jax.ShapeDtypeStruct((lanes, slots), jnp.bfloat16),
+            jax.ShapeDtypeStruct((TILE_DEV, slots), jnp.bfloat16),
+            jax.ShapeDtypeStruct((8, slots), jnp.int32),
+            jax.ShapeDtypeStruct((1, slots), f32),
+        ),
+        in_specs=[SMEM] * 4 + [VMEM] * 5 + [pl.BlockSpec(memory_space=pl.ANY)],
+        out_specs=(VMEM,) * 5,
+        compiler_params=pltpu.CompilerParams(vmem_limit_bytes=6 << 20),
+        cost_estimate=pl.CostEstimate(flops=1 << 20, bytes_accessed=1 << 20, transcendentals=0),
+        name="prepare",
+    )(sigma_table, gamma_table, plasma_table, g_kernel, row_count,
+      surf_cell.reshape(1, slots), surf_owner.reshape(1, slots), surf_tile.reshape(1, slots), surf_normal.reshape(1, slots), edges)
     counts = [p.shape[0] for p in parts]
     n_ghost = 1 if n_y == 2 else 2
     outgoing = pl.pallas_call(
-        functools.partial(rows_kernel, len(parts), n_y),
+        functools.partial(rows_kernel, len(parts)),
         out_shape=[jax.ShapeDtypeStruct((sum(counts), 8, lanes), f32)] * n_ghost,
-        in_specs=[VMEM] * len(parts),
+        in_specs=[VMEM] * len(parts) + [pl.BlockSpec(memory_space=pl.ANY)],
         out_specs=[VMEM] * n_ghost,
         compiler_params=pltpu.CompilerParams(vmem_limit_bytes=6 << 20),
         name="rows",
-    )(*parts)
+    )(*parts, prepared[-1])
     ghosts = [send(v, "gy", bool(i)) for i, v in enumerate(outgoing)]
 
     owners = n_x * n_y
-    slots = surf_cell.size
     wide = 2 * lanes
     e_out, h_out, part = pl.pallas_call(
         functools.partial(main_kernel, sizes, steps, sigma_table.shape[0], counts),
@@ -344,7 +365,7 @@
             jax.ShapeDtypeStruct(h_field.shape, f32),
             jax.ShapeDtypeStruct((owners, 8, TILE_DEV), f32),
         ),
-        in_specs=[VMEM] * (len(parts) + n_ghost) + [SMEM] * 5 + [VMEM] * 4,
+        in_specs=[VMEM] * (len(parts) + n_ghost + len(prepared)),
         out_specs=(VMEM,) * 3,
         scratch_shapes=[
             pltpu.VMEM((10, 3 * planes, rows + 8, wide), f32),
@@ -354,8 +375,7 @@
         ],
         compiler_params=pltpu.CompilerParams(vmem_limit_bytes=24 << 20),
         name="march",
-    )(*parts, *ghosts, sigma_table, gamma_table, plasma_table, g_kernel, row_count,
-      surf_cell.reshape(1, slots), surf_owner.reshape(1, slots), surf_tile.reshape(1, slots), surf_normal.reshape(1, slots))
+    )(*parts, *ghosts, *prepared)
     got = lax.all_to_all(part, ("gx", "gy"), split_axis=0, concat_axis=0, tiled=True)
     force = jnp.sum(got[:, :3], axis=0)
     return e_out, h_out, force

time: 36.4 us -> 30.8 us (0.85)
  local copies, waits for them, and re-layouts: 4.09 us -> 0.65 us
  waiting for transfers between devices: 6.56 us -> 4.62 us
  Pallas kernels: 3.98 us -> 5.36 us
  blocking collectives: 10.9 us -> 9.95 us
  starting transfers between devices: 8.51 us -> 7.97 us
    unnamed x24 -> x17, local copies, waits for them, and re-layouts: 4.09 us -> 0.65 us
    ppermute x9 -> x7, waiting for transfers between devices: 6.56 us -> 4.62 us  [send(): return lax.ppermute(value, AXES, full_swap(sizes, axis, second))]
    pallas_call x1, Pallas kernels: 0.22 us -> 1.36 us  [local(): pl.pallas_call(functools.partial(pack_kernel, steps), out_shape=(jax.Shap...]
    all_to_all x1, blocking collectives: 10.9 us -> 9.95 us  [local(): lax.all_to_all(part, ('gx', 'gy'), split_axis=0, concat_axis=0, tiled=True)]
    pallas_call x1 -> x2, Pallas kernels: 0.05 us -> 0.82 us  [the longest x1 0.79 us: local(): pl.pallas_call(functools.partial(prepare_kernel, materials, steps, planes...]
    ppermute x9 -> x7, starting transfers between devices: 8.51 us -> 7.97 us  [send(): return lax.ppermute(value, AXES, full_swap(sizes, axis, second))]
    pallas_call x1, Pallas kernels: 3.7 us -> 3.18 us  [local(): pl.pallas_call(functools.partial(main_kernel, sizes, steps, sigma_table.s...]
  transfers between devices with their start and end apart: 9 -> 7, of which waited for: 4 -> 3; matrix products, arithmetic and copies ran while one was open for 0% -> 0% of each run, Pallas kernels for 0% -> 3%
where the time goes in v3:
time: 30.8 us; the launch traced here: 30.6 us
  blocking collectives  9.95 us (32%)
  starting transfers between devices  7.97 us (26%)
  Pallas kernels  5.36 us (17%)
  waiting for transfers between devices  4.62 us (15%)
  between operations  1.45 us (5%)
  local copies, waits for them, and re-layouts  0.65 us (2%)
  other arithmetic  0.59 us (2%)
    all_to_all x1, blocking collectives, local(): lax.all_to_all(part, ('gx', 'gy'), split_axis=0, concat_axis=0, tiled=True)  9.95 us
    ppermute x7, starting transfers between devices, send(): return lax.ppermute(value, AXES, full_swap(sizes, axis, second))  7.97 us
    ppermute x7, waiting for transfers between devices, send(): return lax.ppermute(value, AXES, full_swap(sizes, axis, second))  4.62 us
    pallas_call x1, Pallas kernels, local(): pl.pallas_call(functools.partial(main_kernel, sizes, steps, sigma_table.s...  3.18 us
    pallas_call x1, Pallas kernels, local(): pl.pallas_call(functools.partial(pack_kernel, steps), out_shape=(jax.Shap...  1.36 us
    pallas_call x1, Pallas kernels, local(): pl.pallas_call(functools.partial(prepare_kernel, materials, steps, planes...  0.79 us
    unnamed x17, local copies, waits for them, and re-layouts  0.65 us
  transfers between devices with their start and end apart: 7, of which 3 were waited for; matrix products, arithmetic and copies ran while one was open for 0% of the time, Pallas kernels for 3%

profile of v3, /device:TPU:0, one launch (start us, length us, event | category | flops | bytes accessed | tf_op | source)
XLA Modules:
  0.0 30.6 jit_solution(3285010105787321571)
XLA Ops:
  0.6 1.4 %pack.1 = (f32[40,16,128]{2,1,0:T(8,128)S(1)}, f32[2,16,128]{2,1,0:T(8,128)S(1)}, f32[2,16,128]{2,1,0:T(8,128)S(1)}) custom-call(f32[12,16,128]{2,1,0:T(8,128)} %bitcast.11, f32[12,16,128]{2,1,0:T(8,128)} %bitcast.12, f32[12,16,128]{2,1,0:T(8,128)} %bitcast.13, s32[4,16,128]{2,1,0:T(8,128)} %m_ref.1), custom_call_target="tpu_custom_call" | custom-call | tf_op jit(solution)/shard_map/pack/pallas_call | solution.py:306
  2.0 0.6 %collective-permute-start.1 = (f32[40,16,128]{2,1,0:T(8,128)S(1)}, f32[40,16,128]{2,1,0:T(8,128)S(1)}, u32[]{:S(2)}, u32[]{:S(2)}) collective-permute-start(f32[40,16,128]{2,1,0:T(8,128)S(1)} %get-tuple-element.14.refs_0_), channel_id=1, source_target_pairs={{0,4},{1,5},{2,6},{3,7},{4,0},{5,1},{6,2},{7,3},{8,16},{9,17},{10,... | collective-permute-start | bytes 983048 | tf_op jit(solution)/shard_map/ppermute | solution.py:323
  2.6 4.1 %collective-permute-start = (f32[40,16,128]{2,1,0:T(8,128)S(1)}, f32[40,16,128]{2,1,0:T(8,128)S(1)}, u32[]{:S(2)}, u32[]{:S(2)}) collective-permute-start(f32[40,16,128]{2,1,0:T(8,128)S(1)} %get-tuple-element.14.refs_0_), channel_id=1, source_target_pairs={{0,8},{1,9},{2,10},{3,11},{4,12},{5,13},{6,14},{7,15},{8,0},{9,1},... | collective-permute-start | bytes 983048 | tf_op jit(solution)/shard_map/ppermute | solution.py:323
  6.7 1.5 %collective-permute-start.2 = (f32[2,16,128]{2,1,0:T(8,128)S(1)}, f32[2,16,128]{2,1,0:T(8,128)S(1)}, u32[]{:S(2)}, u32[]{:S(2)}) collective-permute-start(f32[2,16,128]{2,1,0:T(8,128)S(1)} %get-tuple-element.15), channel_id=1, source_target_pairs={{0,1},{1,0},{2,3},{3,2},{4,5},{5,4},{6,7},{7,6},{8,9},{9,8},{10,11... | collective-permute-start | bytes 49160 | tf_op jit(solution)/shard_map/ppermute | solution.py:323
  8.2 0.0 collective-permute-start.3
  8.2 2.2 %collective-permute-done.2 = f32[2,16,128]{2,1,0:T(8,128)S(1)} collective-permute-done((f32[2,16,128]{2,1,0:T(8,128)S(1)}, f32[2,16,128]{2,1,0:T(8,128)S(1)}, u32[]{:S(2)}, u32[]{:S(2)}) %collective-permute-start.2) | collective-permute-done | bytes 16416 | tf_op jit(solution)/shard_map/ppermute | solution.py:323
  10.4 0.0 collective-permute-done.3
  10.4 0.0 copy-start.3
  10.5 0.0 copy-start.6
  10.5 0.0 copy-start.7
  10.5 0.1 collective-permute-start.5
  10.6 1.6 %collective-permute-start.4 = (f32[4,16,128]{2,1,0:T(8,128)S(1)}, f32[4,16,128]{2,1,0:T(8,128)S(1)}, u32[]{:S(2)}, u32[]{:S(2)}) collective-permute-start(f32[4,16,128]{2,1,0:T(8,128)S(1)} %constant_dynamic-update-slice_fusion.after_ref.refs_3_), channel_id=1, source_target_pairs={{0,8},{1,9},{2,10},{3,11},{4,12},{5,13},{6,14},{7,15},{8,0},{9,1},... | collective-permute-start | bytes 98312 | tf_op jit(solution)/shard_map/ppermute | solution.py:323
  12.9 0.0 copy-start
  12.9 0.0 copy-start.4
  12.9 0.0 copy-start.5
  12.9 0.0 copy-done.2
  12.9 0.0 copy-done.3
  12.9 0.0 copy-done.6
  12.9 0.0 copy-done.7
  13.0 0.0 copy-done.1
  13.0 0.6 %copy-done = s32[1,1,1,1024]{3,2,1,0:T(1,128)S(1)} copy-done((s32[1,1,1,1024]{3,2,1,0:T(1,128)S(1)}, s32[1,1,1,1024]{3,2,1,0:T(1,128)}, u32[]{:S(2)}) %copy-start) | copy-done | bytes 4120
  13.6 0.0 copy-done.4
  13.6 0.8 %prepare.1 = (f32[16,8,128]{2,1,0:T(8,128)S(1)}, bf16[128,1024]{1,0:T(8,128)(2,1)S(1)}, bf16[128,1024]{1,0:T(8,128)(2,1)S(1)}, s32[8,1024]{1,0:T(8,128)S(1)}, f32[1,1024]{1,0:T(1,128)S(1)}) custom-call(f32[3]{0:T(128)S(1)} %copy-done.4, f32[3]{0:T(128)S(1)} %copy-done.5, f32[3]{0:T(128)S(1)} %copy-done.6, f32[4]{0:T(128)S(1)} %copy-done.7, ...), custom_call_target="tpu_custom_call" | custom-call | flops 1048576 | bytes 1048576 | tf_op jit(solution)/shard_map/prepare/pallas_call | solution.py:331
  14.4 0.0 collective-permute-done.5.refs_5_
  14.4 0.4 %collective-permute-done.4.refs_4_ = f32[4,16,128]{2,1,0:T(8,128)S(1)} collective-permute-done((f32[4,16,128]{2,1,0:T(8,128)S(1)}, f32[4,16,128]{2,1,0:T(8,128)S(1)}, u32[]{:S(2)}, u32[]{:S(2)}) %collective-permute-start.4) | collective-permute-done | bytes 32800 | tf_op jit(solution)/shard_map/ppermute | solution.py:323
  14.8 0.0 collective-permute-done.1.refs_2_
  14.8 0.0 collective-permute-done.refs_1_
  14.9 0.1 collective-permute-start.6
  14.9 1.9 %collective-permute-done.6.refs_6_ = f32[132,8,128]{2,1,0:T(8,128)S(1)} collective-permute-done((f32[132,8,128]{2,1,0:T(8,128)S(1)}, f32[132,8,128]{2,1,0:T(8,128)S(1)}, u32[]{:S(2)}, u32[]{:S(2)}) %collective-permute-start.6) | collective-permute-done | bytes 540704 | tf_op jit(solution)/shard_map/ppermute | solution.py:323
  16.9 3.2 %march.1 = (f32[3,4,16,128]{3,2,1,0:T(8,128)}, f32[3,4,16,128]{3,2,1,0:T(8,128)}, f32[8,8,128]{2,1,0:T(8,128)S(1)}) custom-call(f32[40,16,128]{2,1,0:T(8,128)S(1)} %get-tuple-element.14.refs_0_, f32[40,16,128]{2,1,0:T(8,128)S(1)} %collective-permute-done.refs_1_, f32[40,16,128]{2,1,0:T(8,128)S(1)} %collective-permute-done.1.refs_2_, ...), custom_call_target="tpu_custom_call" | custom-call | tf_op jit(solution)/shard_map/march/pallas_call | solution.py:361
  20.0 10.0 %all_to_all.5 = f32[8,8,128]{2,1,0:T(8,128)S(1)} all-to-all(f32[8,8,128]{2,1,0:T(8,128)S(1)} %get-tuple-element.24), channel_id=1, replica_groups=mesh['gx'=4,'gy'=2,'gz'=4] {'gx','gy'}, dimensions={0} | all-to-all | bytes 65536 | tf_op jit(solution)/shard_map/all_to_all | solution.py:379
  30.0 0.6 %slice_reduce_fusion = f32[3,128]{1,0:T(4,128)} fusion(f32[8,8,128]{2,1,0:T(8,128)S(1)} %all_to_all.5), kind=kLoop, calls=%fused_computation | loop fusion | flops 2688 | bytes 13824 | tf_op jit(solution)/shard_map/reduce_sum | solution.py:380
  (6 shorter events, 0.0 us)
Async XLA Ops:
  2.0 12.8 %collective-permute-start.1 = (f32[40,16,128]{2,1,0:T(8,128)S(1)}, f32[40,16,128]{2,1,0:T(8,128)S(1)}, u32[]{:S(2)}, u32[]{:S(2)}) collective-permute-start(f32[40,16,128]{2,1,0:T(8,128)S(1)} %get-tuple-element.14.refs_0_), channel_id=1, source_target_pairs={{0,4},{1,5},{2,6},{3,7},{4,0},{5,1},{6,2},{7,3},{8,16},{9,17},{10,... | collective-permute-start | bytes 983048 | tf_op jit(solution)/shard_map/ppermute | solution.py:323
  2.6 12.3 %collective-permute-start = (f32[40,16,128]{2,1,0:T(8,128)S(1)}, f32[40,16,128]{2,1,0:T(8,128)S(1)}, u32[]{:S(2)}, u32[]{:S(2)}) collective-permute-start(f32[40,16,128]{2,1,0:T(8,128)S(1)} %get-tuple-element.14.refs_0_), channel_id=1, source_target_pairs={{0,8},{1,9},{2,10},{3,11},{4,12},{5,13},{6,14},{7,15},{8,0},{9,1},... | collective-permute-start | bytes 983048 | tf_op jit(solution)/shard_map/ppermute | solution.py:323
  6.7 3.7 %collective-permute-start.2 = (f32[2,16,128]{2,1,0:T(8,128)S(1)}, f32[2,16,128]{2,1,0:T(8,128)S(1)}, u32[]{:S(2)}, u32[]{:S(2)}) collective-permute-start(f32[2,16,128]{2,1,0:T(8,128)S(1)} %get-tuple-element.15), channel_id=1, source_target_pairs={{0,1},{1,0},{2,3},{3,2},{4,5},{5,4},{6,7},{7,6},{8,9},{9,8},{10,11... | collective-permute-start | bytes 49160 | tf_op jit(solution)/shard_map/ppermute | solution.py:323
  8.2 2.3 %collective-permute-start.3 = (f32[2,16,128]{2,1,0:T(8,128)S(1)}, f32[2,16,128]{2,1,0:T(8,128)S(1)}, u32[]{:S(2)}, u32[]{:S(2)}) collective-permute-start(f32[2,16,128]{2,1,0:T(8,128)S(1)} %get-tuple-element.16), channel_id=1, source_target_pairs={{0,4},{1,2},{2,1},{3,7},{4,0},{5,6},{6,5},{7,3},{8,12},{9,10},{10,... | collective-permute-start | bytes 49160 | tf_op jit(solution)/shard_map/ppermute | solution.py:323
  10.4 2.5 %copy-start.2 = (s32[1,1,1,1024]{3,2,1,0:T(1,128)S(1)}, s32[1,1,1,1024]{3,2,1,0:T(1,128)}, u32[]{:S(2)}) copy-start(s32[1,1,1,1024]{3,2,1,0:T(1,128)} %param.23) | copy-start | bytes 12292
  10.4 2.5 %copy-start.3 = (s32[1,1,1,1024]{3,2,1,0:T(1,128)S(1)}, s32[1,1,1,1024]{3,2,1,0:T(1,128)}, u32[]{:S(2)}) copy-start(s32[1,1,1,1024]{3,2,1,0:T(1,128)} %param.24) | copy-start | bytes 12292
  10.5 2.5 %copy-start.6 = (f32[3]{0:T(128)S(1)}, f32[3]{0:T(128)}, u32[]{:S(2)}) copy-start(f32[3]{0:T(128)} %plasma_ref.1) | copy-start | bytes 40
  10.5 2.5 %copy-start.7 = (f32[4]{0:T(128)S(1)}, f32[4]{0:T(128)}, u32[]{:S(2)}) copy-start(f32[4]{0:T(128)} %g_ref.1) | copy-start | bytes 52
  10.5 3.9 %collective-permute-start.5 = (f32[4,16,128]{2,1,0:T(8,128)S(1)}, f32[4,16,128]{2,1,0:T(8,128)S(1)}, u32[]{:S(2)}, u32[]{:S(2)}) collective-permute-start(f32[4,16,128]{2,1,0:T(8,128)S(1)} %constant_dynamic-update-slice_fusion.after_ref.refs_3_), channel_id=1, source_target_pairs={{0,4},{1,5},{2,6},{3,7},{4,0},{5,1},{6,2},{7,3},{8,16},{9,17},{10,... | collective-permute-start | bytes 98312 | tf_op jit(solution)/shard_map/ppermute | solution.py:323
  10.6 4.3 %collective-permute-start.4 = (f32[4,16,128]{2,1,0:T(8,128)S(1)}, f32[4,16,128]{2,1,0:T(8,128)S(1)}, u32[]{:S(2)}, u32[]{:S(2)}) collective-permute-start(f32[4,16,128]{2,1,0:T(8,128)S(1)} %constant_dynamic-update-slice_fusion.after_ref.refs_3_), channel_id=1, source_target_pairs={{0,8},{1,9},{2,10},{3,11},{4,12},{5,13},{6,14},{7,15},{8,0},{9,1},... | collective-permute-start | bytes 98312 | tf_op jit(solution)/shard_map/ppermute | solution.py:323
  12.2 0.7 %copy-start.1 = (s32[1,1,1,1024,1]{3,4,2,1,0:T(1,128)S(1)}, s32[1,1,1,1024,1]{3,4,2,1,0:T(1,128)}, u32[]{:S(2)}) copy-start(s32[1,1,1,1024,1]{3,4,2,1,0:T(1,128)} %param.22) | copy-start | bytes 12292
  12.9 0.7 %copy-start = (s32[1,1,1,1024]{3,2,1,0:T(1,128)S(1)}, s32[1,1,1,1024]{3,2,1,0:T(1,128)}, u32[]{:S(2)}) copy-start(s32[1,1,1,1024]{3,2,1,0:T(1,128)} %param.21) | copy-start | bytes 12292
  12.9 0.7 %copy-start.4 = (f32[3]{0:T(128)S(1)}, f32[3]{0:T(128)}, u32[]{:S(2)}) copy-start(f32[3]{0:T(128)} %sigma_ref.1) | copy-start | bytes 40
  12.9 0.7 %copy-start.5 = (f32[3]{0:T(128)S(1)}, f32[3]{0:T(128)}, u32[]{:S(2)}) copy-start(f32[3]{0:T(128)} %gamma_ref.1) | copy-start | bytes 40
  14.9 2.0 %collective-permute-start.6 = (f32[132,8,128]{2,1,0:T(8,128)S(1)}, f32[132,8,128]{2,1,0:T(8,128)S(1)}, u32[]{:S(2)}, u32[]{:S(2)}) collective-permute-start(f32[132,8,128]{2,1,0:T(8,128)S(1)} %rows.1), channel_id=1, source_target_pairs={{0,4},{1,5},{2,6},{3,7},{4,0},{5,1},{6,2},{7,3},{8,12},{9,13},{10,... | collective-permute-start | bytes 1622024 | tf_op jit(solution)/shard_map/ppermute | solution.py:323

commit v4 on v3

v4 whole, which is shorter than its diff:
```python
import functools

import jax
import jax.numpy as jnp
from jax import lax
from jax.experimental import pallas as pl
from jax.experimental.pallas import tpu as pltpu
from jax.sharding import PartitionSpec as P


STEP_DT = 0.5
FACE_AREA = 0.25
TILE_DEV = 128
PAIRS = ((0, 0), (0, 1), (0, 2), (1, 1), (1, 2), (2, 2))
AXES = ("gx", "gy", "gz")
VMEM = pl.BlockSpec(memory_space=pltpu.VMEM)
SMEM = pl.BlockSpec(memory_space=pltpu.SMEM)


def partner(index, size, second):
    if not second:
        return index ^ 1
    return (index - 1) % size if index % 2 == 0 else (index + 1) % size


def full_swap(sizes, axis, second=False):
    pairs = []
    at = AXES.index(axis)
    for x in range(sizes[0]):
        for y in range(sizes[1]):
            for z in range(sizes[2]):
                to = [x, y, z]
                if second and to[at] in (0, sizes[at] - 1) and axis != "gy":
                    to[1] = y ^ 1
                else:
                    to[at] = partner(to[at], sizes[at], second)
                pairs.append(((x * sizes[1] + y) * sizes[2] + z, (to[0] * sizes[1] + to[1]) * sizes[2] + to[2]))
    return pairs


def pack_kernel(depth, n_ghost, *refs):
    e_ref, h_ref, j_ref, m_ref = refs[:4]
    n_small = (len(refs) - 4 - 4 - n_ghost) // 2
    small, refs = refs[4 : 4 + n_small], refs[4 + n_small :]
    brick_ref, edge_ref, refs = refs[0], refs[1], refs[2:]
    sends, kept, (m_buf, sems) = refs[:n_ghost], refs[n_ghost : n_ghost + n_small], refs[n_ghost + n_small :]
    planes, rows, lanes = m_ref.shape
    count = 3 * planes
    copies = [pltpu.make_async_copy(ref, brick_ref.at[pl.ds(i * count, count)], sems.at[i]) for i, ref in enumerate((e_ref, h_ref, j_ref))]
    copies.append(pltpu.make_async_copy(m_ref, m_buf, sems.at[3]))
    copies += [pltpu.make_async_copy(src, dst, sems.at[4 + i]) for i, (src, dst) in enumerate(zip(small, kept, strict=True))]
    for copy in copies:
        copy.start()
    width = 2 * depth * planes
    per_tile = lanes // width
    lane = lax.broadcasted_iota(jnp.int32, (rows, lanes), 1)
    packed = [jnp.zeros((rows, lanes), jnp.float32) for _ in range(edge_ref.shape[0])]
    for j in range(3 * count + planes):
        if j % count == 0:
            copies[j // count].wait()
        if j >= 3 * count:
            brick_ref[j] = (m_buf[j - 3 * count] + 1).astype(jnp.float32)
        value = brick_ref[j]
        tile, start = j // planes // per_tile, j // planes % per_tile * width + j % planes * 2 * depth
        turned = pltpu.roll(value, (start + depth) % lanes, 1)
        packed[tile] = jnp.where((lane >= start) & (lane < start + 2 * depth), turned, packed[tile])
    is_odd = lax.axis_index("gy") % 2 == 1
    for tile, value in enumerate(packed):
        edge_ref[tile] = value
        first, last = value[:8], value[rows - 8 :]
        sends[0][tile] = jnp.where(is_odd, first, last)
        if n_ghost > 1:
            sends[1][tile] = jnp.where(is_odd, last, first)
    for copy in copies[4:]:
        copy.wait()


def sides_y(depth, n_y, lanes):
    y = lax.axis_index("gy")
    even = y % 2 == 0
    row = lax.broadcasted_iota(jnp.int32, (8, lanes), 0)
    upper_to = jnp.where(y < n_y - 1, depth, 0)
    lower_from = jnp.where(y > 0, 8 - depth, 8)

    def pick(values):
        if len(values) == 1:
            wanted = (row >= jnp.where(even, 0, lower_from)) & (row < jnp.where(even, upper_to, 8))
            return jnp.where(wanted, values[0], 0.0)
        upper = jnp.where(even, values[0], values[1])
        lower = jnp.where(even, values[1], values[0])
        return jnp.where(row < upper_to, upper, jnp.where(row >= lower_from, lower, 0.0))

    return pick


def widen_kernel(depth, n_y, edge_ref, *refs):
    ghosts, out = refs[:-1], refs[-1]
    pick = sides_y(depth, n_y, edge_ref.shape[2])
    rows = edge_ref.shape[1]
    for tile in range(edge_ref.shape[0]):
        out[tile, :rows] = edge_ref[tile]
        out[tile, rows:] = pick([g[tile] for g in ghosts])


def merge_kernel(depth, n_z, first_ref, second_ref, out_ref):
    z = lax.axis_index("gz")
    even = z % 2 == 0
    shape = out_ref.shape[1:]
    place = lax.broadcasted_iota(jnp.int32, shape, 1) % (2 * depth)
    is_lower = place < jnp.where(z > 0, depth, 0)
    is_upper = place >= jnp.where(z < n_z - 1, depth, 2 * depth)
    for tile in range(out_ref.shape[0]):
        first, second = first_ref[tile], second_ref[tile]
        upper = jnp.where(even, first, second)
        lower = jnp.where(even, second, first)
        out_ref[tile] = jnp.where(is_upper, upper, jnp.where(is_lower, lower, 0.0))


def rows_kernel(depth, n_in, *refs):
    ins, outs = refs[:n_in], refs[n_in + 1 :]
    is_odd = lax.axis_index("gy") % 2
    row = lax.broadcasted_iota(jnp.int32, (8, outs[0].shape[2]), 0)
    at = 0
    for ref in ins:
        count, rows, _ = ref.shape
        for which, out in enumerate(outs):
            last = (1 - is_odd) if which == 0 else is_odd
            start = pl.multiple_of(last * (rows - 8), 8)
            mine = (row >= jnp.where(last == 1, 8 - depth, 0)) & (row < jnp.where(last == 1, 8, depth))
            for j in range(0, count, 2):
                kept, turned = ref[j, pl.ds(start, 8), :], ref[j + 1, pl.ds(start, 8), :]
                out[(at + j) // 2] = jnp.where(mine, kept, pltpu.roll(turned, 4, 0))
        at += count


def prepare_kernel(materials, steps, lanes, sigma_ref, gamma_ref, plasma_ref, g_ref,
                   cell_ref, owner_ref, tile_ref, normal_ref, count_ref, after_ref,
                   table_ref, hot_ref, tile_hot_ref, ints_ref, scale_ref):
    del after_ref
    slots = cell_ref.shape[1]
    shape = table_ref.shape[1:]

    def splat(ref, at):
        return jnp.broadcast_to(ref[:, at : at + 1], shape)

    for which in range(materials):
        sigma, gamma, plasma = splat(sigma_ref, which), splat(gamma_ref, which), splat(plasma_ref, which)
        table_ref[4 * which] = (1.0 - sigma * STEP_DT / 2) / (1.0 + sigma * STEP_DT / 2)
        table_ref[4 * which + 1] = STEP_DT / (1.0 + sigma * STEP_DT / 2)
        table_ref[4 * which + 2] = (1.0 - gamma * STEP_DT / 2) / (1.0 + gamma * STEP_DT / 2)
        table_ref[4 * which + 3] = plasma * STEP_DT / (1.0 + gamma * STEP_DT / 2)
    for t in range(steps):
        table_ref[4 * materials + t] = splat(g_ref, t)
    cell, normal = cell_ref[...], normal_ref[...]
    in_lane, in_row = cell % lanes, cell // lanes
    hot = lax.broadcasted_iota(jnp.int32, (lanes, slots), 0) == in_lane
    hot_ref[...] = jnp.where(hot, 1.0, 0.0).astype(jnp.bfloat16)
    tile_hot = lax.broadcasted_iota(jnp.int32, (TILE_DEV, slots), 0) == tile_ref[...]
    tile_hot_ref[...] = jnp.where(tile_hot, 1.0, 0.0).astype(jnp.bfloat16)
    ints_ref[0:1] = in_row
    ints_ref[1:2] = owner_ref[...]
    ints_ref[2:3] = normal // 2
    live = lax.broadcasted_iota(jnp.int32, (1, slots), 1) < count_ref[0, 0, 0]
    sign = (1 - 2 * (normal % 2)).astype(jnp.float32)
    scale_ref[...] = jnp.where(live, FACE_AREA * sign, 0.0)


def main_kernel(sizes, steps, materials, n_ghost, *refs):
    n_x, n_y, _ = sizes
    bricks, ghosts, refs = refs[:3], refs[3 : 3 + n_ghost], refs[3 + n_ghost :]
    edge_refs, refs = refs[:3], refs[3:]
    table_ref, hot_ref, tile_hot_ref, ints_ref, scale_ref = refs[:5]
    e_out, h_out, part_out = refs[5:8]
    field, coef, side, side_coef, tensor = refs[8:13]
    n_msg, rows, lanes = bricks[0].shape
    planes = e_out.shape[1]
    depth = steps
    x, y, z = (lax.axis_index(a) for a in AXES)
    even_x = x % 2 == 0
    low_x, high_x, low_y, low_z = x > 0, x < n_x - 1, y > 0, z > 0
    pick = sides_y(depth, n_y, lanes)
    full = rows + 8

    def whole(which, j):
        at = which * n_msg + j
        values = [g[at // 2] for g in ghosts]
        if at % 2:
            values = [pltpu.roll(v, 4, 0) for v in values]
        return jnp.concatenate([bricks[which][j], pick(values)], 0)

    for j in range(n_msg):
        f, p = j // planes, j % planes
        first, second = whole(1, j), whole(2, j)
        field[f, planes + p] = whole(0, j)
        field[f, p] = jnp.where(low_x, jnp.where(even_x, second, first), 0.0)
        field[f, 2 * planes + p] = jnp.where(high_x, jnp.where(even_x, first, second), 0.0)

    width = 2 * depth * planes
    per_tile = lanes // width
    lane = lax.broadcasted_iota(jnp.int32, (full, lanes), 1)
    at_low = lane < jnp.where(low_x, width, 0)
    at_own = (lane >= width) & (lane < 2 * width)
    at_high = (lane >= 2 * width) & (lane < jnp.where(high_x, 3 * width, 0))
    tiles = []
    for tile in range(edge_refs[0].shape[0]):
        own, first, second = (r[tile] for r in edge_refs)
        tiles.append((jnp.where(even_x, second, first), own, jnp.where(even_x, first, second)))
    for f in range(n_msg // planes):
        start = f % per_tile * width
        low, own, high = (
            pltpu.roll(v, (cls * width - start) % lanes, 1) if cls * width != start else v
            for cls, v in enumerate(tiles[f // per_tile])
        )
        side[f] = jnp.where(at_low, low, jnp.where(at_own, own, jnp.where(at_high, high, 0.0)))

    table = [[table_ref[4 * m + i] for i in range(4)] for m in range(materials)]

    def look_up(code, which):
        value = jnp.zeros((8, lanes), jnp.float32)
        for m in range(materials):
            value = jnp.where(code == float(m + 1), table[m][which], value)
        return value

    for r in range(0, full, 8):
        for which in range(4):
            for plane in range(1, 3 * planes - 1):
                coef[which, plane, r : r + 8] = look_up(field[9, plane, r : r + 8], which)
            side_coef[which, r : r + 8] = look_up(side[9, r : r + 8], which)

    row = lax.broadcasted_iota(jnp.int32, (full, lanes), 0)
    dt_all = jnp.where(row < jnp.where(low_y, full, full - depth), STEP_DT, 0.0)
    dt_low = jnp.where(low_x, dt_all, 0.0)
    dt_side = jnp.where((lane >= jnp.where(low_x, 0, width)) & (lane < 3 * width), dt_all, 0.0)
    dt_side = jnp.where(lane % (2 * depth) >= jnp.where(low_z, 0, depth), dt_side, 0.0)

    def turn(v, by):
        by = by % lanes
        return pltpu.roll(v, by, 1) if by else v

    def next_y(v):
        return pltpu.roll(v, full - 1, 0)

    def prev_y(v):
        return pltpu.roll(v, 1, 0)

    def above(plane):
        return 2 * depth * plane + depth

    def next_z(v, ghost, plane):
        return jnp.where(lane == lanes - 1, turn(ghost, lanes - 1 - above(plane)), turn(v, -1))

    def prev_z(v, ghost, plane):
        return jnp.where(lane == 0, turn(ghost, 1 - above(plane)), turn(v, 1))

    last = 3 * planes - 1
    for t in range(1, steps + 1):
        final = t == steps
        keep_rows = rows if final else full
        h_planes = range(t - 1, last - t + 1)
        ex, ey, ez, hx, hy, hz = (side[i] for i in range(6))
        ex_z, ey_z = turn(ex, -1), turn(ey, -1)
        for plane in h_planes:
            here = lane == above(plane) - 1
            ex_z = jnp.where(here, turn(field[0, plane], above(plane) - 1), ex_z)
            ey_z = jnp.where(here, turn(field[1, plane], above(plane) - 1), ey_z)
        ey_x, ez_x = turn(ey, -2 * depth), turn(ez, -2 * depth)
        ghx = hx - dt_side * ((next_y(ez) - ez) - (ey_z - ey))
        ghy = hy - dt_side * ((ex_z - ex) - (ez_x - ez))
        ghz = hz - dt_side * ((ey_x - ey) - (next_y(ex) - ex))
        gex, gey, gez = ex, ey, ez
        hx_above, hy_above = turn(ghx, 1), turn(ghy, 1)
        for plane in h_planes:
            ex, ey, ez = field[0, plane], field[1, plane], field[2, plane]
            hx, hy, hz = field[3, plane], field[4, plane], field[5, plane]
            ey_x, ez_x = field[1, plane + 1], field[2, plane + 1]
            dt = dt_low if plane < planes else dt_all
            hy = hy - dt * ((next_z(ex, gex, plane) - ex) - (ez_x - ez))
            hz = hz - dt * ((ey_x - ey) - (next_y(ex) - ex))
            field[4, plane] = hy
            field[5, plane] = hz
            if plane < t:
                continue
            hx = hx - dt * ((next_y(ez) - ez) - (next_z(ey, gey, plane) - ey))
            field[3, plane] = hx
            if not final:
                here = lane == above(plane)
                hx_above = jnp.where(here, turn(hx, above(plane) - (lanes - 1)), hx_above)
                hy_above = jnp.where(here, turn(hy, above(plane) - (lanes - 1)), hy_above)
            hy_x, hz_x = field[4, plane - 1], field[5, plane - 1]
            curls = (
                (hz - prev_y(hz)) - (hy - prev_z(hy, ghy, plane)),
                (hx - prev_z(hx, ghx, plane)) - (hz - hz_x),
                (hy - hy_x) - (hx - prev_y(hx)),
            )
            keep_e, gain_e, keep_j, gain_j = (coef[i, plane, :keep_rows] for i in range(4))
            for comp, (old, curl) in enumerate(zip((ex, ey, ez), curls, strict=True)):
                drude = keep_j * field[6 + comp, plane, :keep_rows] + gain_j * old[:keep_rows]
                if not final:
                    field[6 + comp, plane] = drude
                field[comp, plane, :keep_rows] = keep_e * old[:keep_rows] + gain_e * (curl[:keep_rows] - drude)
        if not final:
            side[3], side[4], side[5] = ghx, ghy, ghz
            hy_x, hz_x = turn(ghy, 2 * depth), turn(ghz, 2 * depth)
            curls = (
                (ghz - prev_y(ghz)) - (ghy - hy_above),
                (ghx - hx_above) - (ghz - hz_x),
                (ghy - hy_x) - (ghx - prev_y(ghx)),
            )
            keep_e, gain_e, keep_j, gain_j = (side_coef[i] for i in range(4))
            for comp, (old, curl) in enumerate(zip((gex, gey, gez), curls, strict=True)):
                drude = keep_j * side[6 + comp] + gain_j * old
                side[6 + comp] = drude
                side[comp] = keep_e * old + gain_e * (curl - drude)
        g = table_ref[4 * materials + t - 1]
        g = jnp.concatenate([g] * (rows // 8), 0)
        for plane in range(planes):
            e = [field[i, planes + plane, :rows] for i in range(3)]
            h = [field[3 + i, planes + plane, :rows] for i in range(3)]
            prod = {p: e[p[0]] * e[p[1]] + h[p[0]] * h[p[1]] for p in PAIRS}
            energy = 0.5 * (prod[0, 0] + prod[1, 1] + prod[2, 2])
            for i, p in enumerate(PAIRS):
                value = prod[p] - energy if p[0] == p[1] else prod[p]
                value = g * value
                if t > 1:
                    value = tensor[i, pl.ds(plane * rows, rows), :] + value
                tensor[i, pl.ds(plane * rows, rows), :] = value
            if final:
                for i in range(3):
                    e_out[i, plane] = e[i]
                    h_out[i, plane] = h[i]

    def halves(v):
        high = v.astype(jnp.bfloat16)
        return high, (v - high.astype(jnp.float32)).astype(jnp.bfloat16)

    cells = planes * rows
    high, low = halves(tensor[...].reshape(len(PAIRS) * cells, lanes))
    lhs = jnp.concatenate([high, low], 1)
    slots = hot_ref.shape[1]
    owners = part_out.shape[0]
    chunk = 256
    total = jnp.zeros((2 * owners * 8, TILE_DEV), jnp.float32)
    for at in range(0, slots, chunk):
        here = slice(at, at + chunk)
        in_row, owner, axis = ints_ref[0:1, here], ints_ref[1:2, here], ints_ref[2:3, here]
        hot = hot_ref[:, here]
        picked = jnp.dot(lhs, jnp.concatenate([hot, hot], 0), preferred_element_type=jnp.float32)
        in_row = lax.broadcasted_iota(jnp.int32, (cells, chunk), 0) == in_row
        vals = {
            p: jnp.sum(jnp.where(in_row, picked[i * cells : (i + 1) * cells], 0.0), axis=0, keepdims=True)
            for i, p in enumerate(PAIRS)
        }
        row_force = []
        for i in range(3):
            by = [vals[min(i, a), max(i, a)] for a in range(3)]
            row_force.append(scale_ref[:, here] * jnp.where(axis == 0, by[0], jnp.where(axis == 1, by[1], by[2])))
        stacked = jnp.concatenate(row_force + [jnp.zeros((5, chunk), jnp.float32)], 0)
        spread = jnp.concatenate([jnp.where(owner == o, stacked, 0.0) for o in range(owners)], 0)
        a_high, a_low = halves(spread)
        a = jnp.concatenate([a_high, a_low], 0)
        total = total + lax.dot_general(a, tile_hot_ref[:, here], (((1,), (1,)), ((), ())), preferred_element_type=jnp.float32)
    part = total[: owners * 8] + total[owners * 8 :]
    for o in range(owners):
        part_out[o] = part[o * 8 : (o + 1) * 8]


def local(sizes, *args):
    return body(sizes, *args)


def body(sizes, e_field, h_field, current, material, sigma_table, gamma_table, plasma_table, g_kernel,
          surf_cell, surf_owner, surf_tile, surf_normal, row_count):
    n_x, n_y, n_z = sizes
    steps = g_kernel.shape[0]
    planes, rows, lanes = material.shape
    f32 = jnp.float32
    n_msg = 10 * planes
    per_tile = lanes // (2 * steps * planes)
    z_tiles = -(-10 // per_tile)
    n_ghost = 1 if n_y == 2 else 2
    slots = surf_cell.size
    materials = sigma_table.shape[0]
    hbm = pl.BlockSpec(memory_space=pltpu.HBM)

    def shape(*dims, dtype=f32):
        return jax.ShapeDtypeStruct(dims, dtype)

    def grant(mib):
        return pltpu.CompilerParams(vmem_limit_bytes=mib << 20)

    def send(value, axis, second=False):
        return lax.ppermute(value, AXES, full_swap(sizes, axis, second))

    small = [
        sigma_table.reshape(1, materials),
        gamma_table.reshape(1, materials),
        plasma_table.reshape(1, materials),
        g_kernel.reshape(1, steps),
    ] + [v.reshape(1, slots) for v in (surf_cell, surf_owner, surf_tile, surf_normal)]
    args = [v.reshape(3 * planes, rows, lanes) for v in (e_field, h_field, current)] + [material] + small
    packed = pl.pallas_call(
        functools.partial(pack_kernel, steps, n_ghost),
        out_shape=[shape(n_msg, rows, lanes), shape(z_tiles, rows, lanes)]
        + [shape(z_tiles, 8, lanes)] * n_ghost
        + [shape(*v.shape, dtype=v.dtype) for v in small],
        in_specs=[hbm] * len(args),
        out_specs=[VMEM] * (2 + n_ghost + len(small)),
        scratch_shapes=[pltpu.VMEM((planes, rows, lanes), jnp.int32), pltpu.SemaphoreType.DMA((len(args),))],
        compiler_params=grant(4),
        name="pack",
    )(*(pltpu.with_memory_space_constraint(v, pltpu.HBM) for v in args))
    brick, edge, outgoing, small = packed[0], packed[1], packed[2 : 2 + n_ghost], packed[2 + n_ghost :]

    x_first, x_second = send(brick, "gx"), send(brick, "gx", True)
    ghosts = [send(v, "gy", bool(i)) for i, v in enumerate(outgoing)]
    edge = pl.pallas_call(
        functools.partial(widen_kernel, steps, n_y),
        out_shape=shape(z_tiles, rows + 8, lanes),
        in_specs=[VMEM] * (1 + n_ghost),
        out_specs=VMEM,
        compiler_params=grant(2),
        name="widen",
    )(edge, *ghosts)
    edges = pl.pallas_call(
        functools.partial(merge_kernel, steps, n_z),
        out_shape=shape(z_tiles, rows + 8, lanes),
        in_specs=[VMEM] * 2,
        out_specs=VMEM,
        compiler_params=grant(2),
        name="merge",
    )(send(edge, "gz"), send(edge, "gz", True))
    edges = [edges, send(edges, "gx"), send(edges, "gx", True)]

    prepare = pl.pallas_call(
        functools.partial(prepare_kernel, materials, steps, lanes),
        out_shape=[
            shape(4 * materials + steps, 8, lanes),
            shape(lanes, slots, dtype=jnp.bfloat16),
            shape(TILE_DEV, slots, dtype=jnp.bfloat16),
            shape(8, slots, dtype=jnp.int32),
            shape(1, slots),
        ],
        in_specs=[VMEM] * len(small) + [SMEM, pl.BlockSpec(memory_space=pl.ANY)],
        out_specs=[VMEM] * 5,
        compiler_params=grant(6),
        cost_estimate=pl.CostEstimate(flops=1 << 20, bytes_accessed=1 << 20, transcendentals=0),
        name="prepare",
    )
    prepared = prepare(*small, row_count, edges[0])

    bricks = [brick, x_first, x_second]
    outgoing = pl.pallas_call(
        functools.partial(rows_kernel, steps, len(bricks)),
        out_shape=[shape(len(bricks) * n_msg // 2, 8, lanes)] * n_ghost,
        in_specs=[VMEM] * len(bricks) + [pl.BlockSpec(memory_space=pl.ANY)],
        out_specs=[VMEM] * n_ghost,
        compiler_params=grant(6),
        name="rows",
    )(*bricks, prepared[-1])
    ghosts = [send(v, "gy", bool(i)) for i, v in enumerate(outgoing)]

    owners = n_x * n_y
    full = rows + 8
    e_out, h_out, part = pl.pallas_call(
        functools.partial(main_kernel, sizes, steps, materials, n_ghost),
        out_shape=(shape(*e_field.shape), shape(*h_field.shape), shape(owners, 8, TILE_DEV)),
        in_specs=[VMEM] * (len(bricks) + n_ghost + len(edges) + len(prepared)),
        out_specs=(VMEM,) * 3,
        scratch_shapes=[
            pltpu.VMEM((10, 3 * planes, full, lanes), f32),
            pltpu.VMEM((4, 3 * planes, full, lanes), f32),
            pltpu.VMEM((10, full, lanes), f32),
            pltpu.VMEM((4, full, lanes), f32),
            pltpu.VMEM((len(PAIRS), planes * rows, lanes), f32),
        ],
        compiler_params=grant(24),
        name="march",
    )(*bricks, *ghosts, *edges, *prepared)
    got = lax.all_to_all(part, ("gx", "gy"), split_axis=0, concat_axis=0, tiled=True)
    force = jnp.sum(got[:, :3], axis=0)
    return e_out, h_out, force


def solution(mesh):
    sizes = tuple(mesh.shape[a] for a in AXES)
    return jax.shard_map(
        functools.partial(local, sizes),
        mesh=mesh,
        in_specs=(
            P(None, "gx", "gy", "gz"),
            P(None, "gx", "gy", "gz"),
            P(None, "gx", "gy", "gz"),
            P("gx", "gy", "gz"),
            P(),
            P(),
            P(),
            P(),
            P("gx", "gy", "gz", None),
            P("gx", "gy", "gz", None, None),
            P("gx", "gy", "gz", None),
            P("gx", "gy", "gz", None),
            P("gx", "gy", "gz"),
        ),
        out_specs=(
            P(None, "gx", "gy", "gz"),
            P(None, "gx", "gy", "gz"),
            P(None, ("gx", "gy", "gz")),
        ),
        check_vma=False,
    )
```

time: 30.8 us -> 31.7 us (1.029)
  waiting for transfers between devices: 4.62 us -> 6.72 us
  Pallas kernels: 5.36 us -> 4.44 us
  local copies, waits for them, and re-layouts: 0.65 us -> 0 us
    ppermute x7 -> x8, waiting for transfers between devices: 4.62 us -> 6.72 us  [send(): return lax.ppermute(value, AXES, full_swap(sizes, axis, second))]
    pallas_call x4 -> x6, Pallas kernels: 5.36 us -> 4.44 us  [the longest x1 2.78 us: body(): pl.pallas_call(functools.partial(main_kernel, sizes, steps, materials, n_...]
    unnamed x17 -> x0, local copies, waits for them, and re-layouts: 0.65 us -> none
    ppermute x7 -> x8, starting transfers between devices: 7.97 us -> 8.27 us  [send(): return lax.ppermute(value, AXES, full_swap(sizes, axis, second))]
  transfers between devices with their start and end apart: 7 -> 8, of which waited for: 3 -> 4; matrix products, arithmetic and copies ran while one was open for 0% -> 0% of each run, Pallas kernels for 3% -> 1%
where the time goes in v4:
time: 31.7 us; the launch traced here: 31.5 us
  blocking collectives  10.1 us (32%)
  starting transfers between devices  8.27 us (26%)
  waiting for transfers between devices  6.72 us (21%)
  Pallas kernels  4.44 us (14%)
  between operations  1.33 us (4%)
  other arithmetic  0.59 us (2%)
    all_to_all x1, blocking collectives, body(): lax.all_to_all(part, ('gx', 'gy'), split_axis=0, concat_axis=0, tiled=True)  10.1 us
    ppermute x8, starting transfers between devices, send(): return lax.ppermute(value, AXES, full_swap(sizes, axis, second))  8.27 us
    ppermute x8, waiting for transfers between devices, send(): return lax.ppermute(value, AXES, full_swap(sizes, axis, second))  6.72 us
    pallas_call x1, Pallas kernels, body(): pl.pallas_call(functools.partial(main_kernel, sizes, steps, materials, n_...  2.78 us
    pallas_call x1, Pallas kernels, body(): pl.pallas_call(functools.partial(pack_kernel, steps, n_ghost), out_shape=...  1.38 us
  transfers between devices with their start and end apart: 8, of which 4 were waited for; matrix products, arithmetic and copies ran while one was open for 0% of the time, Pallas kernels for 1%

profile of v4, /device:TPU:0, one launch (start us, length us, event | category | flops | bytes accessed | tf_op | source)
XLA Modules:
  0.0 31.5 jit_solution(2837476276935965792)
XLA Ops:
  0.6 1.4 %pack.1 = (f32[40,16,128]{2,1,0:T(8,128)S(1)}, f32[3,16,128]{2,1,0:T(8,128)S(1)}, f32[3,8,128]{2,1,0:T(8,128)S(1)}, f32[1,3]{1,0:T(1,128)S(1)}, f32[1,3]{1,0:T(1...) custom-call(f32[12,16,128]{2,1,0:T(8,128)} %bitcast.11, ...), custom_call_target="tpu_custom_call" | custom-call | tf_op jit(solution)/shard_map/pack/pallas_call | solution.py:401
  2.0 3.1 %collective-permute-start = (f32[40,16,128]{2,1,0:T(8,128)S(1)}, f32[40,16,128]{2,1,0:T(8,128)S(1)}, u32[]{:S(2)}, u32[]{:S(2)}) collective-permute-start(f32[40,16,128]{2,1,0:T(8,128)S(1)} %get-tuple-element.22.refs_0_), channel_id=1, source_target_pairs={{0,8},{1,9},{2,10},{3,11},{4,12},{5,13},{6,14},{7,15},{8,0},{9,1},... | collective-permute-start | bytes 983048 | tf_op jit(solution)/shard_map/ppermute | solution.py:392
  5.1 0.0 collective-permute-start.1
  5.1 0.5 %collective-permute-start.2 = (f32[3,8,128]{2,1,0:T(8,128)S(1)}, f32[3,8,128]{2,1,0:T(8,128)S(1)}, u32[]{:S(2)}, u32[]{:S(2)}) collective-permute-start(f32[3,8,128]{2,1,0:T(8,128)S(1)} %get-tuple-element.32), channel_id=1, source_target_pairs={{0,4},{1,5},{2,6},{3,7},{4,0},{5,1},{6,2},{7,3},{8,12},{9,13},{10,... | collective-permute-start | bytes 36872 | tf_op jit(solution)/shard_map/ppermute | solution.py:392
  5.7 1.1 %collective-permute-done.2.refs_0_ = f32[3,8,128]{2,1,0:T(8,128)S(1)} collective-permute-done((f32[3,8,128]{2,1,0:T(8,128)S(1)}, f32[3,8,128]{2,1,0:T(8,128)S(1)}, u32[]{:S(2)}, u32[]{:S(2)}) %collective-permute-start.2) | collective-permute-done | bytes 12320 | tf_op jit(solution)/shard_map/ppermute | solution.py:392
  6.8 1.5 %collective-permute-start.3 = (f32[3,24,128]{2,1,0:T(8,128)S(1)}, f32[3,24,128]{2,1,0:T(8,128)S(1)}, u32[]{:S(2)}, u32[]{:S(2)}) collective-permute-start(f32[3,24,128]{2,1,0:T(8,128)S(1)} %widen.1), channel_id=1, source_target_pairs={{0,1},{1,0},{2,3},{3,2},{4,5},{5,4},{6,7},{7,6},{8,9},{9,8},{10,11... | collective-permute-start | bytes 110600 | tf_op jit(solution)/shard_map/ppermute | solution.py:392
  8.3 0.0 collective-permute-start.4
  8.9 1.8 %collective-permute-done.3.first_ref = f32[3,24,128]{2,1,0:T(8,128)S(1)} collective-permute-done((f32[3,24,128]{2,1,0:T(8,128)S(1)}, f32[3,24,128]{2,1,0:T(8,128)S(1)}, u32[]{:S(2)}, u32[]{:S(2)}) %collective-permute-start.3) | collective-permute-done | bytes 36896 | tf_op jit(solution)/shard_map/ppermute | solution.py:392
  10.8 0.0 collective-permute-done.4.second_ref
  10.8 0.2 prepare.1
  11.0 1.8 %collective-permute-done.refs_1_ = f32[40,16,128]{2,1,0:T(8,128)S(1)} collective-permute-done((f32[40,16,128]{2,1,0:T(8,128)S(1)}, f32[40,16,128]{2,1,0:T(8,128)S(1)}, u32[]{:S(2)}, u32[]{:S(2)}) %collective-permute-start) | collective-permute-done | bytes 327712 | tf_op jit(solution)/shard_map/ppermute | solution.py:392
  12.9 0.0 collective-permute-done.1.refs_2_
  12.9 0.1 collective-permute-start.5
  13.0 2.9 %collective-permute-start.6 = (f32[3,24,128]{2,1,0:T(8,128)S(1)}, f32[3,24,128]{2,1,0:T(8,128)S(1)}, u32[]{:S(2)}, u32[]{:S(2)}) collective-permute-start(f32[3,24,128]{2,1,0:T(8,128)S(1)} %merge.1.after_ref.refs_4_), channel_id=1, source_target_pairs={{0,8},{1,9},{2,10},{3,11},{4,12},{5,13},{6,14},{7,15},{8,0},{9,1},... | collective-permute-start | bytes 110600 | tf_op jit(solution)/shard_map/ppermute | solution.py:392
  15.9 0.2 collective-permute-start.7
  16.1 1.9 %collective-permute-done.6.refs_5_ = f32[3,24,128]{2,1,0:T(8,128)S(1)} collective-permute-done((f32[3,24,128]{2,1,0:T(8,128)S(1)}, f32[3,24,128]{2,1,0:T(8,128)S(1)}, u32[]{:S(2)}, u32[]{:S(2)}) %collective-permute-start.6) | collective-permute-done | bytes 36896 | tf_op jit(solution)/shard_map/ppermute | solution.py:392
  18.0 0.0 collective-permute-done.7.refs_6_
  18.0 0.0 collective-permute-done.5.refs_3_
  18.0 2.8 %march.1 = (f32[3,4,16,128]{3,2,1,0:T(8,128)}, f32[3,4,16,128]{3,2,1,0:T(8,128)}, f32[8,8,128]{2,1,0:T(8,128)S(1)}) custom-call(f32[40,16,128]{2,1,0:T(8,128)S(1)} %get-tuple-element.22.refs_0_, f32[40,16,128]{2,1,0:T(8,128)S(1)} %collective-permute-done.refs_1_, f32[40,16,128]{2,1,0:T(8,128)S(1)} %collective-permute-done.1.refs_2_, ...), custom_call_target="tpu_custom_call" | custom-call | tf_op jit(solution)/shard_map/march/pallas_call | solution.py:464
  20.8 10.1 %all_to_all.5 = f32[8,8,128]{2,1,0:T(8,128)S(1)} all-to-all(f32[8,8,128]{2,1,0:T(8,128)S(1)} %get-tuple-element.40), channel_id=1, replica_groups=mesh['gx'=4,'gy'=2,'gz'=4] {'gx','gy'}, dimensions={0} | all-to-all | bytes 65536 | tf_op jit(solution)/shard_map/all_to_all | solution.py:479
  30.9 0.6 %slice_reduce_fusion = f32[3,128]{1,0:T(4,128)} fusion(f32[8,8,128]{2,1,0:T(8,128)S(1)} %all_to_all.5), kind=kLoop, calls=%fused_computation | loop fusion | flops 2688 | bytes 13824 | tf_op jit(solution)/shard_map/reduce_sum | solution.py:480
  (3 shorter events, 0.1 us)
Async XLA Ops:
  2.0 10.8 %collective-permute-start = (f32[40,16,128]{2,1,0:T(8,128)S(1)}, f32[40,16,128]{2,1,0:T(8,128)S(1)}, u32[]{:S(2)}, u32[]{:S(2)}) collective-permute-start(f32[40,16,128]{2,1,0:T(8,128)S(1)} %get-tuple-element.22.refs_0_), channel_id=1, source_target_pairs={{0,8},{1,9},{2,10},{3,11},{4,12},{5,13},{6,14},{7,15},{8,0},{9,1},... | collective-permute-start | bytes 983048 | tf_op jit(solution)/shard_map/ppermute | solution.py:392
  5.1 7.7 %collective-permute-start.1 = (f32[40,16,128]{2,1,0:T(8,128)S(1)}, f32[40,16,128]{2,1,0:T(8,128)S(1)}, u32[]{:S(2)}, u32[]{:S(2)}) collective-permute-start(f32[40,16,128]{2,1,0:T(8,128)S(1)} %get-tuple-element.22.refs_0_), channel_id=1, source_target_pairs={{0,4},{1,5},{2,6},{3,7},{4,0},{5,1},{6,2},{7,3},{8,16},{9,17},{10,... | collective-permute-start | bytes 983048 | tf_op jit(solution)/shard_map/ppermute | solution.py:392
  5.1 1.6 %collective-permute-start.2 = (f32[3,8,128]{2,1,0:T(8,128)S(1)}, f32[3,8,128]{2,1,0:T(8,128)S(1)}, u32[]{:S(2)}, u32[]{:S(2)}) collective-permute-start(f32[3,8,128]{2,1,0:T(8,128)S(1)} %get-tuple-element.32), channel_id=1, source_target_pairs={{0,4},{1,5},{2,6},{3,7},{4,0},{5,1},{6,2},{7,3},{8,12},{9,13},{10,... | collective-permute-start | bytes 36872 | tf_op jit(solution)/shard_map/ppermute | solution.py:392
  6.8 4.0 %collective-permute-start.3 = (f32[3,24,128]{2,1,0:T(8,128)S(1)}, f32[3,24,128]{2,1,0:T(8,128)S(1)}, u32[]{:S(2)}, u32[]{:S(2)}) collective-permute-start(f32[3,24,128]{2,1,0:T(8,128)S(1)} %widen.1), channel_id=1, source_target_pairs={{0,1},{1,0},{2,3},{3,2},{4,5},{5,4},{6,7},{7,6},{8,9},{9,8},{10,11... | collective-permute-start | bytes 110600 | tf_op jit(solution)/shard_map/ppermute | solution.py:392
  8.3 2.5 %collective-permute-start.4 = (f32[3,24,128]{2,1,0:T(8,128)S(1)}, f32[3,24,128]{2,1,0:T(8,128)S(1)}, u32[]{:S(2)}, u32[]{:S(2)}) collective-permute-start(f32[3,24,128]{2,1,0:T(8,128)S(1)} %widen.1), channel_id=1, source_target_pairs={{0,4},{1,2},{2,1},{3,7},{4,0},{5,6},{6,5},{7,3},{8,12},{9,10},{10,... | collective-permute-start | bytes 110600 | tf_op jit(solution)/shard_map/ppermute | solution.py:392
  12.9 5.1 %collective-permute-start.5 = (f32[60,8,128]{2,1,0:T(8,128)S(1)}, f32[60,8,128]{2,1,0:T(8,128)S(1)}, u32[]{:S(2)}, u32[]{:S(2)}) collective-permute-start(f32[60,8,128]{2,1,0:T(8,128)S(1)} %rows.1), channel_id=1, source_target_pairs={{0,4},{1,5},{2,6},{3,7},{4,0},{5,1},{6,2},{7,3},{8,12},{9,13},{10,... | collective-permute-start | bytes 737288 | tf_op jit(solution)/shard_map/ppermute | solution.py:392
  13.0 5.0 %collective-permute-start.6 = (f32[3,24,128]{2,1,0:T(8,128)S(1)}, f32[3,24,128]{2,1,0:T(8,128)S(1)}, u32[]{:S(2)}, u32[]{:S(2)}) collective-permute-start(f32[3,24,128]{2,1,0:T(8,128)S(1)} %merge.1.after_ref.refs_4_), channel_id=1, source_target_pairs={{0,8},{1,9},{2,10},{3,11},{4,12},{5,13},{6,14},{7,15},{8,0},{9,1},... | collective-permute-start | bytes 110600 | tf_op jit(solution)/shard_map/ppermute | solution.py:392
  15.9 2.1 %collective-permute-start.7 = (f32[3,24,128]{2,1,0:T(8,128)S(1)}, f32[3,24,128]{2,1,0:T(8,128)S(1)}, u32[]{:S(2)}, u32[]{:S(2)}) collective-permute-start(f32[3,24,128]{2,1,0:T(8,128)S(1)} %merge.1.after_ref.refs_4_), channel_id=1, source_target_pairs={{0,4},{1,5},{2,6},{3,7},{4,0},{5,1},{6,2},{7,3},{8,16},{9,17},{10,... | collective-permute-start | bytes 110600 | tf_op jit(solution)/shard_map/ppermute | solution.py:392

commit v5 on v4

--- a/solution.py
+++ b/solution.py
@@ -38,32 +38,42 @@
     return pairs
 
 
+def slot_order(planes):
+    end = planes - 1
+    head = [(f, 0) for f in (3, 6, 7, 8, 9)]
+    tail = [(f, end) for f in (0, 3, 4, 5, 6, 7, 8, 9)]
+    rest = [(f, p) for f in range(10) for p in range(planes) if (f, p) not in head + tail]
+    return head + rest + tail, len(head), len(head) + len(rest) + len(tail)
+
+
 def pack_kernel(depth, n_ghost, *refs):
-    e_ref, h_ref, j_ref, m_ref = refs[:4]
-    n_small = (len(refs) - 4 - 4 - n_ghost) // 2
-    small, refs = refs[4 : 4 + n_small], refs[4 + n_small :]
-    brick_ref, edge_ref, refs = refs[0], refs[1], refs[2:]
-    sends, kept, (m_buf, sems) = refs[:n_ghost], refs[n_ghost : n_ghost + n_small], refs[n_ghost + n_small :]
-    planes, rows, lanes = m_ref.shape
-    count = 3 * planes
-    copies = [pltpu.make_async_copy(ref, brick_ref.at[pl.ds(i * count, count)], sems.at[i]) for i, ref in enumerate((e_ref, h_ref, j_ref))]
-    copies.append(pltpu.make_async_copy(m_ref, m_buf, sems.at[3]))
-    copies += [pltpu.make_async_copy(src, dst, sems.at[4 + i]) for i, (src, dst) in enumerate(zip(small, kept, strict=True))]
+    inputs, refs = refs[:4], refs[4:]
+    brick_ref, pay_first, pay_second, edge_ref, refs = *refs[:4], refs[4:]
+    sends, bufs, sems = refs[:n_ghost], refs[n_ghost : n_ghost + 4], refs[n_ghost + 4]
+    copies = [pltpu.make_async_copy(src, buf, sems.at[i]) for i, (src, buf) in enumerate(zip(inputs, bufs, strict=True))]
     for copy in copies:
         copy.start()
+    planes, rows, lanes = bufs[3].shape
+    order, _, n_msg = slot_order(planes)
+    place = {slot: i for i, slot in enumerate(order)}
     width = 2 * depth * planes
     per_tile = lanes // width
     lane = lax.broadcasted_iota(jnp.int32, (rows, lanes), 1)
     packed = [jnp.zeros((rows, lanes), jnp.float32) for _ in range(edge_ref.shape[0])]
-    for j in range(3 * count + planes):
-        if j % count == 0:
-            copies[j // count].wait()
-        if j >= 3 * count:
-            brick_ref[j] = (m_buf[j - 3 * count] + 1).astype(jnp.float32)
-        value = brick_ref[j]
-        tile, start = j // planes // per_tile, j // planes % per_tile * width + j % planes * 2 * depth
-        turned = pltpu.roll(value, (start + depth) % lanes, 1)
-        packed[tile] = jnp.where((lane >= start) & (lane < start + 2 * depth), turned, packed[tile])
+    for f in range(10):
+        if f % 3 == 0:
+            copies[f // 3].wait()
+        for p in range(planes):
+            value = (bufs[3][p] + 1).astype(jnp.float32) if f == 9 else bufs[f // 3][f % 3 * planes + p]
+            brick_ref[place[f, p]] = value
+            tile, start = f // per_tile, f % per_tile * width + p * 2 * depth
+            turned = pltpu.roll(value, (start + depth) % lanes, 1)
+            packed[tile] = jnp.where((lane >= start) & (lane < start + 2 * depth), turned, packed[tile])
+    n_pay = pay_first.shape[0]
+    to_upper = n_msg - n_pay
+    is_even = lax.axis_index("gx") % 2 == 0
+    pay_first[...] = brick_ref[pl.ds(jnp.where(is_even, to_upper, 0), n_pay)]
+    pay_second[...] = brick_ref[pl.ds(jnp.where(is_even, 0, to_upper), n_pay)]
     is_odd = lax.axis_index("gy") % 2 == 1
     for tile, value in enumerate(packed):
         edge_ref[tile] = value
@@ -71,8 +81,6 @@
         sends[0][tile] = jnp.where(is_odd, first, last)
         if n_ghost > 1:
             sends[1][tile] = jnp.where(is_odd, last, first)
-    for copy in copies[4:]:
-        copy.wait()
 
 
 def sides_y(depth, n_y, lanes):
@@ -120,23 +128,30 @@
     ins, outs = refs[:n_in], refs[n_in + 1 :]
     is_odd = lax.axis_index("gy") % 2
     row = lax.broadcasted_iota(jnp.int32, (8, outs[0].shape[2]), 0)
-    at = 0
-    for ref in ins:
-        count, rows, _ = ref.shape
-        for which, out in enumerate(outs):
-            last = (1 - is_odd) if which == 0 else is_odd
-            start = pl.multiple_of(last * (rows - 8), 8)
-            mine = (row >= jnp.where(last == 1, 8 - depth, 0)) & (row < jnp.where(last == 1, 8, depth))
-            for j in range(0, count, 2):
-                kept, turned = ref[j, pl.ds(start, 8), :], ref[j + 1, pl.ds(start, 8), :]
-                out[(at + j) // 2] = jnp.where(mine, kept, pltpu.roll(turned, 4, 0))
-        at += count
-
-
-def prepare_kernel(materials, steps, lanes, sigma_ref, gamma_ref, plasma_ref, g_ref,
-                   cell_ref, owner_ref, tile_ref, normal_ref, count_ref, after_ref,
-                   table_ref, hot_ref, tile_hot_ref, ints_ref, scale_ref):
-    del after_ref
+    planes = [(ref, j) for ref in ins for j in range(ref.shape[0])]
+    rows = ins[0].shape[1]
+    for which, out in enumerate(outs):
+        last = (1 - is_odd) if which == 0 else is_odd
+        start = pl.multiple_of(last * (rows - 8), 8)
+        mine = (row >= jnp.where(last == 1, 8 - depth, 0)) & (row < jnp.where(last == 1, 8, depth))
+        for at in range(0, len(planes), 2):
+            value = planes[at][0][planes[at][1], pl.ds(start, 8), :]
+            if at + 1 < len(planes):
+                turned = planes[at + 1][0][planes[at + 1][1], pl.ds(start, 8), :]
+                value = jnp.where(mine, value, pltpu.roll(turned, 4, 0))
+            out[at // 2] = value
+
+
+def prepare_kernel(materials, steps, lanes, *refs):
+    inputs, count_ref, refs = refs[:8], refs[8], refs[10:]
+    table_ref, hot_ref, tile_hot_ref, ints_ref, scale_ref = refs[:5]
+    bufs, sems = refs[5:13], refs[13]
+    copies = [pltpu.make_async_copy(src, buf, sems.at[i]) for i, (src, buf) in enumerate(zip(inputs, bufs, strict=True))]
+    for copy in copies:
+        copy.start()
+    for copy in copies:
+        copy.wait()
+    sigma_ref, gamma_ref, plasma_ref, g_ref, cell_ref, owner_ref, tile_ref, normal_ref = bufs
     slots = cell_ref.shape[1]
     shape = table_ref.shape[1:]
 
@@ -171,7 +186,7 @@
     edge_refs, refs = refs[:3], refs[3:]
     table_ref, hot_ref, tile_hot_ref, ints_ref, scale_ref = refs[:5]
     e_out, h_out, part_out = refs[5:8]
-    field, coef, side, side_coef, tensor = refs[8:13]
+    field, coef, side, side_coef, tensor, sems = refs[8:14]
     n_msg, rows, lanes = bricks[0].shape
     planes = e_out.shape[1]
     depth = steps
@@ -181,19 +196,27 @@
     pick = sides_y(depth, n_y, lanes)
     full = rows + 8
 
+    order, _, _ = slot_order(planes)
+    place = {slot: i for i, slot in enumerate(order)}
+    n_pay = bricks[1].shape[0]
+
     def whole(which, j):
-        at = which * n_msg + j
+        at = j if which == 0 else n_msg + (which - 1) * n_pay + j
         values = [g[at // 2] for g in ghosts]
         if at % 2:
             values = [pltpu.roll(v, 4, 0) for v in values]
         return jnp.concatenate([bricks[which][j], pick(values)], 0)
 
-    for j in range(n_msg):
-        f, p = j // planes, j % planes
-        first, second = whole(1, j), whole(2, j)
-        field[f, planes + p] = whole(0, j)
-        field[f, p] = jnp.where(low_x, jnp.where(even_x, second, first), 0.0)
-        field[f, 2 * planes + p] = jnp.where(high_x, jnp.where(even_x, first, second), 0.0)
+    for f, p in order:
+        field[f, planes + p] = whole(0, place[f, p])
+        at = place[f, p] - (n_msg - n_pay)
+        if at >= 0:
+            first, second = whole(1, at), whole(2, at)
+            field[f, p] = jnp.where(low_x, jnp.where(even_x, second, first), 0.0)
+        at = place[f, p]
+        if at < n_pay:
+            first, second = whole(1, at), whole(2, at)
+            field[f, 2 * planes + p] = jnp.where(high_x, jnp.where(even_x, first, second), 0.0)
 
     width = 2 * depth * planes
     per_tile = lanes // width
@@ -324,10 +347,14 @@
                 if t > 1:
                     value = tensor[i, pl.ds(plane * rows, rows), :] + value
                 tensor[i, pl.ds(plane * rows, rows), :] = value
-            if final:
-                for i in range(3):
-                    e_out[i, plane] = e[i]
-                    h_out[i, plane] = h[i]
+        if final:
+            own = pl.ds(planes, planes)
+            outs = [
+                pltpu.make_async_copy(field.at[pl.ds(3 * i, 3), own, pl.ds(0, rows)], out, sems.at[i])
+                for i, out in enumerate((e_out, h_out))
+            ]
+            for copy in outs:
+                copy.start()
 
     def halves(v):
         high = v.astype(jnp.bfloat16)
@@ -362,6 +389,8 @@
     part = total[: owners * 8] + total[owners * 8 :]
     for o in range(owners):
         part_out[o] = part[o * 8 : (o + 1) * 8]
+    for copy in outs:
+        copy.wait()
 
 
 def local(sizes, *args):
@@ -374,7 +403,8 @@
     steps = g_kernel.shape[0]
     planes, rows, lanes = material.shape
     f32 = jnp.float32
-    n_msg = 10 * planes
+    _, head, n_msg = slot_order(planes)
+    n_pay = n_msg - head
     per_tile = lanes // (2 * steps * planes)
     z_tiles = -(-10 // per_tile)
     n_ghost = 1 if n_y == 2 else 2
@@ -397,21 +427,22 @@
         plasma_table.reshape(1, materials),
         g_kernel.reshape(1, steps),
     ] + [v.reshape(1, slots) for v in (surf_cell, surf_owner, surf_tile, surf_normal)]
-    args = [v.reshape(3 * planes, rows, lanes) for v in (e_field, h_field, current)] + [material] + small
+    small = [pltpu.with_memory_space_constraint(v, pltpu.HBM) for v in small]
+    args = [v.reshape(3 * planes, rows, lanes) for v in (e_field, h_field, current)] + [material]
     packed = pl.pallas_call(
         functools.partial(pack_kernel, steps, n_ghost),
-        out_shape=[shape(n_msg, rows, lanes), shape(z_tiles, rows, lanes)]
-        + [shape(z_tiles, 8, lanes)] * n_ghost
-        + [shape(*v.shape, dtype=v.dtype) for v in small],
+        out_shape=[shape(n_msg, rows, lanes), shape(n_pay, rows, lanes), shape(n_pay, rows, lanes), shape(z_tiles, rows, lanes)]
+        + [shape(z_tiles, 8, lanes)] * n_ghost,
         in_specs=[hbm] * len(args),
-        out_specs=[VMEM] * (2 + n_ghost + len(small)),
-        scratch_shapes=[pltpu.VMEM((planes, rows, lanes), jnp.int32), pltpu.SemaphoreType.DMA((len(args),))],
+        out_specs=[VMEM] * (4 + n_ghost),
+        scratch_shapes=[pltpu.VMEM(v.shape, v.dtype) for v in args] + [pltpu.SemaphoreType.DMA((len(args),))],
         compiler_params=grant(4),
         name="pack",
     )(*(pltpu.with_memory_space_constraint(v, pltpu.HBM) for v in args))
-    brick, edge, outgoing, small = packed[0], packed[1], packed[2 : 2 + n_ghost], packed[2 + n_ghost :]
-
-    x_first, x_second = send(brick, "gx"), send(brick, "gx", True)
+    brick, pay_first, pay_second, edge = packed[:4]
+    outgoing = packed[4:]
+
+    x_first, x_second = send(pay_first, "gx"), send(pay_second, "gx", True)
     ghosts = [send(v, "gy", bool(i)) for i, v in enumerate(outgoing)]
     edge = pl.pallas_call(
         functools.partial(widen_kernel, steps, n_y),
@@ -440,8 +471,9 @@
             shape(8, slots, dtype=jnp.int32),
             shape(1, slots),
         ],
-        in_specs=[VMEM] * len(small) + [SMEM, pl.BlockSpec(memory_space=pl.ANY)],
+        in_specs=[hbm] * len(small) + [SMEM, pl.BlockSpec(memory_space=pl.ANY)],
         out_specs=[VMEM] * 5,
+        scratch_shapes=[pltpu.VMEM(v.shape, v.dtype) for v in small] + [pltpu.SemaphoreType.DMA((len(small),))],
         compiler_params=grant(6),
         cost_estimate=pl.CostEstimate(flops=1 << 20, bytes_accessed=1 << 20, transcendentals=0),
         name="prepare",
@@ -451,7 +483,7 @@
     bricks = [brick, x_first, x_second]
     outgoing = pl.pallas_call(
         functools.partial(rows_kernel, steps, len(bricks)),
-        out_shape=[shape(len(bricks) * n_msg // 2, 8, lanes)] * n_ghost,
+        out_shape=[shape(-(-(n_msg + 2 * n_pay) // 2), 8, lanes)] * n_ghost,
         in_specs=[VMEM] * len(bricks) + [pl.BlockSpec(memory_space=pl.ANY)],
         out_specs=[VMEM] * n_ghost,
         compiler_params=grant(6),
@@ -465,13 +497,14 @@
         functools.partial(main_kernel, sizes, steps, materials, n_ghost),
         out_shape=(shape(*e_field.shape), shape(*h_field.shape), shape(owners, 8, TILE_DEV)),
         in_specs=[VMEM] * (len(bricks) + n_ghost + len(edges) + len(prepared)),
-        out_specs=(VMEM,) * 3,
+        out_specs=(hbm, hbm, VMEM),
         scratch_shapes=[
             pltpu.VMEM((10, 3 * planes, full, lanes), f32),
             pltpu.VMEM((4, 3 * planes, full, lanes), f32),
             pltpu.VMEM((10, full, lanes), f32),
             pltpu.VMEM((4, full, lanes), f32),
             pltpu.VMEM((len(PAIRS), planes * rows, lanes), f32),
+            pltpu.SemaphoreType.DMA((2,)),
         ],
         compiler_params=grant(24),
         name="march",

time: 31.7 us -> 30.5 us (0.962)
  waiting for transfers between devices: 6.72 us -> 4.97 us
  Pallas kernels: 4.44 us -> 4.91 us
    ppermute x8, waiting for transfers between devices: 6.72 us -> 4.97 us  [send(): return lax.ppermute(value, AXES, full_swap(sizes, axis, second))]
    pallas_call x1, Pallas kernels: 0.23 us -> 1.1 us  [body(): prepared = prepare(*small, row_count, edges[0])]
  transfers between devices with their start and end apart: 8 -> 8, of which waited for: 4 -> 4; matrix products, arithmetic and copies ran while one was open for 0% -> 0% of each run, Pallas kernels for 1% -> 4%
where the time goes in v5:
time: 30.5 us; the launch traced here: 30.2 us
  blocking collectives  10.2 us (33%)
  starting transfers between devices  8.27 us (27%)
  waiting for transfers between devices  4.97 us (16%)
  Pallas kernels  4.91 us (16%)
  between operations  1.33 us (4%)
  other arithmetic  0.59 us (2%)
    all_to_all x1, blocking collectives, body(): lax.all_to_all(part, ('gx', 'gy'), split_axis=0, concat_axis=0, tiled=True)  10.2 us
    ppermute x8, starting transfers between devices, send(): return lax.ppermute(value, AXES, full_swap(sizes, axis, second))  8.27 us
    ppermute x8, waiting for transfers between devices, send(): return lax.ppermute(value, AXES, full_swap(sizes, axis, second))  4.97 us
    pallas_call x1, Pallas kernels, body(): pl.pallas_call(functools.partial(main_kernel, sizes, steps, materials, n_...  2.47 us
    pallas_call x1, Pallas kernels, body(): pl.pallas_call(functools.partial(pack_kernel, steps, n_ghost), out_shape=...  1.29 us
    pallas_call x1, Pallas kernels, body(): prepared = prepare(*small, row_count, edges[0])  1.1 us
  transfers between devices with their start and end apart: 8, of which 4 were waited for; matrix products, arithmetic and copies ran while one was open for 0% of the time, Pallas kernels for 4%

profile of v5, /device:TPU:0, one launch (start us, length us, event | category | flops | bytes accessed | tf_op | source)
XLA Modules:
  0.0 30.2 jit_solution(10000468357849096474)
XLA Ops:
  0.6 1.3 %pack.1 = (f32[40,16,128]{2,1,0:T(8,128)S(1)}, f32[35,16,128]{2,1,0:T(8,128)S(1)}, f32[35,16,128]{2,1,0:T(8,128)S(1)}, f32[3,16,128]{2,1,0:T(8,128)S(1)}, f32[3,8,128]{2,1,0:T(8,128)S(1)}) custom-call(f32[12,16,128]{2,1,0:T(8,128)} %bitcast.11, f32[12,16,128]{2,1,0:T(8,128)} %bitcast.12, f32[12,16,128]{2,1,0:T(8,128)} %bitcast.13, s32[4,16,128]{2,1,0:T(8,128)} %refs_3_.1), custom_call_target="tpu_custom_call" | custom-call | tf_op jit(solution)/shard_map/pack/pallas_call | solution.py:432
  1.9 3.1 %collective-permute-start = (f32[35,16,128]{2,1,0:T(8,128)S(1)}, f32[35,16,128]{2,1,0:T(8,128)S(1)}, u32[]{:S(2)}, u32[]{:S(2)}) collective-permute-start(f32[35,16,128]{2,1,0:T(8,128)S(1)} %get-tuple-element.17), channel_id=1, source_target_pairs={{0,8},{1,9},{2,10},{3,11},{4,12},{5,13},{6,14},{7,15},{8,0},{9,1},... | collective-permute-start | bytes 860168 | tf_op jit(solution)/shard_map/ppermute | solution.py:422
  5.0 0.0 collective-permute-start.1
  5.0 0.5 %collective-permute-start.2 = (f32[3,8,128]{2,1,0:T(8,128)S(1)}, f32[3,8,128]{2,1,0:T(8,128)S(1)}, u32[]{:S(2)}, u32[]{:S(2)}) collective-permute-start(f32[3,8,128]{2,1,0:T(8,128)S(1)} %get-tuple-element.20), channel_id=1, source_target_pairs={{0,4},{1,5},{2,6},{3,7},{4,0},{5,1},{6,2},{7,3},{8,12},{9,13},{10,... | collective-permute-start | bytes 36872 | tf_op jit(solution)/shard_map/ppermute | solution.py:422
  5.6 1.1 %collective-permute-done.2.refs_0_ = f32[3,8,128]{2,1,0:T(8,128)S(1)} collective-permute-done((f32[3,8,128]{2,1,0:T(8,128)S(1)}, f32[3,8,128]{2,1,0:T(8,128)S(1)}, u32[]{:S(2)}, u32[]{:S(2)}) %collective-permute-start.2) | collective-permute-done | bytes 12320 | tf_op jit(solution)/shard_map/ppermute | solution.py:422
  6.6 1.5 %collective-permute-start.3 = (f32[3,24,128]{2,1,0:T(8,128)S(1)}, f32[3,24,128]{2,1,0:T(8,128)S(1)}, u32[]{:S(2)}, u32[]{:S(2)}) collective-permute-start(f32[3,24,128]{2,1,0:T(8,128)S(1)} %widen.1), channel_id=1, source_target_pairs={{0,1},{1,0},{2,3},{3,2},{4,5},{5,4},{6,7},{7,6},{8,9},{9,8},{10,11... | collective-permute-start | bytes 110600 | tf_op jit(solution)/shard_map/ppermute | solution.py:422
  8.1 0.0 collective-permute-start.4
  8.8 1.8 %collective-permute-done.3.first_ref = f32[3,24,128]{2,1,0:T(8,128)S(1)} collective-permute-done((f32[3,24,128]{2,1,0:T(8,128)S(1)}, f32[3,24,128]{2,1,0:T(8,128)S(1)}, u32[]{:S(2)}, u32[]{:S(2)}) %collective-permute-start.3) | collective-permute-done | bytes 36896 | tf_op jit(solution)/shard_map/ppermute | solution.py:422
  10.6 0.0 collective-permute-done.4.second_ref
  10.6 1.1 %prepare.1 = (f32[16,8,128]{2,1,0:T(8,128)S(1)}, bf16[128,1024]{1,0:T(8,128)(2,1)S(1)}, bf16[128,1024]{1,0:T(8,128)(2,1)S(1)}, s32[8,1024]{1,0:T(8,128)S(1)}, f32[1,1024]{1,0:T(1,128)S(1)}) custom-call(f32[1,3]{1,0:T(1,128)} %bitcast.18, f32[1,3]{1,0:T(1,128)} %bitcast.19, f32[1,3]{1,0:T(1,128)} %bitcast.20, f32[1,4]{1,0:T(1,128)} %bitcast.21, ...), custom_call_target="tpu_custom_call" | custom-call | flops 1048576 | bytes 1048576 | tf_op jit(solution)/shard_map/prepare/pallas_call | solution.py:481
  11.7 0.1 collective-permute-done.refs_1_
  11.9 0.0 collective-permute-done.1.refs_2_
  11.9 0.1 collective-permute-start.5
  12.0 2.9 %collective-permute-start.6 = (f32[3,24,128]{2,1,0:T(8,128)S(1)}, f32[3,24,128]{2,1,0:T(8,128)S(1)}, u32[]{:S(2)}, u32[]{:S(2)}) collective-permute-start(f32[3,24,128]{2,1,0:T(8,128)S(1)} %merge.1.refs_9_.refs_4_), channel_id=1, source_target_pairs={{0,8},{1,9},{2,10},{3,11},{4,12},{5,13},{6,14},{7,15},{8,0},{9,1},... | collective-permute-start | bytes 110600 | tf_op jit(solution)/shard_map/ppermute | solution.py:422
  14.9 0.2 collective-permute-start.7
  15.1 1.9 %collective-permute-done.6.refs_5_ = f32[3,24,128]{2,1,0:T(8,128)S(1)} collective-permute-done((f32[3,24,128]{2,1,0:T(8,128)S(1)}, f32[3,24,128]{2,1,0:T(8,128)S(1)}, u32[]{:S(2)}, u32[]{:S(2)}) %collective-permute-start.6) | collective-permute-done | bytes 36896 | tf_op jit(solution)/shard_map/ppermute | solution.py:422
  17.0 0.0 collective-permute-done.7.refs_6_
  17.0 0.0 collective-permute-done.5.refs_3_
  17.0 2.5 %march.1 = (f32[3,4,16,128]{3,2,1,0:T(8,128)}, f32[3,4,16,128]{3,2,1,0:T(8,128)}, f32[8,8,128]{2,1,0:T(8,128)S(1)}) custom-call(f32[40,16,128]{2,1,0:T(8,128)S(1)} %get-tuple-element.16.refs_0_, f32[35,16,128]{2,1,0:T(8,128)S(1)} %collective-permute-done.refs_1_, f32[35,16,128]{2,1,0:T(8,128)S(1)} %collective-permute-done.1.refs_2_, ...), custom_call_target="tpu_custom_call" | custom-call | tf_op jit(solution)/shard_map/march/pallas_call | solution.py:496
  19.5 10.2 %all_to_all.5 = f32[8,8,128]{2,1,0:T(8,128)S(1)} all-to-all(f32[8,8,128]{2,1,0:T(8,128)S(1)} %get-tuple-element.28), channel_id=1, replica_groups=mesh['gx'=4,'gy'=2,'gz'=4] {'gx','gy'}, dimensions={0} | all-to-all | bytes 65536 | tf_op jit(solution)/shard_map/all_to_all | solution.py:512
  29.6 0.6 %slice_reduce_fusion = f32[3,128]{1,0:T(4,128)} fusion(f32[8,8,128]{2,1,0:T(8,128)S(1)} %all_to_all.5), kind=kLoop, calls=%fused_computation | loop fusion | flops 2688 | bytes 13824 | tf_op jit(solution)/shard_map/reduce_sum | solution.py:513
  (3 shorter events, 0.1 us)
Async XLA Ops:
  1.9 9.9 %collective-permute-start = (f32[35,16,128]{2,1,0:T(8,128)S(1)}, f32[35,16,128]{2,1,0:T(8,128)S(1)}, u32[]{:S(2)}, u32[]{:S(2)}) collective-permute-start(f32[35,16,128]{2,1,0:T(8,128)S(1)} %get-tuple-element.17), channel_id=1, source_target_pairs={{0,8},{1,9},{2,10},{3,11},{4,12},{5,13},{6,14},{7,15},{8,0},{9,1},... | collective-permute-start | bytes 860168 | tf_op jit(solution)/shard_map/ppermute | solution.py:422
  5.0 6.8 %collective-permute-start.1 = (f32[35,16,128]{2,1,0:T(8,128)S(1)}, f32[35,16,128]{2,1,0:T(8,128)S(1)}, u32[]{:S(2)}, u32[]{:S(2)}) collective-permute-start(f32[35,16,128]{2,1,0:T(8,128)S(1)} %get-tuple-element.18), channel_id=1, source_target_pairs={{0,4},{1,5},{2,6},{3,7},{4,0},{5,1},{6,2},{7,3},{8,16},{9,17},{10,... | collective-permute-start | bytes 860168 | tf_op jit(solution)/shard_map/ppermute | solution.py:422
  5.0 1.6 %collective-permute-start.2 = (f32[3,8,128]{2,1,0:T(8,128)S(1)}, f32[3,8,128]{2,1,0:T(8,128)S(1)}, u32[]{:S(2)}, u32[]{:S(2)}) collective-permute-start(f32[3,8,128]{2,1,0:T(8,128)S(1)} %get-tuple-element.20), channel_id=1, source_target_pairs={{0,4},{1,5},{2,6},{3,7},{4,0},{5,1},{6,2},{7,3},{8,12},{9,13},{10,... | collective-permute-start | bytes 36872 | tf_op jit(solution)/shard_map/ppermute | solution.py:422
  6.6 4.0 %collective-permute-start.3 = (f32[3,24,128]{2,1,0:T(8,128)S(1)}, f32[3,24,128]{2,1,0:T(8,128)S(1)}, u32[]{:S(2)}, u32[]{:S(2)}) collective-permute-start(f32[3,24,128]{2,1,0:T(8,128)S(1)} %widen.1), channel_id=1, source_target_pairs={{0,1},{1,0},{2,3},{3,2},{4,5},{5,4},{6,7},{7,6},{8,9},{9,8},{10,11... | collective-permute-start | bytes 110600 | tf_op jit(solution)/shard_map/ppermute | solution.py:422
  8.1 2.5 %collective-permute-start.4 = (f32[3,24,128]{2,1,0:T(8,128)S(1)}, f32[3,24,128]{2,1,0:T(8,128)S(1)}, u32[]{:S(2)}, u32[]{:S(2)}) collective-permute-start(f32[3,24,128]{2,1,0:T(8,128)S(1)} %widen.1), channel_id=1, source_target_pairs={{0,4},{1,2},{2,1},{3,7},{4,0},{5,6},{6,5},{7,3},{8,12},{9,10},{10,... | collective-permute-start | bytes 110600 | tf_op jit(solution)/shard_map/ppermute | solution.py:422
  11.9 5.1 %collective-permute-start.5 = (f32[55,8,128]{2,1,0:T(8,128)S(1)}, f32[55,8,128]{2,1,0:T(8,128)S(1)}, u32[]{:S(2)}, u32[]{:S(2)}) collective-permute-start(f32[55,8,128]{2,1,0:T(8,128)S(1)} %rows.1), channel_id=1, source_target_pairs={{0,4},{1,5},{2,6},{3,7},{4,0},{5,1},{6,2},{7,3},{8,12},{9,13},{10,... | collective-permute-start | bytes 675848 | tf_op jit(solution)/shard_map/ppermute | solution.py:422
  12.0 5.0 %collective-permute-start.6 = (f32[3,24,128]{2,1,0:T(8,128)S(1)}, f32[3,24,128]{2,1,0:T(8,128)S(1)}, u32[]{:S(2)}, u32[]{:S(2)}) collective-permute-start(f32[3,24,128]{2,1,0:T(8,128)S(1)} %merge.1.refs_9_.refs_4_), channel_id=1, source_target_pairs={{0,8},{1,9},{2,10},{3,11},{4,12},{5,13},{6,14},{7,15},{8,0},{9,1},... | collective-permute-start | bytes 110600 | tf_op jit(solution)/shard_map/ppermute | solution.py:422
  14.9 2.1 %collective-permute-start.7 = (f32[3,24,128]{2,1,0:T(8,128)S(1)}, f32[3,24,128]{2,1,0:T(8,128)S(1)}, u32[]{:S(2)}, u32[]{:S(2)}) collective-permute-start(f32[3,24,128]{2,1,0:T(8,128)S(1)} %merge.1.refs_9_.refs_4_), channel_id=1, source_target_pairs={{0,4},{1,5},{2,6},{3,7},{4,0},{5,1},{6,2},{7,3},{8,16},{9,17},{10,... | collective-permute-start | bytes 110600 | tf_op jit(solution)/shard_map/ppermute | solution.py:422
